TPU v7x, 32 devices: a whole 2x2x4 slice. The times are simulated.
32 devices in a mesh: wide: 8 (over z, y), narrow: 4 (over x, core).
Axes of the slice: x: 2, y: 2, z: 4, core: 2. Of those that a mesh axis runs over, the one named last changes fastest.
Arguments:
- tokens: bfloat16 [16384, 768], P(('wide', 'narrow')), may hold values from -6 to 6
- item_lengths: int32 [32], P('wide'), may hold values from 0 to 1024, as said below
- w_query: bfloat16 [768, 768], P(None, 'narrow'), may hold values from -0.3125 to 0.3125
- b_query: bfloat16 [768], P('narrow'), may hold values from -1.25 to 1.25
- w_key: bfloat16 [768, 768], P(None, 'narrow'), may hold values from -0.3125 to 0.3125
- w_value: bfloat16 [768, 768], P(None, 'narrow'), may hold values from -0.21875 to 0.21875
- b_value: bfloat16 [768], P('narrow'), may hold values from -1.25 to 1.25
- w_out: bfloat16 [768, 768], P('narrow'), may hold values from -0.875 to 0.875
- b_out: bfloat16 [768], replicated, may hold values from -1.25 to 1.25
- gain_attn: bfloat16 [768], replicated, may hold values from 0.5 to 1.5
- shift_attn: bfloat16 [768], replicated, may hold values from -1.25 to 1.25
- w_up: bfloat16 [768, 3072], P(None, 'narrow'), may hold values from -0.21875 to 0.21875
- b_up: bfloat16 [3072], P('narrow'), may hold values from -1.25 to 1.25
- w_down: bfloat16 [3072, 768], P('narrow'), may hold values from -0.109375 to 0.109375
- b_down: bfloat16 [768], replicated, may hold values from -1.25 to 1.25
- gain_ffn: bfloat16 [768], replicated, may hold values from 0.5 to 1.5
- shift_ffn: bfloat16 [768], replicated, may hold values from -1.25 to 1.25
- out_grad: bfloat16 [16384, 768], P(('wide', 'narrow')), may hold values from -6 to 6
Outputs:
- layer_out: bfloat16 [16384, 768], P(('wide', 'narrow'))
- token_grad: float32 [16384, 768], P(('wide', 'narrow'))
- w_query_grad: float32 [768, 768], P(None, 'narrow')
- b_query_grad: float32 [768], P('narrow')
- w_key_grad: float32 [768, 768], P(None, 'narrow')
- w_value_grad: float32 [768, 768], P(None, 'narrow')
- b_value_grad: float32 [768], P('narrow')
- w_out_grad: float32 [768, 768], P('narrow')
- b_out_grad: float32 [768], replicated
- gain_attn_grad: float32 [768], replicated
- shift_attn_grad: float32 [768], replicated
- w_up_grad: float32 [768, 3072], P(None, 'narrow')
- b_up_grad: float32 [3072], P('narrow')
- w_down_grad: float32 [3072, 768], P('narrow')
- b_down_grad: float32 [768], replicated
- gain_ffn_grad: float32 [768], replicated
- shift_ffn_grad: float32 [768], replicated
Inputs may be any that keep to these rules, and one draw needn't show every extreme that they name: `item_lengths`: the 4 entries of each index of wide list its items in token order, each of 512 or 1024 tokens, together 2048, followed by zeros; some index of wide holds only items of 1024 tokens.
All inputs are finite; a program needn't handle non-finite values.
Results may differ from a plain program's by a relative error of at most 0.02.
Values may be sent and summed in bfloat16 or wider, within the bound.
No kernel may reach another device: no remote copies, remote signals or barrier semaphores. Data moves between devices by JAX's collectives and lax.ppermute only.
A program may use at most 128 MiB of HBM per device.

v0:
```python
import functools

import jax
import jax.numpy as jnp
from jax import lax
from jax.experimental import pallas as pl
from jax.experimental.pallas import tpu as pltpu
from jax.sharding import PartitionSpec as P

HD = 64
F32 = jnp.float32
BF = jnp.bfloat16
MIB = 1 << 20

norm_eps = 1e-12
masked_shift = 1e30
half_root = 0.7071067811865476
inv_root_two_pi = 0.3989422804014327
score_scale = HD**-0.5

VM = pl.BlockSpec(memory_space=pltpu.VMEM)
SM = pl.BlockSpec(memory_space=pltpu.SMEM)
ANY = pl.BlockSpec(memory_space=pl.ANY)


def dot(left, right):
    return jnp.dot(left, right, preferred_element_type=F32)


def contract_rows(left, right):
    return lax.dot_general(left, right, (((0,), (0,)), ((), ())), preferred_element_type=F32)


def contract_cols(left, right):
    return lax.dot_general(left, right, (((1,), (1,)), ((), ())), preferred_element_type=F32)


def shape(dims, dtype):
    return jax.ShapeDtypeStruct(dims, dtype)


def row(ref):
    return ref[...].astype(F32).reshape(1, -1)


class Arriving:
    def __init__(self, source, buffer, sem):
        self.buffer = buffer
        self.shape = buffer.shape
        self.dtype = buffer.dtype
        self.copy = pltpu.make_async_copy(source, buffer, sem)
        self.started = False
        self.waiting = True
        self.then = []

    def start(self):
        if not self.started:
            self.copy.start()
            self.started = True

    def wait(self):
        self.start()
        if self.waiting:
            self.copy.wait()
            self.waiting = False
            for other in self.then:
                other.start()

    def __getitem__(self, index):
        self.wait()
        return self.buffer[index]


class Leaving:
    def __init__(self, target, buffer, sem):
        self.buffer = buffer
        self.shape = buffer.shape
        self.dtype = buffer.dtype
        self.copy = pltpu.make_async_copy(buffer, target, sem)
        self.sent = False

    def __getitem__(self, index):
        return self.buffer[index]

    def __setitem__(self, index, value):
        self.buffer[index] = value

    def send(self):
        if not self.sent:
            self.copy.start()
            self.sent = True


def call(
    kernel, name, out_shape, args, smem=0, scratch=(), vmem=60, after=(), raw=(), part=(), first=0,
    stay=(), stay_out=(),
):
    count = len(args)
    outs = len(out_shape)
    loaded = [i for i in range(smem, count) if i not in raw and i not in stay]
    leaving_out = [n for n in range(outs) if n not in stay_out]
    part = dict(part)

    def held(i):
        dims = (part[i][1], *args[i].shape[1:]) if i in part else args[i].shape
        return pltpu.VMEM(dims, args[i].dtype)

    buffers = [held(i) for i in loaded]
    buffers += [pltpu.VMEM(out_shape[n].shape, out_shape[n].dtype) for n in leaving_out]

    def body(*refs):
        given = list(refs[:count])
        refs = refs[count + len(after) :]
        results, refs = list(refs[:outs]), refs[outs:]
        own, refs = refs[: len(buffers)], refs[len(buffers) :]
        in_sems, out_sems, refs = refs[0], refs[1], refs[2:]
        for n, i in enumerate(loaded):
            source = given[i].at[pl.ds(*part[i])] if i in part else given[i]
            given[i] = Arriving(source, own[n], in_sems.at[n])
        late = [given[i] for i in loaded if first and i >= first]
        for i in loaded:
            if given[i] not in late:
                given[i].start()
                given[i].then = late
        for m, n in enumerate(leaving_out):
            results[n] = Leaving(results[n], own[len(loaded) + m], out_sems.at[m])
        kernel(*given, *results, *refs)
        for i in loaded:
            given[i].wait()
        for n in leaving_out:
            results[n].send()
        for n in leaving_out:
            results[n].copy.wait()

    in_specs = [SM] * smem + [VM if i in stay else ANY for i in range(smem, count)]
    return pl.pallas_call(
        body,
        out_shape=tuple(out_shape),
        in_specs=in_specs + [ANY] * len(after),
        out_specs=tuple(VM if n in stay_out else ANY for n in range(outs)),
        scratch_shapes=[
            *buffers, pltpu.SemaphoreType.DMA((max(len(loaded), 1),)),
            pltpu.SemaphoreType.DMA((max(len(leaving_out), 1),)), *scratch,
        ],
        compiler_params=pltpu.CompilerParams(vmem_limit_bytes=vmem * MIB),
        cost_estimate=pl.CostEstimate(flops=1000, transcendentals=0, bytes_accessed=1000),
        name=name,
    )(*args, *after)


def send(ref):
    if isinstance(ref, Leaving):
        ref.send()


def arrive(*refs):
    for ref in refs:
        if isinstance(ref, Arriving):
            ref.wait()


def chunks(extent, size, body):
    def step(i, carry):
        body(pl.ds(pl.multiple_of(i * size, size), size))
        return carry

    lax.fori_loop(0, extent // size, step, 0)


def masked(picked, a):
    return jnp.where(picked, a.astype(F32), 0.0).astype(BF)


def joint_kernel(wq_ref, wk_ref, wv_ref, wo_ref, bq_ref, bv_ref, bu_ref, out_ref, tail_s):
    cols = wq_ref.shape[0]
    for i, ref in enumerate((wq_ref, wk_ref, wv_ref, wo_ref)):
        out_ref[i * cols : (i + 1) * cols] = ref[...]
    tail_s[...] = jnp.zeros_like(tail_s)
    tail_s[0:1, 0:cols] = row(bq_ref)
    tail_s[1:2, 0:cols] = row(bv_ref)
    tail_s[2:3, :] = row(bu_ref)
    out_ref[4 * cols : 4 * cols + 16] = tail_s[...].astype(BF)


def pack_joint(w_query, w_key, w_value, w_out, b_query, b_value, b_up):
    width, cols = w_query.shape
    return call(
        joint_kernel, "pack_joint", [shape((4 * cols + 16, width), BF)],
        (w_query.T, w_key.T, w_value.T, w_out, b_query, b_value, b_up),
        scratch=[pltpu.VMEM((16, width), F32)],
    )[0]


def neighbour(lens_ref, me_ref, rows):
    me = me_ref[0]
    here = me * rows
    first = jnp.int32(0)
    start = jnp.int32(0)
    length = jnp.int32(0)
    for j in range(lens_ref.shape[0]):
        n = lens_ref[j]
        inside = (first <= here) & (here < first + n)
        start = jnp.where(inside, first, start)
        length = jnp.where(inside, n, length)
        first = first + n
    other = jnp.where(start == here, me + 1, me - 1)
    return length > rows, other == (me ^ 1)


def pick_other(use_core, core_ref, mid_ref, buffer, sem):
    from_core = pltpu.make_async_copy(core_ref, buffer, sem)
    from_mid = pltpu.make_async_copy(mid_ref, buffer, sem)

    @pl.when(use_core)
    def _():
        from_core.start()

    @pl.when(jnp.logical_not(use_core))
    def _():
        from_mid.start()

    return from_core


def attend_block(flag, own_ref, oth_s, a_ref, outs, scratch):
    ctx_ref, ct_ref, lse_ref, q_ref, k_ref, v_ref = outs
    qt_s, vt_s = scratch
    rows, cols = q_ref.shape
    tail = a_ref[4 * cols : 4 * cols + 16].astype(F32)
    wk = a_ref[cols : 2 * cols]
    wv = a_ref[2 * cols : 3 * cols]
    near = slice(0, rows)
    far = slice(rows, 2 * rows)
    q = (contract_cols(own_ref[...], a_ref[0:cols]) + tail[0:1, 0:cols]).astype(BF)
    q = q * jnp.asarray(score_scale, BF)
    q_ref[...] = q
    qt_s[...] = q.T
    for part, tok_ref in ((near, own_ref), (far, oth_s)):
        k_ref[part] = contract_cols(tok_ref[...], wk).astype(BF)
        v = (contract_cols(tok_ref[...], wv) + tail[1:2, 0:cols]).astype(BF)
        v_ref[part] = v
        vt_s[:, part] = v.T
    head_of_row = lax.broadcasted_iota(jnp.int32, (cols, 1), 0) // HD

    def head(h, carry):
        hs = pl.ds(pl.multiple_of(h * HD, HD), HD)
        q_h = masked(head_of_row == h, qt_s[...])
        s_own = dot(k_ref[near], q_h)
        s_other = dot(k_ref[far], q_h)
        top_own = jnp.max(s_own, axis=0, keepdims=True)
        top_other = jnp.max(s_other, axis=0, keepdims=True)
        top = jnp.where(flag, jnp.maximum(top_own, top_other), top_own)
        p_own = jnp.exp(s_own - top)
        p_other = jnp.exp(s_other - jnp.where(flag, top, masked_shift))
        total = jnp.sum(p_own, axis=0, keepdims=True) + jnp.sum(p_other, axis=0, keepdims=True)
        c = dot(vt_s[hs, near], p_own.astype(BF)) + dot(vt_s[hs, far], p_other.astype(BF))
        ct_ref[hs] = c * (1.0 / total)
        lse_ref[pl.ds(h, 1)] = top + jnp.log(total)
        return carry

    lax.fori_loop(0, cols // HD, head, 0)
    ctx_ref[...] = ct_ref[...].T.astype(BF)


def block_outs(rows, cols):
    return [
        shape((rows, cols), BF), shape((cols, rows), F32), shape((cols // HD, rows), F32),
        shape((rows, cols), BF), shape((2 * rows, cols), BF), shape((2 * rows, cols), BF),
    ]


def attend_scratch(rows, width, cols):
    return [
        pltpu.VMEM((rows, width), BF), pltpu.SemaphoreType.DMA,
        pltpu.VMEM((cols, rows), BF), pltpu.VMEM((cols, 2 * rows), BF),
    ]


class Once:
    def __init__(self, copy, buffer):
        self.copy = copy
        self.buffer = buffer

    def __call__(self):
        if self.copy is not None:
            self.copy.wait()
            self.copy = None
        return self.buffer[...]


def attend_pair_kernel(
    lens_ref, me_ref, core_ref, mid_ref, own_ref, a0_ref, a1_ref, *refs, after
):
    targets = refs[after : after + 12]
    own_s, a_s, *held = refs[after + 12 : after + 20]
    own_sem, a_sem, out_sem, oth_s, oth_sem, qt_s, vt_s = refs[after + 20 :]
    own_copy = pltpu.make_async_copy(own_ref, own_s, own_sem)
    own_copy.start()
    weights = [
        pltpu.make_async_copy(ref, a_s.at[i], a_sem.at[i]) for i, ref in enumerate((a0_ref, a1_ref))
    ]
    weights[0].start()
    flag, use_core = neighbour(lens_ref, me_ref, own_ref.shape[0])
    other = pick_other(use_core, core_ref, mid_ref, oth_s, oth_sem)
    leaving = [
        [
            pltpu.make_async_copy(buffer.at[i], targets[6 * i + n], out_sem.at[i, n])
            for n, buffer in enumerate(held)
        ]
        for i in range(2)
    ]
    own_copy.wait()

    def block(i, carry):
        @pl.when(i == 0)
        def _():
            weights[0].wait()
            other.wait()
            weights[1].start()

        @pl.when(i == 1)
        def _():
            weights[1].wait()

        attend_block(
            flag, own_s, oth_s, a_s.at[i], [buffer.at[i] for buffer in held], (qt_s, vt_s)
        )
        for n in range(2):

            @pl.when(i == n)
            def _():
                for copy in leaving[n]:
                    copy.start()

        return carry

    lax.fori_loop(0, 2, block, 0)
    for copies in leaving:
        for copy in copies:
            copy.wait()


def attend_pair(name, lens, me, own, tok_core, tok_mid, blocks, after=()):
    rows, width = own.shape
    cols = (blocks[0].shape[0] - 16) // 4
    outs = block_outs(rows, cols)
    got = pl.pallas_call(
        functools.partial(attend_pair_kernel, after=len(after)),
        out_shape=tuple(outs * 2),
        in_specs=[SM, SM] + [ANY] * (5 + len(after)),
        out_specs=tuple([ANY] * 12),
        scratch_shapes=[
            pltpu.VMEM(own.shape, BF), pltpu.VMEM((2, *blocks[0].shape), BF),
            *[pltpu.VMEM((2, *o.shape), o.dtype) for o in outs],
            pltpu.SemaphoreType.DMA, pltpu.SemaphoreType.DMA((2,)), pltpu.SemaphoreType.DMA((2, 6)),
            *attend_scratch(rows, width, cols),
        ],
        compiler_params=pltpu.CompilerParams(vmem_limit_bytes=60 * MIB),
        cost_estimate=pl.CostEstimate(flops=1000, transcendentals=0, bytes_accessed=1000),
        name=name,
    )(lens, me, tok_core, tok_mid, own, *blocks, *after)
    return got[:6], got[6:]


def norm_near_kernel(
    own_ref, c0_ref, w0_ref, c1_ref, w1_ref, c2_ref, w2_ref, c3_ref, w3_ref, bo_ref, gain_ref, shift_ref,
    u0_ref, bias0_ref, d0_ref, u1_ref, bias1_ref, d1_ref,
    unit_ref, inv_ref, low_ref, act0_ref, sl0_ref, act1_ref, sl1_ref, sum_ref,
):
    pairs = ((c0_ref, w0_ref), (c1_ref, w1_ref), (c2_ref, w2_ref), (c3_ref, w3_ref))
    vectors = row(bo_ref), row(gain_ref), row(shift_ref)
    for pair in pairs:
        arrive(*pair)
    arrive(own_ref)

    def rows_of(rs):
        resid = own_ref[rs].astype(F32) + vectors[0]
        for c_ref, w_ref in pairs:
            resid = resid + dot(c_ref[rs], w_ref[...])
        unit, inverse = unit_of(resid)
        unit_ref[rs] = unit
        inv_ref[rs] = inverse
        low_ref[rs] = (unit * vectors[1] + vectors[2]).astype(BF)

    chunks(own_ref.shape[0], 256, rows_of)
    send(unit_ref)
    send(inv_ref)
    send(low_ref)
    up_down(low_ref, bias0_ref, (u0_ref,), d0_ref, act0_ref, sl0_ref, sum_ref, True)
    up_down(low_ref, bias1_ref, (u1_ref,), d1_ref, act1_ref, sl1_ref, sum_ref, False)


def norm_near(own, ctxs, joints, b_out, gain, shift, ups, downs, after=()):
    rows, width = own.shape
    units = downs[0].shape[0]
    at = joints[0].shape[0] - 16
    piece = shape((rows, units), BF)
    cols = ctxs[0].shape[1]
    terms = [x for pair in zip(ctxs, joints) for x in pair]
    return call(
        norm_near_kernel, "norm_near",
        [
            shape((rows, width), F32), shape((rows, 1), F32), shape((rows, width), BF),
            piece, piece, piece, piece, shape((rows, width), F32),
        ],
        (
            own, *terms, b_out, gain, shift,
            ups[0], joints[0], downs[0], ups[1], joints[1], downs[1],
        ),
        part={2 * i + 2: (3 * cols, cols) for i in range(4)} | {13: (at, 16), 16: (at, 16)},
        after=after, first=12,
    )


def attend_back_block(
    flag, g_ref, wo_ref, saved, own_ref, other, grad_ref, sums, b_s, bu_ref, vec_ref, scratch
):
    ct_ref, lse_ref, q_ref, k_ref, v_ref = saved
    d_s = sums
    gt_s, qt_s, kt_s, dqt_s, p_s, ds_s, dk_s, dv_s, dot_s, g_s, t_s = scratch
    rows, cols = q_ref.shape
    near = slice(0, rows)
    far = slice(rows, 2 * rows)
    arrive(g_ref, wo_ref)
    other = other()
    arrive(q_ref)

    def query_rows(rs):
        g = contract_cols(g_ref[rs], wo_ref[...]).astype(BF)
        g_s[rs] = g
        gt_s[:, rs] = g.T
        qt_s[:, rs] = q_ref[rs].T

    chunks(rows, 256, query_rows)
    arrive(k_ref)

    def key_rows(rs):
        kt_s[:, rs] = k_ref[rs].T

    chunks(2 * rows, 256, key_rows)
    dot_s[...] = gt_s[...].astype(F32) * ct_ref[...]
    dk_s[...] = jnp.zeros(dk_s.shape, F32)
    dv_s[...] = jnp.zeros(dv_s.shape, F32)
    head_of_row = lax.broadcasted_iota(jnp.int32, (cols, 1), 0) // HD
    head_of_lane = lax.broadcasted_iota(jnp.int32, (1, cols), 1) // HD
    arrive(q_ref, k_ref, v_ref, lse_ref)

    def head(h, carry):
        hs = pl.ds(pl.multiple_of(h * HD, HD), HD)
        row_dot = jnp.sum(dot_s[hs], axis=0, keepdims=True)
        q_h = masked(head_of_row == h, qt_s[...])
        g_h = masked(head_of_row == h, gt_s[...])
        lse = lse_ref[pl.ds(h, 1)]
        for part, shift in ((near, lse), (far, jnp.where(flag, lse, masked_shift))):
            p = jnp.exp(dot(k_ref[part], q_h) - shift)
            p_s[part] = p.astype(BF)
            ds_s[part] = (p * (dot(v_ref[part], g_h) - row_dot)).astype(BF)
        dqt_s[hs] = dot(kt_s[hs], ds_s[...])
        dk_s[...] += dot(ds_s[...], masked(head_of_lane == h, q_ref[...]))
        dv_s[...] += dot(p_s[...], masked(head_of_lane == h, g_s[...]))
        return carry

    lax.fori_loop(0, cols // HD, head, 0)
    dqt = (dqt_s[...] * score_scale).astype(BF)
    dq = dqt.T
    d_s[near, 0:cols] = dq
    d_s[far, 0:cols] = jnp.zeros((rows, cols), BF)
    t_s[0:cols, near] = dqt
    b_s[...] = jnp.zeros(b_s.shape, F32)

    def grad_rows(rs):
        dk = dk_s[rs].astype(BF)
        dv = dv_s[rs].astype(BF)
        d_s[rs, cols : 2 * cols] = dk
        d_s[rs, 2 * cols : 3 * cols] = dv
        t_s[cols : 2 * cols, rs] = dk.T
        t_s[2 * cols : 3 * cols, rs] = dv.T
        b_s[1:2, 0:cols] += jnp.sum(dv.astype(F32), axis=0, keepdims=True)

    chunks(2 * rows, 256, grad_rows)
    t_s[3 * cols : 4 * cols, near] = ct_ref[...].astype(BF)
    b_s[0:1, 0:cols] = jnp.sum(dq.astype(F32), axis=0, keepdims=True)
    b_s[2:3] = bu_ref[...]
    b_s[8:16] = vec_ref[...]
    grad_ref[4 * cols : 4 * cols + 16] = b_s[...].astype(BF)
    grad_ref[4 * cols + 16 :] = jnp.zeros((grad_ref.shape[0] - 4 * cols - 16, b_s.shape[1]), BF)
    other()
    send(d_s)
    arrive(own_ref)
    width = own_ref.shape[1]

    def weight_terms(cs):
        tok = own_ref[:, cs]
        grad_ref[0:cols, cs] = dot(t_s[0:cols, near], tok).astype(BF)
        grad_ref[cols : 3 * cols, cs] = (
            dot(t_s[cols : 3 * cols, near], tok) + dot(t_s[cols : 3 * cols, far], other.buffer[:, cs])
        ).astype(BF)
        grad_ref[3 * cols : 4 * cols, cs] = dot(t_s[3 * cols : 4 * cols, near], g_ref[:, cs]).astype(BF)

    chunks(width, 256, weight_terms)
    send(grad_ref)


def attend_back_kernel(
    lens_ref, me_ref, core_ref, mid_ref,
    g_ref, wo_ref, q_ref, k_ref, lse_ref, v_ref, ct_ref, own_ref, bu_ref, vec_ref,
    grad_ref, d_ref, oth_s, oth_sem, b_s, *scratch,
):
    flag, use_core = neighbour(lens_ref, me_ref, own_ref.shape[0])
    attend_back_block(
        flag, g_ref, wo_ref, (ct_ref, lse_ref, q_ref, k_ref, v_ref), own_ref,
        lambda: Once(pick_other(use_core, core_ref, mid_ref, oth_s, oth_sem), oth_s),
        grad_ref, d_ref, b_s, bu_ref, vec_ref, scratch,
    )


def attend_back(lens, me, own, tok_core, tok_mid, g, block, bu, vecs, after=()):
    rows, width = own.shape
    a, (_, ct, lse, q, k, v) = block
    cols = q.shape[1]
    args = (lens, me, tok_core, tok_mid, g, a, q, k, lse, v, ct, own, bu, vecs)
    return call(
        attend_back_kernel, "attend_back",
        [shape((4 * cols + 64, width), BF), shape((2 * rows, 3 * cols), BF)],
        args, smem=2, raw=(2, 3), after=after, first=8, part={5: (3 * cols, cols)},
        scratch=[
            pltpu.VMEM((rows, width), BF), pltpu.SemaphoreType.DMA, pltpu.VMEM((16, width), F32),
            pltpu.VMEM((cols, rows), BF), pltpu.VMEM((cols, rows), BF),
            pltpu.VMEM((cols, 2 * rows), BF), pltpu.VMEM((cols, rows), F32),
            pltpu.VMEM((2 * rows, rows), BF), pltpu.VMEM((2 * rows, rows), BF),
            pltpu.VMEM((2 * rows, cols), F32), pltpu.VMEM((2 * rows, cols), F32),
            pltpu.VMEM((cols, rows), F32), pltpu.VMEM((rows, cols), BF),
            pltpu.VMEM((4 * cols, 2 * rows), BF),
        ],
    )


def other_grad_kernel(*refs):
    ds, weights, out_ref = refs[0:4], refs[4:8], refs[8]
    arrive(*ds, *weights)
    depth = ds[0].shape[1]

    def features_of(cs):
        total = dot(ds[0][...], weights[0][0:depth, cs])
        for d_ref, w_ref in zip(ds[1:], weights[1:]):
            total = total + dot(d_ref[...], w_ref[0:depth, cs])
        out_ref[:, cs] = total.astype(out_ref.dtype)

    chunks(out_ref.shape[1], 256, features_of)


def other_grad(ds, joints, rows, after=()):
    width = joints[0].shape[1]
    return call(
        other_grad_kernel, "other_grad", [shape((rows, width), BF)], (*ds, *joints), after=after,
        part={i: (rows, rows) for i in range(4)} | {i: (0, ds[0].shape[1]) for i in range(4, 8)},
    )[0]


def unit_of(residual):
    centre = jnp.mean(residual, axis=1, keepdims=True)
    spread = residual - centre
    inverse = lax.rsqrt(jnp.mean(spread * spread, axis=1, keepdims=True) + norm_eps)
    return spread * inverse, inverse


def norm_back(upstream, unit_rows, inverse, gain):
    unit_grad = upstream * gain
    return inverse * (
        unit_grad
        - jnp.mean(unit_grad, axis=1, keepdims=True)
        - unit_rows * jnp.mean(unit_grad * unit_rows, axis=1, keepdims=True)
    )


def up_down(low_ref, bias_ref, up_refs, down_ref, act_ref, slope_ref, sum_ref, start):
    up_ref = up_refs[0]
    arrive(low_ref, bias_ref, up_ref)

    def units_of(cs):
        pre = bias_ref[:, cs].astype(F32)[2:3] + dot(low_ref[...], up_ref[:, cs])
        phi = 0.5 + 0.5 * lax.erf(pre * half_root)
        act_ref[:, cs] = (pre * phi).astype(BF)
        slope_ref[:, cs] = (phi + pre * jnp.exp(-0.5 * pre * pre) * inv_root_two_pi).astype(BF)

    chunks(up_ref.shape[1], 256, units_of)
    send(act_ref)
    send(slope_ref)
    arrive(down_ref)

    def features_of(cs):
        part = dot(act_ref[...], down_ref[:, cs])
        sum_ref[:, cs] = part if start else sum_ref[:, cs] + part

    chunks(down_ref.shape[1], 256, features_of)


def ffn_back_block(
    g_ref, low_ref, act_ref, slope_ref, down_ref, up_refs, outs, sum_in_ref, sum_ref, pre_s
):
    down_grad_ref, up_grad_ref, bias_ref = outs
    up_ref = up_refs[0]
    arrive(g_ref, act_ref, slope_ref, down_ref)

    def units_of(cs):
        g = g_ref[...]
        down_grad_ref[cs] = contract_rows(act_ref[:, cs], g).astype(BF)
        pre = (contract_cols(g, down_ref[cs]) * slope_ref[:, cs].astype(F32)).astype(BF)
        pre_s[:, cs] = pre
        bias_ref[:, cs] = jnp.sum(pre.astype(F32), axis=0, keepdims=True)

    chunks(down_ref.shape[0], 256, units_of)
    send(down_grad_ref)
    arrive(low_ref, up_ref, sum_in_ref)

    def features_of(cs):
        pre = pre_s[...]
        up_grad_ref[cs] = contract_rows(low_ref[:, cs], pre).astype(BF)
        sum_ref[:, cs] = sum_in_ref[:, cs] + contract_cols(pre, up_ref[cs])

    chunks(up_ref.shape[0], 256, features_of)
    send(up_grad_ref)


def ffn_grad_outs(width, units):
    return [shape((units, width), BF), shape((width, units), BF), shape((1, units), F32)]


def ffn_far_kernel(
    low_ref, u2_ref, bias2_ref, d2_ref, u3_ref, bias3_ref, d3_ref,
    sum_in_ref, unit_ref, gain1_ref, shift1_ref, bd_ref, gain2_ref, shift2_ref, out_grad_ref,
    act2_ref, sl2_ref, out_ref, low_grad_ref, vec_ref,
    down_grad_ref, up_grad_ref, bu_ref, sum_ref,
    act3_s, sl3_s, pre_s, part_s,
):
    up_down(low_ref, bias2_ref, (u2_ref,), d2_ref, act2_ref, sl2_ref, part_s, True)
    up_down(low_ref, bias3_ref, (u3_ref,), d3_ref, act3_s, sl3_s, part_s, False)
    gain1, gain2, shift2 = row(gain1_ref), row(gain2_ref), row(shift2_ref)
    shift1 = row(shift1_ref) + row(bd_ref)
    arrive(unit_ref, sum_in_ref, out_grad_ref)
    vec_ref[...] = jnp.zeros(vec_ref.shape, F32)

    def rows_of(rs):
        resid = unit_ref[rs] * gain1 + shift1 + sum_in_ref[rs] + part_s[rs]
        unit, inverse = unit_of(resid)
        out_ref[rs] = (unit * gain2 + shift2).astype(BF)
        upstream = out_grad_ref[rs].astype(F32)
        vec_ref[0:1] += jnp.sum(upstream * unit, axis=0, keepdims=True)
        vec_ref[1:2] += jnp.sum(upstream, axis=0, keepdims=True)
        back = norm_back(upstream, unit, inverse, gain2)
        sum_ref[rs] = back
        g = back.astype(BF)
        low_grad_ref[rs] = g
        vec_ref[2:3] += jnp.sum(g.astype(F32), axis=0, keepdims=True)

    chunks(unit_ref.shape[0], 256, rows_of)
    send(out_ref)
    send(low_grad_ref)
    ffn_back_block(
        low_grad_ref, low_ref, act3_s, sl3_s, d3_ref, (u3_ref,),
        (down_grad_ref, up_grad_ref, bu_ref), sum_ref, sum_ref, pre_s,
    )


def ffn_far(
    low, joints, ups, downs, near, unit, gain1, shift1, b_down, gain2, shift2, out_grad, after=()
):
    rows, width = low.shape
    units = downs[0].shape[0]
    at = joints[0].shape[0] - 16
    piece = shape((rows, units), BF)
    return call(
        ffn_far_kernel, "ffn_far",
        [
            piece, piece, shape((rows, width), BF), shape((rows, width), BF), shape((8, width), F32),
            *ffn_grad_outs(width, units), shape((rows, width), F32),
        ],
        (
            low, ups[0], joints[0], downs[0], ups[1], joints[1], downs[1], near, unit,
            gain1, shift1, b_down, gain2, shift2, out_grad,
        ),
        part={2: (at, 16), 5: (at, 16)}, first=4, after=after,
        scratch=[pltpu.VMEM((rows, units), BF)] * 3 + [pltpu.VMEM((rows, width), F32)],
    )


def ffn_back_kernel(
    g_ref, act_ref, down_ref, slope_ref, low_ref, up_ref, sum_in_ref,
    down_grad_ref, up_grad_ref, bu_ref, sum_ref, pre_s,
):
    ffn_back_block(
        g_ref, low_ref, act_ref, slope_ref, down_ref, (up_ref,),
        (down_grad_ref, up_grad_ref, bu_ref), sum_in_ref, sum_ref, pre_s,
    )


def ffn_back(g, low, act, slope, up, down, acc, after=()):
    rows, width = low.shape
    units = down.shape[0]
    return call(
        ffn_back_kernel, "ffn_back",
        [*ffn_grad_outs(width, units), shape((rows, width), F32)],
        (g, act, down, slope, low, up, acc), after=after, first=2,
        scratch=[pltpu.VMEM((rows, units), BF)],
    )


def ffn_last_kernel(
    g_ref, act1_ref, d1_ref, sl1_ref, low_ref, u1_ref, act0_ref, d0_ref, sl0_ref, u0_ref, sum_in_ref,
    unit_ref, inv_ref, gain_ref, vec_in_ref, *refs,
):
    low_ref_out, resid_ref, vec_ref = refs[6:9]
    sum_s, pre_s = refs[9:]
    ffn_back_block(
        g_ref, low_ref, act1_ref, sl1_ref, d1_ref, (u1_ref,), refs[0:3], sum_in_ref, sum_s, pre_s
    )
    ffn_back_block(
        g_ref, low_ref, act0_ref, sl0_ref, d0_ref, (u0_ref,), refs[3:6], sum_s, sum_s, pre_s
    )
    gain = row(gain_ref)
    arrive(unit_ref, inv_ref)
    vec_ref[...] = vec_in_ref[...]

    def rows_of(rs):
        upstream = sum_s[rs]
        unit = unit_ref[rs]
        vec_ref[4:5] += jnp.sum(upstream * unit, axis=0, keepdims=True)
        vec_ref[5:6] += jnp.sum(upstream, axis=0, keepdims=True)
        back = norm_back(upstream, unit, inv_ref[rs], gain)
        resid_ref[rs] = back
        low = back.astype(BF)
        low_ref_out[rs] = low
        vec_ref[6:7] += jnp.sum(low.astype(F32), axis=0, keepdims=True)

    chunks(unit_ref.shape[0], 256, rows_of)
    send(resid_ref)
    send(low_ref_out)


def ffn_last(g, low, acts, slopes, ups, downs, acc, unit, inverse, gain, vecs, after=()):
    rows, width = low.shape
    units = downs[0].shape[0]
    return call(
        ffn_last_kernel, "ffn_last",
        [
            *ffn_grad_outs(width, units), *ffn_grad_outs(width, units),
            shape((rows, width), BF), shape((rows, width), F32), shape((8, width), F32),
        ],
        (
            g, acts[1], downs[1], slopes[1], low, ups[1], acts[0], downs[0], slopes[0], ups[0], acc,
            unit, inverse, gain, vecs,
        ),
        after=after, first=2,
        scratch=[pltpu.VMEM((rows, width), F32), pltpu.VMEM((rows, units), BF)],
    )


def spread_small_kernel(in_ref, bq_ref, bv_ref, bu_ref, *rest):
    sums = in_ref[...]
    cols = bq_ref.shape[0]
    bq_ref[...] = sums[0:1, 0:cols].reshape(cols)
    bv_ref[...] = sums[1:2, 0:cols].reshape(cols)
    bu_ref[...] = sums[2:3].reshape(-1)
    for at, ref in zip((8, 9, 10, 12, 13, 14), rest):
        ref[...] = sums[at : at + 1].reshape(-1)


def spread_small(sums, cols, units):
    width = sums.shape[1]
    return call(
        spread_small_kernel, "spread_small",
        [shape((cols,), F32), shape((cols,), F32), shape((units,), F32)] + [shape((width,), F32)] * 6,
        (sums,), part={0: (2 * cols, 16)},
    )


def swap(a, axis, distance):
    size = lax.axis_size(axis)
    return lax.ppermute(a, axis, [(i, i ^ distance) for i in range(size)])


def to_core(a):
    return swap(a, "narrow", 1)


def to_chip(a):
    return swap(a, "narrow", 2)


def to_middle(a):
    return lax.ppermute(a, "narrow", [(1, 2), (2, 1)])


def wide_bits():
    size = lax.axis_size("wide")
    bits = []
    while size > 1:
        assert size % 2 == 0
        bits.append(len(bits))
        size //= 2
    return bits


def part_of(a, which, parts):
    rows = a.shape[0] // parts
    return lax.dynamic_slice_in_dim(a, which * rows, rows, 0)


def in_order(side, mine, got):
    return jnp.where(side == 0, jnp.concatenate([mine, got]), jnp.concatenate([got, mine]))


def hold(a, *others):
    return lax.optimization_barrier((a, *others))[0]


def add_low(*terms):
    total = terms[0].astype(F32)
    for term in terms[1:]:
        total = total + term.astype(F32)
    return total.astype(BF)


def side_of(bit):
    return (lax.axis_index("wide") >> bit) & 1


def own_piece(a):
    at = 0
    for bit in wide_bits():
        at = 2 * at + side_of(bit)
    return part_of(a, at, lax.axis_size("wide"))


class WideSum:
    def __init__(self, a):
        self.a = a
        self.step = 0
        self.send()

    def send(self):
        bit = self.step
        if bit < 3:
            side = side_of(bit)
            self.keep = part_of(self.a, side, 2)
            self.sent = part_of(self.a, 1 - side, 2)
        else:
            self.keep = self.sent = self.a
        self.got = swap(self.sent, "wide", 1 << bit)

    def advance(self, *waits):
        got = hold(self.got, *waits) if waits else self.got
        self.a = add_low(self.keep, got)
        self.step += 1
        if self.step < len(wide_bits()):
            self.send()

    def piece(self, *waits):
        while self.step < len(wide_bits()):
            self.advance(*waits)
            waits = ()
        return self.a


class WideGather:
    def __init__(self, a, bits=(2, 1, 0)):
        self.a = self.sent = a
        self.bits = bits
        self.step = 0
        self.send()

    def send(self):
        self.sent = self.a
        self.got = swap(self.a, "wide", 1 << self.bits[self.step])

    def advance(self, *waits):
        got = hold(self.got, *waits) if waits else self.got
        self.a = in_order(side_of(self.bits[self.step]), self.a, got)
        self.step += 1
        if self.step < len(self.bits):
            self.send()

    def whole(self, *waits):
        while self.step < len(self.bits):
            self.advance(*waits)
            waits = ()
        return self.a


def local(
    tokens, item_lengths, w_query, b_query, w_key, w_value, b_value, w_out, b_out,
    gain_attn, shift_attn, w_up, b_up, w_down, b_down, gain_ffn, shift_ffn, out_grad,
):
    rows, width = tokens.shape
    cols = w_query.shape[1]
    units = w_up.shape[1]
    assert lax.axis_size("narrow") == 4
    me = lax.axis_index("narrow").reshape(1)

    tok_mid = to_middle(tokens)
    tok_core = to_core(tokens)
    pieces = to_chip(own_piece(w_down))
    joint = pack_joint(w_query, w_key, w_value, w_out, b_query, b_value, b_up)
    joint_core = to_core(joint)
    joint_chip = to_chip(hold(joint, pieces, tok_mid))
    down_gather = WideGather(pieces, wide_bits()[::-1])
    while down_gather.step < len(down_gather.bits) - 2:
        down_gather.advance(joint_core)
    near0, near1 = attend_pair(
        "attend_near", item_lengths, me, tokens, tok_core, tok_mid, [joint, joint_core],
        (down_gather.sent,),
    )
    down_gather.advance(near1[2])
    gate = down_gather.sent
    joint_chip = hold(joint_chip, gate)
    joint_diag = to_core(joint_chip)
    up_chip = to_chip(hold(w_up, joint_chip))
    up_core = to_core(hold(w_up, joint_chip))
    down_core = to_core(hold(w_down, joint_chip))
    far2, far3 = attend_pair(
        "attend_far", item_lengths, me, tokens, tok_core, tok_mid, [joint_chip, joint_diag], (gate,)
    )
    joints = [joint, joint_core, joint_chip, joint_diag]
    saved = [near0, near1, far2, far3]
    unit_one, inv_one, low, act0, sl0, act1, sl1, near_sum = norm_near(
        tokens, [s[0] for s in saved], joints, b_out, gain_attn, shift_attn,
        [w_up, up_core], [w_down, down_core],
    )
    down_chip = down_gather.whole(inv_one)
    down_diag = to_core(down_chip)
    up_chip = hold(up_chip, down_chip)
    up_diag = to_core(up_chip)
    act2, sl2, layer_out, ffn_grad, vecs, down_d, up_d, bu_d, acc = ffn_far(
        low, joints[2:], [up_chip, up_diag], [down_chip, down_diag],
        near_sum, unit_one, gain_attn, shift_attn, b_down, gain_ffn, shift_ffn, out_grad,
    )

    up_from_core = to_core(up_d)
    down_from_core = to_core(down_d)
    down_x, up_x, bu_x, acc = ffn_back(ffn_grad, low, act2, sl2, up_chip, down_chip, acc)
    up_far = add_low(up_x, hold(up_from_core, bu_x))
    up_sum = to_chip(up_far)
    down_far = add_low(down_x, hold(down_from_core, up_far))
    down_sum = to_chip(down_far)
    down_c, up_c, bu_c, down_o, up_o, bu_o, attn_grad, resid_one, vecs = ffn_last(
        ffn_grad, low, (act0, act1), (sl0, sl1), (w_up, up_core), (w_down, down_core), acc,
        unit_one, inv_one, gain_attn, vecs, (up_far, down_far),
    )
    up_back = to_core(up_c)
    down_back = to_core(down_c)
    grads, parts = [None] * 4, [None] * 4
    bus = (bu_o, bu_c, bu_x, bu_d)

    def back_attend(r, *after):
        grads[r], parts[r] = attend_back(
            item_lengths, me, tokens, tok_core, tok_mid, attn_grad, (joints[r], saved[r]),
            bus[r], vecs, after,
        )
        return grads[r]

    mark = back_attend(3)
    up_sum = hold(up_sum, mark)
    near_up = WideSum(add_low(up_o, hold(up_back, up_sum), up_sum))
    down_near = add_low(down_o, hold(down_back, near_up.sent))
    joint_from_core = to_core(hold(grads[3], down_near))
    mark = back_attend(2, near_up.sent, down_near)
    down_sum = hold(down_sum, mark)
    near_down = WideSum(add_low(down_near, down_sum))
    joint_far = add_low(grads[2], hold(joint_from_core, near_down.a))
    joint_sum = to_chip(joint_far)
    near_up.advance(joint_far)
    mark = back_attend(1, joint_far, near_up.sent, near_down.sent)
    near_up.advance(mark)
    near_down.advance(near_up.sent)
    joint_back = to_core(hold(grads[1], near_down.sent))
    mark = back_attend(0, near_up.sent, near_down.sent)
    joint_sum = hold(joint_sum, mark)
    joint_back = hold(joint_back, joint_sum)

    def rows_of(a, part):
        return a[: 2 * cols] if part == 0 else a[2 * cols :]

    def joint_part(i, *waits):
        own = rows_of(grads[0], i)
        return WideSum(add_low(own, hold(rows_of(joint_sum, i), *waits), rows_of(joint_back, i)))

    first = joint_part(0)
    second = joint_part(1, first.sent)
    up_gather = WideGather(near_up.piece(second.sent))
    near_down.advance(up_gather.sent)
    oth_low = other_grad(parts, joints, rows, (near_down.sent,))
    oth_core, oth_mid = to_core(oth_low), to_middle(oth_low)
    first.advance(oth_low)
    up_gather.advance(first.sent)
    down_gather = WideGather(near_down.piece(up_gather.sent))
    second.advance(down_gather.sent)
    first.advance(second.sent)
    up_gather.advance(first.sent)
    down_gather.advance(up_gather.sent)
    second.advance(down_gather.sent)
    first = WideGather(first.piece(second.sent))
    down_gather.advance(first.sent)
    second = WideGather(second.piece(down_gather.sent))
    first.advance(second.sent)
    second.advance(first.sent)
    first.advance(second.sent)
    token_grad = take_back(
        item_lengths, me, hold(oth_core, first.sent), hold(oth_mid, first.sent), resid_one,
        parts, joints,
    )
    second.advance(first.sent)
    w_up_grad = up_gather.whole(token_grad).astype(F32)
    w_down_grad = down_gather.whole(w_up_grad).astype(F32)
    qk_grad = first.whole(w_down_grad).astype(F32)
    vo_grad = second.whole(qk_grad).astype(F32)
    bq, bv, bu, gain_ffn_g, shift_ffn_g, b_down_g, gain_attn_g, shift_attn_g, b_out_g = spread_small(
        vo_grad, cols, units
    )
    joint_grads = [qk_grad[:cols], qk_grad[cols:], vo_grad[:cols]]
    w_out_grad = vo_grad[cols : 2 * cols]
    return (
        layer_out,
        token_grad,
        joint_grads[0].T,
        bq,
        joint_grads[1].T,
        joint_grads[2].T,
        bv,
        w_out_grad,
        b_out_g,
        gain_attn_g,
        shift_attn_g,
        w_up_grad,
        bu,
        w_down_grad,
        b_down_g,
        gain_ffn_g,
        shift_ffn_g,
    )


def take_back_kernel(lens_ref, me_ref, core_ref, mid_ref, *refs):
    ds, weights, resid_ref, out_ref, oth_s, oth_sem = refs[0:4], refs[4:8], *refs[8:]
    flag, use_core = neighbour(lens_ref, me_ref, resid_ref.shape[0])
    other = pick_other(use_core, core_ref, mid_ref, oth_s, oth_sem)
    arrive(*ds, *weights, resid_ref)
    other.wait()
    depth = ds[0].shape[1]

    def features_of(cs):
        total = resid_ref[:, cs] + jnp.where(flag, oth_s[:, cs].astype(F32), 0.0)
        for d_ref, w_ref in zip(ds, weights):
            total = total + dot(d_ref[...], w_ref[0:depth, cs])
        out_ref[:, cs] = total

    chunks(out_ref.shape[1], 256, features_of)


def take_back(lens, me, core, mid, resid, ds, joints):
    rows, width = resid.shape
    depth = ds[0].shape[1]
    return call(
        take_back_kernel, "take_back", [shape((rows, width), F32)],
        (lens, me, core, mid, *ds, *joints, resid), smem=2, raw=(2, 3),
        part={i: (0, rows) for i in range(4, 8)} | {i: (0, depth) for i in range(8, 12)},
        scratch=[pltpu.VMEM(core.shape, BF), pltpu.SemaphoreType.DMA],
    )[0]


def solution(mesh):
    rows_spec = P(("wide", "narrow"), None)
    col_spec = P(None, "narrow")
    vec_spec = P("narrow")
    row_spec = P("narrow", None)
    full = P()
    return jax.shard_map(
        local,
        mesh=mesh,
        in_specs=(
            rows_spec, P("wide"), col_spec, vec_spec, col_spec, col_spec, vec_spec, row_spec, full,
            full, full, col_spec, vec_spec, row_spec, full, full, full, rows_spec,
        ),
        out_specs=(
            rows_spec, rows_spec, col_spec, vec_spec, col_spec, col_spec, vec_spec, row_spec, full,
            full, full, col_spec, vec_spec, row_spec, full, full, full,
        ),
        check_vma=False,
    )
```

profile of v0, /device:TPU:0, one launch (start us, length us, event | category | flops | bytes accessed | tf_op | source)
XLA Modules:
  0.0 293.4 jit_solution(5023309572128786726)
XLA Ops:
  2.2 2.4 pack_joint.1.a0_ref.refs_2_.refs_13_.refs_5_.refs_4_.refs_8_
  4.7 3.5 %collective-permute-start.2 = (bf16[784,768]{1,0:T(8,128)(2,1)}, bf16[784,768]{1,0:T(8,128)(2,1)S(1)}, u32[]{:S(2)}, u32[]{:S(2)}) collective-permute-start(bf16[784,768]{1,0:T(8,128)(2,1)} %pack_joint.1.a0_ref.refs_2_.refs_13_.refs_5_.refs_4_.refs_8_), channel_id=1, source_target_pairs={{0,1},{1,0},{2,3},{3,2},{4,5},{5,4},{6,7},{7,6},{8,9},{9,8},{10,11... | collective-permute-start | bytes 3612680 | tf_op jit(solution)/shard_map/ppermute | solution.py:779
  9.2 9.7 %collective-permute-done.3 = bf16[96,768]{1,0:T(8,128)(2,1)S(1)} collective-permute-done((bf16[96,768]{1,0:T(8,128)(2,1)S(1)}, bf16[96,768]{1,0:T(8,128)(2,1)S(1)}, u32[]{:S(2)}, u32[]{:S(2)}) %collective-permute-start.3) | collective-permute-done | bytes 147488 | tf_op jit(solution)/shard_map/ppermute | solution.py:779
  19.8 2.6 collective-permute-start.4
  22.4 7.2 %collective-permute-done.4 = bf16[96,768]{1,0:T(8,128)(2,1)S(1)} collective-permute-done((bf16[96,768]{1,0:T(8,128)(2,1)S(1)}, bf16[96,768]{1,0:T(8,128)(2,1)S(1)}, u32[]{:S(2)}, u32[]{:S(2)}) %collective-permute-start.4) | collective-permute-done | bytes 147488 | tf_op jit(solution)/shard_map/ppermute | solution.py:779
  32.7 12.9 %attend_near.1 = (bf16[512,192]{1,0:T(8,128)(2,1)}, f32[192,512]{1,0:T(8,128)}, f32[3,512]{1,0:T(4,128)}, bf16[512,192]{1,0:T(8,128)(2,1)}, bf16[1024,192]{1,0:T...) custom-call(s32[4]{0:T(128)} %refs_0_.11, ...), custom_call_target="tpu_custom_call" | custom-call | flops 1000 | bytes 1000 | tf_op jit(solution)/shard_map/attend_near/pallas_call | solution.py:347
  52.0 12.8 %attend_far.1 = (bf16[512,192]{1,0:T(8,128)(2,1)}, f32[192,512]{1,0:T(8,128)}, f32[3,512]{1,0:T(4,128)}, bf16[512,192]{1,0:T(8,128)(2,1)}, bf16[1024,192]{1,0:T(...) custom-call(s32[4]{0:T(128)} %refs_0_.11, ...), custom_call_target="tpu_custom_call" | custom-call | flops 1000 | bytes 1000 | tf_op jit(solution)/shard_map/attend_far/pallas_call | solution.py:347
  64.8 10.1 %norm_near.1 = (f32[512,768]{1,0:T(8,128)}, f32[512,1]{1,0:T(8,128)}, bf16[512,768]{1,0:T(8,128)(2,1)}, bf16[512,768]{1,0:T(8,128)(2,1)}, bf16[512,768]{1,0:T(8,...) custom-call(bf16[512,768]{1,0:T(8,128)(2,1)} %refs_11_.11, ...), custom_call_target="tpu_custom_call" | custom-call | flops 1000 | bytes 1000 | tf_op jit(solution)/shard_map/norm_near/pallas_call | solution.py:136
  77.2 2.8 collective-permute-done.12.refs_4_
  82.2 13.8 %ffn_far.1 = (bf16[512,768]{1,0:T(8,128)(2,1)}, bf16[512,768]{1,0:T(8,128)(2,1)}, bf16[512,768]{1,0:T(8,128)(2,1)}, bf16[512,768]{1,0:T(8,128)(2,1)}, f32[8,768]...) custom-call(bf16[512,768]{1,0:T(8,128)(2,1)} %get-tuple-element.145., ...), custom_call_target="tpu_custom_call" | custom-call | flops 1000 | bytes 1000 | tf_op jit(solution)/shard_map/ffn_far/pallas_call | solution.py:136
  96.6 7.8 %ffn_back.1 = (bf16[768,768]{1,0:T(8,128)(2,1)}, bf16[768,768]{1,0:T(8,128)(2,1)}, f32[1,768]{1,0:T(1,128)}, f32[512,768]{1,0:T(8,128)}) custom-call(bf16[512,768]{1,0:T(8,128)(2,1)} %get-tuple-element.152.refs_0_, bf16[512,768]{1,0:T(8,128)(2,1)} %get-tuple-element.157.refs_1_, bf16[768,768]{1,0:T(8,128)(2,1)} %copy-done.5, ...), custom_call_target="tpu_custom_call" | custom-call | flops 1000 | bytes 1000 | tf_op jit(solution)/shard_map/ffn_back/pallas_call | solution.py:136
  109.5 13.2 %ffn_last.1 = (bf16[768,768]{1,0:T(8,128)(2,1)}, bf16[768,768]{1,0:T(8,128)(2,1)}, f32[1,768]{1,0:T(1,128)}, bf16[768,768]{1,0:T(8,128)(2,1)}, bf16[768,768]{1,0...) custom-call(bf16[512,768]{1,0:T(8,128)(2,1)} %get-tuple-element.152.refs_0_, ...), custom_call_target="tpu_custom_call" | custom-call | flops 1000 | bytes 1000 | tf_op jit(solution)/shard_map/ffn_last/pallas_call | solution.py:136
  123.7 11.3 %attend_back.4 = (bf16[832,768]{1,0:T(8,128)(2,1)}, bf16[1024,576]{1,0:T(8,128)(2,1)}) custom-call(s32[4]{0:T(128)} %refs_0_.11, s32[1]{0:T(128)} %bitcast.me_ref.refs_1_, bf16[512,768]{1,0:T(8,128)(2,1)} %collective-permute-done.core_ref.refs_2_, bf16[512,768]{1,0:T(8,128)(2,1)} %collective-permute-done.1.mid_ref.refs_3_, ...), custom_call_target="tpu_custom_call" | custom-call | flops 1000 | bytes 1000 | tf_op jit(solution)/shard_map/attend_back/pallas_call | solution.py:136
  139.5 2.6 add_convert_fusion.2.refs_15_
  143.7 11.3 %attend_back.5 = (bf16[832,768]{1,0:T(8,128)(2,1)}, bf16[1024,576]{1,0:T(8,128)(2,1)}) custom-call(s32[4]{0:T(128)} %refs_0_.11, s32[1]{0:T(128)} %bitcast.me_ref.refs_1_, bf16[512,768]{1,0:T(8,128)(2,1)} %collective-permute-done.core_ref.refs_2_, bf16[512,768]{1,0:T(8,128)(2,1)} %collective-permute-done.1.mid_ref.refs_3_, ...), custom_call_target="tpu_custom_call" | custom-call | flops 1000 | bytes 1000 | tf_op jit(solution)/shard_map/attend_back/pallas_call | solution.py:136
  155.0 5.0 %collective-permute-done.21 = bf16[768,768]{1,0:T(8,128)(2,1)} collective-permute-done((bf16[768,768]{1,0:T(8,128)(2,1)S(1)}, bf16[768,768]{1,0:T(8,128)(2,1)}, u32[]{:S(2)}, u32[]{:S(2)}) %collective-permute-start.21) | collective-permute-done | bytes 1179680 | tf_op jit(solution)/shard_map/ppermute | solution.py:779
  165.2 2.3 collective-permute-start.22
  169.8 11.4 %attend_back.6 = (bf16[832,768]{1,0:T(8,128)(2,1)}, bf16[1024,576]{1,0:T(8,128)(2,1)}) custom-call(s32[4]{0:T(128)} %refs_0_.11, s32[1]{0:T(128)} %bitcast.me_ref.refs_1_, bf16[512,768]{1,0:T(8,128)(2,1)} %collective-permute-done.core_ref.refs_2_, bf16[512,768]{1,0:T(8,128)(2,1)} %collective-permute-done.1.mid_ref.refs_3_, ...), custom_call_target="tpu_custom_call" | custom-call | flops 1000 | bytes 1000 | tf_op jit(solution)/shard_map/attend_back/pallas_call | solution.py:136
  184.6 3.4 %collective-permute-start.25 = (bf16[96,768]{1,0:T(8,128)(2,1)S(1)}, bf16[96,768]{1,0:T(8,128)(2,1)S(1)}, u32[]{:S(2)}, u32[]{:S(2)}) collective-permute-start(bf16[96,768]{1,0:T(8,128)(2,1)S(1)} %constant_dynamic-slice_fusion.8.refs_14_), channel_id=1, source_target_pairs={{0,16},{4,20},{8,24},{12,28},{16,0},{20,4},{24,8},{28,12},{1,17},{... | collective-permute-start | bytes 442376 | tf_op jit(solution)/shard_map/ppermute | solution.py:779
  187.9 11.1 %attend_back.7 = (bf16[832,768]{1,0:T(8,128)(2,1)}, bf16[1024,576]{1,0:T(8,128)(2,1)}) custom-call(s32[4]{0:T(128)} %refs_0_.11, s32[1]{0:T(128)} %bitcast.me_ref.refs_1_, bf16[512,768]{1,0:T(8,128)(2,1)} %collective-permute-done.core_ref.refs_2_, bf16[512,768]{1,0:T(8,128)(2,1)} %collective-permute-done.1.mid_ref.refs_3_, ...), custom_call_target="tpu_custom_call" | custom-call | flops 1000 | bytes 1000 | tf_op jit(solution)/shard_map/attend_back/pallas_call | solution.py:136
  211.8 6.6 %other_grad.1 = bf16[512,768]{1,0:T(8,128)(2,1)} custom-call(bf16[1024,576]{1,0:T(8,128)(2,1)} %get-tuple-element.209.refs_0_.refs_4_, bf16[1024,576]{1,0:T(8,128)(2,1)} %get-tuple-element.210.refs_1_.refs_5_, bf16[1024,576]{1,0:T(8,128)(2,1)} %get-tuple-element.211.refs_2_.refs_6_, bf16[1024,576]{1,0:T(8,128)(2,1)} %get-tuple-element.212.refs_3_.refs_7_, ...), custom_call_target="tpu_custom_call" | custom-call | flops 1000 | bytes 1000 | tf_op jit(solution)/shard_map/other_grad/pallas_call | solution.py:136
  226.6 9.7 %collective-permute-done.37 = bf16[192,768]{1,0:T(8,128)(2,1)S(1)} collective-permute-done((bf16[192,768]{1,0:T(8,128)(2,1)S(1)}, bf16[192,768]{1,0:T(8,128)(2,1)S(1)}, u32[]{:S(2)}, u32[]{:S(2)}) %collective-permute-start.37) | collective-permute-done | bytes 294944 | tf_op jit(solution)/shard_map/ppermute | solution.py:779
  237.2 2.8 collective-permute-done.35
  240.1 3.3 %collective-permute-done.34 = bf16[48,768]{1,0:T(8,128)(2,1)S(1)} collective-permute-done((bf16[48,768]{1,0:T(8,128)(2,1)S(1)}, bf16[48,768]{1,0:T(8,128)(2,1)S(1)}, u32[]{:S(2)}, u32[]{:S(2)}) %collective-permute-start.34) | collective-permute-done | bytes 73760 | tf_op jit(solution)/shard_map/ppermute | solution.py:779
  243.4 8.1 %collective-permute-done.40 = bf16[192,768]{1,0:T(8,128)(2,1)S(1)} collective-permute-done((bf16[192,768]{1,0:T(8,128)(2,1)S(1)}, bf16[192,768]{1,0:T(8,128)(2,1)S(1)}, u32[]{:S(2)}, u32[]{:S(2)}) %collective-permute-start.40) | collective-permute-done | bytes 294944 | tf_op jit(solution)/shard_map/ppermute | solution.py:779
  251.7 3.0 %collective-permute-start.42 = (bf16[56,768]{1,0:T(8,128)(2,1)S(1)}, bf16[56,768]{1,0:T(8,128)(2,1)S(1)}, u32[]{:S(2)}, u32[]{:S(2)}) collective-permute-start(bf16[56,768]{1,0:T(8,128)(2,1)S(1)} %add_convert_fusion.18), channel_id=1, source_target_pairs={{0,16},{4,20},{8,24},{12,28},{16,0},{20,4},{24,8},{28,12},{1,17},{... | collective-permute-start | bytes 258056 | tf_op jit(solution)/shard_map/ppermute | solution.py:779
  254.7 4.7 %collective-permute-done.38 = bf16[48,768]{1,0:T(8,128)(2,1)S(1)} collective-permute-done((bf16[48,768]{1,0:T(8,128)(2,1)S(1)}, bf16[48,768]{1,0:T(8,128)(2,1)S(1)}, u32[]{:S(2)}, u32[]{:S(2)}) %collective-permute-start.38) | collective-permute-done | bytes 73760 | tf_op jit(solution)/shard_map/ppermute | solution.py:779
  261.7 3.0 %collective-permute-done.41 = bf16[96,768]{1,0:T(8,128)(2,1)S(1)} collective-permute-done((bf16[96,768]{1,0:T(8,128)(2,1)S(1)}, bf16[96,768]{1,0:T(8,128)(2,1)S(1)}, u32[]{:S(2)}, u32[]{:S(2)}) %collective-permute-start.41) | collective-permute-done | bytes 147488 | tf_op jit(solution)/shard_map/ppermute | solution.py:779
  266.9 8.2 %take_back.1 = f32[512,768]{1,0:T(8,128)} custom-call(s32[4]{0:T(128)} %refs_0_.11, s32[1]{0:T(128)} %bitcast.me_ref.refs_1_, bf16[512,768]{1,0:T(8,128)(2,1)} %copy-done.27, bf16[512,768]{1,0:T(8,128)(2,1)} %copy-done.28, bf16[1024,576]{1,0:T(8,128)(2,1)} %get-tuple-element.209.refs_0_.refs_4_, bf16[1024,576]{1,0:T(8,128)(2,1)} %get-tuple-element.210.refs_1_.refs_5_, ...), custom_call_target="tpu_custom_call" | custom-call | flops 1000 | bytes 1000 | tf_op jit(solution)/shard_map/take_back/pallas_call | solution.py:136
  278.1 2.9 fusion.1
  281.1 2.5 collective-permute-done.44
  284.8 4.9 %collective-permute-done.48 = bf16[224,768]{1,0:T(8,128)(2,1)S(1)} collective-permute-done((bf16[224,768]{1,0:T(8,128)(2,1)S(1)}, bf16[224,768]{1,0:T(8,128)(2,1)S(1)}, u32[]{:S(2)}, u32[]{:S(2)}) %collective-permute-start.48) | collective-permute-done | bytes 344096 | tf_op jit(solution)/shard_map/ppermute | solution.py:779
  (197 shorter events, 74.7 us)
Async XLA Ops:
  0.7 18.2 %collective-permute-start.1 = (bf16[512,768]{1,0:T(8,128)(2,1)}, bf16[512,768]{1,0:T(8,128)(2,1)}, u32[]{:S(2)}, u32[]{:S(2)}) collective-permute-start(bf16[512,768]{1,0:T(8,128)(2,1)} %refs_11_.11), channel_id=1, source_target_pairs={{1,2},{2,1},{5,6},{6,5},{9,10},{10,9},{13,14},{14,13},{17,18},{18,... | collective-permute-start | bytes 2359304 | tf_op jit(solution)/shard_map/ppermute | solution.py:791
  4.7 25.7 %collective-permute-start.2 = (bf16[784,768]{1,0:T(8,128)(2,1)}, bf16[784,768]{1,0:T(8,128)(2,1)S(1)}, u32[]{:S(2)}, u32[]{:S(2)}) collective-permute-start(bf16[784,768]{1,0:T(8,128)(2,1)} %pack_joint.1.a0_ref.refs_2_.refs_13_.refs_5_.refs_4_.refs_8_), channel_id=1, source_target_pairs={{0,1},{1,0},{2,3},{3,2},{4,5},{5,4},{6,7},{7,6},{8,9},{9,8},{10,11... | collective-permute-start | bytes 3612680 | tf_op jit(solution)/shard_map/ppermute | solution.py:779
  18.8 28.1 %collective-permute-start.5 = (bf16[784,768]{1,0:T(8,128)(2,1)}, bf16[784,768]{1,0:T(8,128)(2,1)S(1)}, u32[]{:S(2)}, u32[]{:S(2)}) collective-permute-start(bf16[784,768]{1,0:T(8,128)(2,1)} %pack_joint.1.a0_ref.refs_2_.refs_13_.refs_5_.refs_4_.refs_8_), channel_id=1, source_target_pairs={{0,2},{1,3},{2,0},{3,1},{4,6},{5,7},{6,4},{7,5},{8,10},{9,11},{10,... | collective-permute-start | bytes 3612680 | tf_op jit(solution)/shard_map/ppermute | solution.py:779
  18.9 13.8 %collective-permute-start = (bf16[512,768]{1,0:T(8,128)(2,1)S(1)}, bf16[512,768]{1,0:T(8,128)(2,1)}, u32[]{:S(2)}, u32[]{:S(2)}) collective-permute-start(bf16[512,768]{1,0:T(8,128)(2,1)S(1)} %copy-done.3), channel_id=1, source_target_pairs={{0,1},{1,0},{2,3},{3,2},{4,5},{5,4},{6,7},{7,6},{8,9},{9,8},{10,11... | collective-permute-start | bytes 2359304 | tf_op jit(solution)/shard_map/ppermute | solution.py:779
  32.0 13.6 %collective-permute-start.6 = (bf16[192,768]{1,0:T(8,128)(2,1)S(1)}, bf16[192,768]{1,0:T(8,128)(2,1)}, u32[]{:S(2)}, u32[]{:S(2)}) collective-permute-start(bf16[192,768]{1,0:T(8,128)(2,1)S(1)} %maximum_select_fusion.9.refs_0_), channel_id=1, source_target_pairs={{0,8},{4,12},{8,0},{12,4},{16,24},{20,28},{24,16},{28,20},{1,9},{5... | collective-permute-start | bytes 884744 | tf_op jit(solution)/shard_map/ppermute | solution.py:779
  47.1 17.7 %collective-permute-start.8 = (bf16[768,768]{1,0:T(8,128)(2,1)}, bf16[768,768]{1,0:T(8,128)(2,1)}, u32[]{:S(2)}, u32[]{:S(2)}) collective-permute-start(bf16[768,768]{1,0:T(8,128)(2,1)} %refs_9_.5), channel_id=1, source_target_pairs={{0,1},{1,0},{2,3},{3,2},{4,5},{5,4},{6,7},{7,6},{8,9},{9,8},{10,11... | collective-permute-start | bytes 3538952 | tf_op jit(solution)/shard_map/ppermute | solution.py:779
  47.6 17.2 %collective-permute-start.9 = (bf16[768,768]{1,0:T(8,128)(2,1)}, bf16[768,768]{1,0:T(8,128)(2,1)}, u32[]{:S(2)}, u32[]{:S(2)}) collective-permute-start(bf16[768,768]{1,0:T(8,128)(2,1)} %refs_7_.1), channel_id=1, source_target_pairs={{0,1},{1,0},{2,3},{3,2},{4,5},{5,4},{6,7},{7,6},{8,9},{9,8},{10,11... | collective-permute-start | bytes 3538952 | tf_op jit(solution)/shard_map/ppermute | solution.py:779
  47.7 28.9 %collective-permute-start.10 = (bf16[768,768]{1,0:T(8,128)(2,1)}, bf16[768,768]{1,0:T(8,128)(2,1)}, u32[]{:S(2)}, u32[]{:S(2)}) collective-permute-start(bf16[768,768]{1,0:T(8,128)(2,1)} %refs_9_.5), channel_id=1, source_target_pairs={{0,2},{1,3},{2,0},{3,1},{4,6},{5,7},{6,4},{7,5},{8,10},{9,11},{10,... | collective-permute-start | bytes 3538952 | tf_op jit(solution)/shard_map/ppermute | solution.py:779
  49.2 25.7 %collective-permute-start.11 = (bf16[384,768]{1,0:T(8,128)(2,1)S(1)}, bf16[384,768]{1,0:T(8,128)(2,1)}, u32[]{:S(2)}, u32[]{:S(2)}) collective-permute-start(bf16[384,768]{1,0:T(8,128)(2,1)S(1)} %maximum_select_fusion.4.refs_0_), channel_id=1, source_target_pairs={{0,4},{4,0},{8,12},{12,8},{16,20},{20,16},{24,28},{28,24},{1,5},{5... | collective-permute-start | bytes 1769480 | tf_op jit(solution)/shard_map/ppermute | solution.py:779
  106.5 29.0 %collective-permute-start.17 = (bf16[768,768]{1,0:T(8,128)(2,1)S(1)}, bf16[768,768]{1,0:T(8,128)(2,1)}, u32[]{:S(2)}, u32[]{:S(2)}) collective-permute-start(bf16[768,768]{1,0:T(8,128)(2,1)S(1)} %add_convert_fusion.5.refs_15_), channel_id=1, source_target_pairs={{0,2},{1,3},{2,0},{3,1},{4,6},{5,7},{6,4},{7,5},{8,10},{9,11},{10,... | collective-permute-start | bytes 3538952 | tf_op jit(solution)/shard_map/ppermute | solution.py:779
  122.8 14.9 %collective-permute-start.19 = (bf16[768,768]{1,0:T(8,128)(2,1)}, bf16[768,768]{1,0:T(8,128)(2,1)}, u32[]{:S(2)}, u32[]{:S(2)}) collective-permute-start(bf16[768,768]{1,0:T(8,128)(2,1)} %get-tuple-element.194), channel_id=1, source_target_pairs={{0,1},{1,0},{2,3},{3,2},{4,5},{5,4},{6,7},{7,6},{8,9},{9,8},{10,11... | collective-permute-start | bytes 3538952 | tf_op jit(solution)/shard_map/ppermute | solution.py:779
  123.3 36.7 %collective-permute-start.21 = (bf16[768,768]{1,0:T(8,128)(2,1)S(1)}, bf16[768,768]{1,0:T(8,128)(2,1)}, u32[]{:S(2)}, u32[]{:S(2)}) collective-permute-start(bf16[768,768]{1,0:T(8,128)(2,1)S(1)} %copy-done.10), channel_id=1, source_target_pairs={{0,2},{1,3},{2,0},{3,1},{4,6},{5,7},{6,4},{7,5},{8,10},{9,11},{10,... | collective-permute-start | bytes 3538952 | tf_op jit(solution)/shard_map/ppermute | solution.py:779
  142.1 19.5 %collective-permute-start.20 = (bf16[832,768]{1,0:T(8,128)(2,1)}, bf16[832,768]{1,0:T(8,128)(2,1)}, u32[]{:S(2)}, u32[]{:S(2)}) collective-permute-start(bf16[832,768]{1,0:T(8,128)(2,1)} %get-tuple-element.197), channel_id=1, source_target_pairs={{0,1},{1,0},{2,3},{3,2},{4,5},{5,4},{6,7},{7,6},{8,9},{9,8},{10,11... | collective-permute-start | bytes 3833864 | tf_op jit(solution)/shard_map/ppermute | solution.py:779
  142.1 21.3 %collective-permute-start.18 = (bf16[384,768]{1,0:T(8,128)(2,1)S(1)}, bf16[384,768]{1,0:T(8,128)(2,1)}, u32[]{:S(2)}, u32[]{:S(2)}) collective-permute-start(bf16[384,768]{1,0:T(8,128)(2,1)S(1)} %constant_dynamic-slice_fusion.11.refs_14_), channel_id=1, source_target_pairs={{0,4},{4,0},{8,12},{12,8},{16,20},{20,16},{24,28},{28,24},{1,5},{5... | collective-permute-start | bytes 1769480 | tf_op jit(solution)/shard_map/ppermute | solution.py:779
  165.2 16.1 %collective-permute-start.22 = (bf16[192,768]{1,0:T(8,128)(2,1)S(1)}, bf16[192,768]{1,0:T(8,128)(2,1)}, u32[]{:S(2)}, u32[]{:S(2)}) collective-permute-start(bf16[192,768]{1,0:T(8,128)(2,1)S(1)} %constant_dynamic-slice_fusion.10.refs_15_), channel_id=1, source_target_pairs={{0,8},{4,12},{8,0},{12,4},{16,24},{20,28},{24,16},{28,20},{1,9},{5... | collective-permute-start | bytes 884744 | tf_op jit(solution)/shard_map/ppermute | solution.py:779
  167.5 14.9 %collective-permute-start.23 = (bf16[384,768]{1,0:T(8,128)(2,1)S(1)}, bf16[384,768]{1,0:T(8,128)(2,1)}, u32[]{:S(2)}, u32[]{:S(2)}) collective-permute-start(bf16[384,768]{1,0:T(8,128)(2,1)S(1)} %constant_dynamic-slice_fusion.9.refs_16_), channel_id=1, source_target_pairs={{0,4},{4,0},{8,12},{12,8},{16,20},{20,16},{24,28},{28,24},{1,5},{5... | collective-permute-start | bytes 1769480 | tf_op jit(solution)/shard_map/ppermute | solution.py:779
  169.1 29.9 %collective-permute-start.26 = (bf16[832,768]{1,0:T(8,128)(2,1)S(1)}, bf16[832,768]{1,0:T(8,128)(2,1)}, u32[]{:S(2)}, u32[]{:S(2)}) collective-permute-start(bf16[832,768]{1,0:T(8,128)(2,1)S(1)} %add_convert_fusion.refs_14_), channel_id=1, source_target_pairs={{0,2},{1,3},{2,0},{3,1},{4,6},{5,7},{6,4},{7,5},{8,10},{9,11},{10,... | collective-permute-start | bytes 3833864 | tf_op jit(solution)/shard_map/ppermute | solution.py:779
  183.7 17.7 %collective-permute-start.27 = (bf16[832,768]{1,0:T(8,128)(2,1)}, bf16[832,768]{1,0:T(8,128)(2,1)}, u32[]{:S(2)}, u32[]{:S(2)}) collective-permute-start(bf16[832,768]{1,0:T(8,128)(2,1)} %get-tuple-element.215), channel_id=1, source_target_pairs={{0,1},{1,0},{2,3},{3,2},{4,5},{5,4},{6,7},{7,6},{8,9},{9,8},{10,11... | collective-permute-start | bytes 3833864 | tf_op jit(solution)/shard_map/ppermute | solution.py:779
  183.8 25.4 %collective-permute-start.24 = (bf16[192,768]{1,0:T(8,128)(2,1)S(1)}, bf16[192,768]{1,0:T(8,128)(2,1)}, u32[]{:S(2)}, u32[]{:S(2)}) collective-permute-start(bf16[192,768]{1,0:T(8,128)(2,1)S(1)} %constant_dynamic-slice_fusion.7.refs_15_), channel_id=1, source_target_pairs={{0,8},{4,12},{8,0},{12,4},{16,24},{20,28},{24,16},{28,20},{1,9},{5... | collective-permute-start | bytes 884744 | tf_op jit(solution)/shard_map/ppermute | solution.py:779
  184.6 23.1 %collective-permute-start.25 = (bf16[96,768]{1,0:T(8,128)(2,1)S(1)}, bf16[96,768]{1,0:T(8,128)(2,1)S(1)}, u32[]{:S(2)}, u32[]{:S(2)}) collective-permute-start(bf16[96,768]{1,0:T(8,128)(2,1)S(1)} %constant_dynamic-slice_fusion.8.refs_14_), channel_id=1, source_target_pairs={{0,16},{4,20},{8,24},{12,28},{16,0},{20,4},{24,8},{28,12},{1,17},{... | collective-permute-start | bytes 442376 | tf_op jit(solution)/shard_map/ppermute | solution.py:779
  203.5 15.0 %collective-permute-start.29 = (bf16[192,768]{1,0:T(8,128)(2,1)}, bf16[192,768]{1,0:T(8,128)(2,1)}, u32[]{:S(2)}, u32[]{:S(2)}) collective-permute-start(bf16[192,768]{1,0:T(8,128)(2,1)} %constant_dynamic-slice_fusion.6), channel_id=1, source_target_pairs={{0,4},{4,0},{8,12},{12,8},{16,20},{20,16},{24,28},{28,24},{1,5},{5... | collective-permute-start | bytes 884744 | tf_op jit(solution)/shard_map/ppermute | solution.py:779
  206.1 17.1 %collective-permute-start.31 = (bf16[224,768]{1,0:T(8,128)(2,1)}, bf16[224,768]{1,0:T(8,128)(2,1)}, u32[]{:S(2)}, u32[]{:S(2)}) collective-permute-start(bf16[224,768]{1,0:T(8,128)(2,1)} %constant_dynamic-slice_fusion.5), channel_id=1, source_target_pairs={{0,4},{4,0},{8,12},{12,8},{16,20},{20,16},{24,28},{28,24},{1,5},{5... | collective-permute-start | bytes 1032200 | tf_op jit(solution)/shard_map/ppermute | solution.py:779
  210.3 12.9 %collective-permute-start.32 = (bf16[96,768]{1,0:T(8,128)(2,1)S(1)}, bf16[96,768]{1,0:T(8,128)(2,1)S(1)}, u32[]{:S(2)}, u32[]{:S(2)}) collective-permute-start(bf16[96,768]{1,0:T(8,128)(2,1)S(1)} %constant_dynamic-slice_fusion.4.refs_8_), channel_id=1, source_target_pairs={{0,16},{4,20},{8,24},{12,28},{16,0},{20,4},{24,8},{28,12},{1,17},{... | collective-permute-start | bytes 442376 | tf_op jit(solution)/shard_map/ppermute | solution.py:779
  218.5 46.6 %collective-permute-start.28 = (bf16[512,768]{1,0:T(8,128)(2,1)}, bf16[512,768]{1,0:T(8,128)(2,1)S(1)}, u32[]{:S(2)}, u32[]{:S(2)}) collective-permute-start(bf16[512,768]{1,0:T(8,128)(2,1)} %other_grad.1), channel_id=1, source_target_pairs={{0,1},{1,0},{2,3},{3,2},{4,5},{5,4},{6,7},{7,6},{8,9},{9,8},{10,11... | collective-permute-start | bytes 2359304 | tf_op jit(solution)/shard_map/ppermute | solution.py:779
  218.5 47.5 %collective-permute-start.43 = (bf16[512,768]{1,0:T(8,128)(2,1)}, bf16[512,768]{1,0:T(8,128)(2,1)S(1)}, u32[]{:S(2)}, u32[]{:S(2)}) collective-permute-start(bf16[512,768]{1,0:T(8,128)(2,1)} %other_grad.1), channel_id=1, source_target_pairs={{1,2},{2,1},{5,6},{6,5},{9,10},{10,9},{13,14},{14,13},{17,18},{18,... | collective-permute-start | bytes 2359304 | tf_op jit(solution)/shard_map/ppermute | solution.py:791
  223.2 13.1 %collective-permute-start.37 = (bf16[192,768]{1,0:T(8,128)(2,1)S(1)}, bf16[192,768]{1,0:T(8,128)(2,1)S(1)}, u32[]{:S(2)}, u32[]{:S(2)}) collective-permute-start(bf16[192,768]{1,0:T(8,128)(2,1)S(1)} %maximum_select_fusion.10), channel_id=1, source_target_pairs={{0,8},{4,12},{8,0},{12,4},{16,24},{20,28},{24,16},{28,20},{1,9},{5... | collective-permute-start | bytes 884744 | tf_op jit(solution)/shard_map/ppermute | solution.py:779
  223.3 13.2 %collective-permute-start.36 = (bf16[96,768]{1,0:T(8,128)(2,1)S(1)}, bf16[96,768]{1,0:T(8,128)(2,1)S(1)}, u32[]{:S(2)}, u32[]{:S(2)}) collective-permute-start(bf16[96,768]{1,0:T(8,128)(2,1)S(1)} %add_convert_fusion.16), channel_id=1, source_target_pairs={{0,16},{4,20},{8,24},{12,28},{16,0},{20,4},{24,8},{28,12},{1,17},{... | collective-permute-start | bytes 442376 | tf_op jit(solution)/shard_map/ppermute | solution.py:779
  226.2 13.8 %collective-permute-start.35 = (bf16[112,768]{1,0:T(8,128)(2,1)S(1)}, bf16[112,768]{1,0:T(8,128)(2,1)S(1)}, u32[]{:S(2)}, u32[]{:S(2)}) collective-permute-start(bf16[112,768]{1,0:T(8,128)(2,1)S(1)} %constant_dynamic-slice_fusion.2), channel_id=1, source_target_pairs={{0,8},{4,12},{8,0},{12,4},{16,24},{20,28},{24,16},{28,20},{1,9},{5... | collective-permute-start | bytes 516104 | tf_op jit(solution)/shard_map/ppermute | solution.py:779
  236.5 40.0 %collective-permute-start.46 = (bf16[384,768]{1,0:T(8,128)(2,1)S(1)}, bf16[384,768]{1,0:T(8,128)(2,1)S(1)}, u32[]{:S(2)}, u32[]{:S(2)}) collective-permute-start(bf16[384,768]{1,0:T(8,128)(2,1)S(1)} %maximum_select_fusion.5), channel_id=1, source_target_pairs={{0,4},{4,0},{8,12},{12,8},{16,20},{20,16},{24,28},{28,24},{1,5},{5... | collective-permute-start | bytes 1769480 | tf_op jit(solution)/shard_map/ppermute | solution.py:779
  260.9 17.2 %collective-permute-start.45 = (bf16[384,768]{1,0:T(8,128)(2,1)S(1)}, bf16[384,768]{1,0:T(8,128)(2,1)}, u32[]{:S(2)}, u32[]{:S(2)}) collective-permute-start(bf16[384,768]{1,0:T(8,128)(2,1)S(1)} %maximum_select_fusion.6), channel_id=1, source_target_pairs={{0,4},{4,0},{8,12},{12,8},{16,20},{20,16},{24,28},{28,24},{1,5},{5... | collective-permute-start | bytes 1769480 | tf_op jit(solution)/shard_map/ppermute | solution.py:779
  265.1 18.5 %collective-permute-start.44 = (bf16[192,768]{1,0:T(8,128)(2,1)S(1)}, bf16[192,768]{1,0:T(8,128)(2,1)}, u32[]{:S(2)}, u32[]{:S(2)}) collective-permute-start(bf16[192,768]{1,0:T(8,128)(2,1)S(1)} %maximum_select_fusion.12), channel_id=1, source_target_pairs={{0,4},{4,0},{8,12},{12,8},{16,20},{20,16},{24,28},{28,24},{1,5},{5... | collective-permute-start | bytes 884744 | tf_op jit(solution)/shard_map/ppermute | solution.py:779
  275.2 14.4 %collective-permute-start.48 = (bf16[224,768]{1,0:T(8,128)(2,1)S(1)}, bf16[224,768]{1,0:T(8,128)(2,1)S(1)}, u32[]{:S(2)}, u32[]{:S(2)}) collective-permute-start(bf16[224,768]{1,0:T(8,128)(2,1)S(1)} %maximum_select_fusion.8), channel_id=1, source_target_pairs={{0,4},{4,0},{8,12},{12,8},{16,20},{20,16},{24,28},{28,24},{1,5},{5... | collective-permute-start | bytes 1032200 | tf_op jit(solution)/shard_map/ppermute | solution.py:779
  (50 other events, 291.7 us)
where the time goes:
time: 295 us; the launch traced here: 293 us
  Pallas kernels  135 us (46%)
  waiting for transfers between devices  69.9 us (24%)
  starting transfers between devices  42.1 us (14%)
  other arithmetic  32.7 us (11%)
  local copies, waits for them, and re-layouts  12.6 us (4%)
    pallas_call x12, Pallas kernels, call(): pl.pallas_call(body, out_shape=tuple(out_shape), in_specs=in_specs + [ANY...  109 us
    ppermute x47, waiting for transfers between devices, swap(): return lax.ppermute(a, axis, [(i, i ^ distance) for i in range(size)])  69.9 us
    ppermute x47, starting transfers between devices, swap(): return lax.ppermute(a, axis, [(i, i ^ distance) for i in range(size)])  39.9 us
    pallas_call x2, Pallas kernels, attend_pair(): pl.pallas_call(functools.partial(attend_pair_kernel, after=len(after)), o...  25.7 us
    convert_element_type x20, other arithmetic, add_low(): return total.astype(BF)  21.5 us
    unnamed x66, local copies, waits for them, and re-layouts  6.02 us
  transfers between devices with their start and end apart: 49, of which 18 were waited for; matrix products, arithmetic and copies ran while one was open for 12% of the time, Pallas kernels for 41%

commit v1 on v0

--- a/solution.py
+++ b/solution.py
@@ -482,8 +482,9 @@
     b_s[0:1, 0:cols] = jnp.sum(dq.astype(F32), axis=0, keepdims=True)
     b_s[2:3] = bu_ref[...]
     b_s[8:16] = vec_ref[...]
-    grad_ref[4 * cols : 4 * cols + 16] = b_s[...].astype(BF)
-    grad_ref[4 * cols + 16 :] = jnp.zeros((grad_ref.shape[0] - 4 * cols - 16, b_s.shape[1]), BF)
+    at = 2 * cols
+    grad_ref[at : at + 16] = b_s[...].astype(BF)
+    grad_ref[at + 16 : at + 64] = jnp.zeros((48, b_s.shape[1]), BF)
     other()
     send(d_s)
     arrive(own_ref)
@@ -492,10 +493,14 @@
     def weight_terms(cs):
         tok = own_ref[:, cs]
         grad_ref[0:cols, cs] = dot(t_s[0:cols, near], tok).astype(BF)
-        grad_ref[cols : 3 * cols, cs] = (
+        terms = (
             dot(t_s[cols : 3 * cols, near], tok) + dot(t_s[cols : 3 * cols, far], other.buffer[:, cs])
         ).astype(BF)
-        grad_ref[3 * cols : 4 * cols, cs] = dot(t_s[3 * cols : 4 * cols, near], g_ref[:, cs]).astype(BF)
+        grad_ref[cols : 2 * cols, cs] = terms[0:cols]
+        grad_ref[at + 64 : at + 64 + cols, cs] = terms[cols : 2 * cols]
+        grad_ref[at + 64 + cols : at + 64 + 2 * cols, cs] = dot(
+            t_s[3 * cols : 4 * cols, near], g_ref[:, cs]
+        ).astype(BF)
 
     chunks(width, 256, weight_terms)
     send(grad_ref)
@@ -978,46 +983,45 @@
     joint_back = hold(joint_back, joint_sum)
 
     def rows_of(a, part):
-        return a[: 2 * cols] if part == 0 else a[2 * cols :]
-
-    def joint_part(i, *waits):
-        own = rows_of(grads[0], i)
-        return WideSum(add_low(own, hold(rows_of(joint_sum, i), *waits), rows_of(joint_back, i)))
-
-    first = joint_part(0)
-    second = joint_part(1, first.sent)
+        return a[: 2 * cols + 64] if part == 0 else a[2 * cols + 64 :]
+
+    def joint_part(i, own, got):
+        return WideSum(add_low(rows_of(own, i), rows_of(got, i), rows_of(joint_back, i)))
+
+    first = joint_part(0, grads[0], joint_sum)
+    second = joint_part(1, grads[0], hold(joint_sum, first.sent))
     up_gather = WideGather(near_up.piece(second.sent))
     near_down.advance(up_gather.sent)
-    oth_low = other_grad(parts, joints, rows, (near_down.sent,))
-    oth_core, oth_mid = to_core(oth_low), to_middle(oth_low)
+    first.advance(near_down.sent)
+    down_gather = WideGather(near_down.piece(first.sent))
+    up_gather.advance(down_gather.sent)
+    second.advance(up_gather.sent)
+    oth_low = other_grad(parts, joints, rows, (second.sent,))
     first.advance(oth_low)
     up_gather.advance(first.sent)
-    down_gather = WideGather(near_down.piece(up_gather.sent))
-    second.advance(down_gather.sent)
-    first.advance(second.sent)
-    up_gather.advance(first.sent)
     down_gather.advance(up_gather.sent)
+    oth_core, oth_mid = to_core(hold(oth_low, down_gather.sent)), to_middle(hold(oth_low, down_gather.sent))
     second.advance(down_gather.sent)
     first = WideGather(first.piece(second.sent))
     down_gather.advance(first.sent)
     second = WideGather(second.piece(down_gather.sent))
     first.advance(second.sent)
-    second.advance(first.sent)
-    first.advance(second.sent)
     token_grad = take_back(
         item_lengths, me, hold(oth_core, first.sent), hold(oth_mid, first.sent), resid_one,
-        parts, joints,
-    )
-    second.advance(first.sent)
-    w_up_grad = up_gather.whole(token_grad).astype(F32)
-    w_down_grad = down_gather.whole(w_up_grad).astype(F32)
+        parts, joints, (first.sent, second.sent),
+    )
+    second.advance(token_grad)
+    first.advance(second.sent)
+    w_up_grad = up_gather.whole(first.sent).astype(F32)
+    second.advance(w_up_grad)
+    w_down_grad = down_gather.whole(second.sent).astype(F32)
     qk_grad = first.whole(w_down_grad).astype(F32)
+    bq, bv, bu, gain_ffn_g, shift_ffn_g, b_down_g, gain_attn_g, shift_attn_g, b_out_g = spread_small(
+        qk_grad, cols, units
+    )
     vo_grad = second.whole(qk_grad).astype(F32)
-    bq, bv, bu, gain_ffn_g, shift_ffn_g, b_down_g, gain_attn_g, shift_attn_g, b_out_g = spread_small(
-        vo_grad, cols, units
-    )
-    joint_grads = [qk_grad[:cols], qk_grad[cols:], vo_grad[:cols]]
-    w_out_grad = vo_grad[cols : 2 * cols]
+    joint_grads = [qk_grad[:cols], qk_grad[cols : 2 * cols], vo_grad[:cols]]
+    w_out_grad = vo_grad[cols:]
     return (
         layer_out,
         token_grad,
@@ -1056,12 +1060,12 @@
     chunks(out_ref.shape[1], 256, features_of)
 
 
-def take_back(lens, me, core, mid, resid, ds, joints):
+def take_back(lens, me, core, mid, resid, ds, joints, after):
     rows, width = resid.shape
     depth = ds[0].shape[1]
     return call(
         take_back_kernel, "take_back", [shape((rows, width), F32)],
-        (lens, me, core, mid, *ds, *joints, resid), smem=2, raw=(2, 3),
+        (lens, me, core, mid, *ds, *joints, resid), smem=2, raw=(2, 3), after=after,
         part={i: (0, rows) for i in range(4, 8)} | {i: (0, depth) for i in range(8, 12)},
         scratch=[pltpu.VMEM(core.shape, BF), pltpu.SemaphoreType.DMA],
     )[0]

time: 295 us -> 282 us (0.956)
  waiting for transfers between devices: 69.9 us -> 59.4 us
  local copies, waits for them, and re-layouts: 12.6 us -> 8.32 us
    ppermute x47, waiting for transfers between devices: 69.9 us -> 59.4 us  [swap(): return lax.ppermute(a, axis, [(i, i ^ distance) for i in range(size)])]
    unnamed x66 -> x70, local copies, waits for them, and re-layouts: 6.02 us -> 5.62 us
  transfers between devices with their start and end apart: 49 -> 49, of which waited for: 18 -> 17; matrix products, arithmetic and copies ran while one was open for 12% -> 11% of each run, Pallas kernels for 41% -> 43%
where the time goes in v1:
time: 282 us; the launch traced here: 281 us
  Pallas kernels  134 us (48%)
  waiting for transfers between devices  59.4 us (21%)
  starting transfers between devices  45 us (16%)
  other arithmetic  32.5 us (12%)
  local copies, waits for them, and re-layouts  8.32 us (3%)
    pallas_call x12, Pallas kernels, call(): pl.pallas_call(body, out_shape=tuple(out_shape), in_specs=in_specs + [ANY...  109 us
    ppermute x47, waiting for transfers between devices, swap(): return lax.ppermute(a, axis, [(i, i ^ distance) for i in range(size)])  59.4 us
    ppermute x47, starting transfers between devices, swap(): return lax.ppermute(a, axis, [(i, i ^ distance) for i in range(size)])  42.8 us
    pallas_call x2, Pallas kernels, attend_pair(): pl.pallas_call(functools.partial(attend_pair_kernel, after=len(after)), o...  25.7 us
    convert_element_type x20, other arithmetic, add_low(): return total.astype(BF)  19.3 us
    select_n x11, other arithmetic, in_order(): jnp.where(side == 0, jnp.concatenate([mine, got]), jnp.concatenate([got,...  7.3 us
  transfers between devices with their start and end apart: 49, of which 17 were waited for; matrix products, arithmetic and copies ran while one was open for 11% of the time, Pallas kernels for 43%

profile of v1, /device:TPU:0, one launch (start us, length us, event | category | flops | bytes accessed | tf_op | source)
XLA Modules:
  0.0 281.2 jit_solution(7255008480816613961)
XLA Ops:
  2.2 2.4 pack_joint.1.a0_ref.refs_2_.refs_13_.refs_5_.refs_4_.refs_8_
  4.7 3.5 %collective-permute-start.2 = (bf16[784,768]{1,0:T(8,128)(2,1)}, bf16[784,768]{1,0:T(8,128)(2,1)S(1)}, u32[]{:S(2)}, u32[]{:S(2)}) collective-permute-start(bf16[784,768]{1,0:T(8,128)(2,1)} %pack_joint.1.a0_ref.refs_2_.refs_13_.refs_5_.refs_4_.refs_8_), channel_id=1, source_target_pairs={{0,1},{1,0},{2,3},{3,2},{4,5},{5,4},{6,7},{7,6},{8,9},{9,8},{10,11... | collective-permute-start | bytes 3612680 | tf_op jit(solution)/shard_map/ppermute | solution.py:784
  9.2 9.7 %collective-permute-done.3 = bf16[96,768]{1,0:T(8,128)(2,1)S(1)} collective-permute-done((bf16[96,768]{1,0:T(8,128)(2,1)S(1)}, bf16[96,768]{1,0:T(8,128)(2,1)S(1)}, u32[]{:S(2)}, u32[]{:S(2)}) %collective-permute-start.3) | collective-permute-done | bytes 147488 | tf_op jit(solution)/shard_map/ppermute | solution.py:784
  19.8 2.6 collective-permute-start.4
  22.4 7.2 %collective-permute-done.4 = bf16[96,768]{1,0:T(8,128)(2,1)S(1)} collective-permute-done((bf16[96,768]{1,0:T(8,128)(2,1)S(1)}, bf16[96,768]{1,0:T(8,128)(2,1)S(1)}, u32[]{:S(2)}, u32[]{:S(2)}) %collective-permute-start.4) | collective-permute-done | bytes 147488 | tf_op jit(solution)/shard_map/ppermute | solution.py:784
  32.7 12.9 %attend_near.1 = (bf16[512,192]{1,0:T(8,128)(2,1)}, f32[192,512]{1,0:T(8,128)}, f32[3,512]{1,0:T(4,128)}, bf16[512,192]{1,0:T(8,128)(2,1)}, bf16[1024,192]{1,0:T...) custom-call(s32[4]{0:T(128)} %refs_0_.11, ...), custom_call_target="tpu_custom_call" | custom-call | flops 1000 | bytes 1000 | tf_op jit(solution)/shard_map/attend_near/pallas_call | solution.py:347
  52.0 12.8 %attend_far.1 = (bf16[512,192]{1,0:T(8,128)(2,1)}, f32[192,512]{1,0:T(8,128)}, f32[3,512]{1,0:T(4,128)}, bf16[512,192]{1,0:T(8,128)(2,1)}, bf16[1024,192]{1,0:T(...) custom-call(s32[4]{0:T(128)} %refs_0_.11, ...), custom_call_target="tpu_custom_call" | custom-call | flops 1000 | bytes 1000 | tf_op jit(solution)/shard_map/attend_far/pallas_call | solution.py:347
  64.9 10.1 %norm_near.1 = (f32[512,768]{1,0:T(8,128)}, f32[512,1]{1,0:T(8,128)}, bf16[512,768]{1,0:T(8,128)(2,1)}, bf16[512,768]{1,0:T(8,128)(2,1)}, bf16[512,768]{1,0:T(8,...) custom-call(bf16[512,768]{1,0:T(8,128)(2,1)} %refs_11_.11, ...), custom_call_target="tpu_custom_call" | custom-call | flops 1000 | bytes 1000 | tf_op jit(solution)/shard_map/norm_near/pallas_call | solution.py:136
  77.3 2.9 %collective-permute-done.12.refs_4_ = bf16[768,768]{1,0:T(8,128)(2,1)S(1)} collective-permute-done((bf16[768,768]{1,0:T(8,128)(2,1)}, bf16[768,768]{1,0:T(8,128)(2,1)S(1)}, u32[]{:S(2)}, u32[]{:S(2)}) %collective-permute-start.12) | collective-permute-done | bytes 1179680 | tf_op jit(solution)/shard_map/ppermute | solution.py:784
  82.3 13.8 %ffn_far.1 = (bf16[512,768]{1,0:T(8,128)(2,1)}, bf16[512,768]{1,0:T(8,128)(2,1)}, bf16[512,768]{1,0:T(8,128)(2,1)}, bf16[512,768]{1,0:T(8,128)(2,1)}, f32[8,768]...) custom-call(bf16[512,768]{1,0:T(8,128)(2,1)} %get-tuple-element.146., ...), custom_call_target="tpu_custom_call" | custom-call | flops 1000 | bytes 1000 | tf_op jit(solution)/shard_map/ffn_far/pallas_call | solution.py:136
  96.7 7.8 %ffn_back.1 = (bf16[768,768]{1,0:T(8,128)(2,1)}, bf16[768,768]{1,0:T(8,128)(2,1)}, f32[1,768]{1,0:T(1,128)}, f32[512,768]{1,0:T(8,128)}) custom-call(bf16[512,768]{1,0:T(8,128)(2,1)} %get-tuple-element.153.refs_0_, bf16[512,768]{1,0:T(8,128)(2,1)} %get-tuple-element.158.refs_1_, bf16[768,768]{1,0:T(8,128)(2,1)} %copy-done.5, ...), custom_call_target="tpu_custom_call" | custom-call | flops 1000 | bytes 1000 | tf_op jit(solution)/shard_map/ffn_back/pallas_call | solution.py:136
  104.6 2.0 add_convert_fusion.5.refs_15_
  109.5 13.2 %ffn_last.1 = (bf16[768,768]{1,0:T(8,128)(2,1)}, bf16[768,768]{1,0:T(8,128)(2,1)}, f32[1,768]{1,0:T(1,128)}, bf16[768,768]{1,0:T(8,128)(2,1)}, bf16[768,768]{1,0...) custom-call(bf16[512,768]{1,0:T(8,128)(2,1)} %get-tuple-element.153.refs_0_, ...), custom_call_target="tpu_custom_call" | custom-call | flops 1000 | bytes 1000 | tf_op jit(solution)/shard_map/ffn_last/pallas_call | solution.py:136
  123.8 11.3 %attend_back.4 = (bf16[832,768]{1,0:T(8,128)(2,1)}, bf16[1024,576]{1,0:T(8,128)(2,1)}) custom-call(s32[4]{0:T(128)} %refs_0_.11, s32[1]{0:T(128)} %bitcast.me_ref.refs_1_, bf16[512,768]{1,0:T(8,128)(2,1)} %collective-permute-done.core_ref.refs_2_, bf16[512,768]{1,0:T(8,128)(2,1)} %collective-permute-done.1.mid_ref.refs_3_, ...), custom_call_target="tpu_custom_call" | custom-call | flops 1000 | bytes 1000 | tf_op jit(solution)/shard_map/attend_back/pallas_call | solution.py:136
  135.6 2.0 add_convert_fusion.3
  139.5 2.6 add_convert_fusion.2.refs_15_
  143.8 11.3 %attend_back.5 = (bf16[832,768]{1,0:T(8,128)(2,1)}, bf16[1024,576]{1,0:T(8,128)(2,1)}) custom-call(s32[4]{0:T(128)} %refs_0_.11, s32[1]{0:T(128)} %bitcast.me_ref.refs_1_, bf16[512,768]{1,0:T(8,128)(2,1)} %collective-permute-done.core_ref.refs_2_, bf16[512,768]{1,0:T(8,128)(2,1)} %collective-permute-done.1.mid_ref.refs_3_, ...), custom_call_target="tpu_custom_call" | custom-call | flops 1000 | bytes 1000 | tf_op jit(solution)/shard_map/attend_back/pallas_call | solution.py:136
  155.0 5.0 %collective-permute-done.21 = bf16[768,768]{1,0:T(8,128)(2,1)} collective-permute-done((bf16[768,768]{1,0:T(8,128)(2,1)S(1)}, bf16[768,768]{1,0:T(8,128)(2,1)}, u32[]{:S(2)}, u32[]{:S(2)}) %collective-permute-start.21) | collective-permute-done | bytes 1179680 | tf_op jit(solution)/shard_map/ppermute | solution.py:784
  169.9 11.4 %attend_back.6 = (bf16[832,768]{1,0:T(8,128)(2,1)}, bf16[1024,576]{1,0:T(8,128)(2,1)}) custom-call(s32[4]{0:T(128)} %refs_0_.11, s32[1]{0:T(128)} %bitcast.me_ref.refs_1_, bf16[512,768]{1,0:T(8,128)(2,1)} %collective-permute-done.core_ref.refs_2_, bf16[512,768]{1,0:T(8,128)(2,1)} %collective-permute-done.1.mid_ref.refs_3_, ...), custom_call_target="tpu_custom_call" | custom-call | flops 1000 | bytes 1000 | tf_op jit(solution)/shard_map/attend_back/pallas_call | solution.py:136
  183.9 2.7 collective-permute-start.27
  188.0 11.1 %attend_back.7 = (bf16[832,768]{1,0:T(8,128)(2,1)}, bf16[1024,576]{1,0:T(8,128)(2,1)}) custom-call(s32[4]{0:T(128)} %refs_0_.11, s32[1]{0:T(128)} %bitcast.me_ref.refs_1_, bf16[512,768]{1,0:T(8,128)(2,1)} %collective-permute-done.core_ref.refs_2_, bf16[512,768]{1,0:T(8,128)(2,1)} %collective-permute-done.1.mid_ref.refs_3_, ...), custom_call_target="tpu_custom_call" | custom-call | flops 1000 | bytes 1000 | tf_op jit(solution)/shard_map/attend_back/pallas_call | solution.py:136
  208.0 4.0 %collective-permute-done.31 = bf16[224,768]{1,0:T(8,128)(2,1)S(1)} collective-permute-done((bf16[224,768]{1,0:T(8,128)(2,1)S(1)}, bf16[224,768]{1,0:T(8,128)(2,1)S(1)}, u32[]{:S(2)}, u32[]{:S(2)}) %collective-permute-start.31) | collective-permute-done | bytes 344096 | tf_op jit(solution)/shard_map/ppermute | solution.py:784
  212.8 7.6 %collective-permute-done.30 = bf16[96,768]{1,0:T(8,128)(2,1)S(1)} collective-permute-done((bf16[96,768]{1,0:T(8,128)(2,1)S(1)}, bf16[96,768]{1,0:T(8,128)(2,1)S(1)}, u32[]{:S(2)}, u32[]{:S(2)}) %collective-permute-start.30) | collective-permute-done | bytes 147488 | tf_op jit(solution)/shard_map/ppermute | solution.py:784
  222.9 6.6 %other_grad.1 = bf16[512,768]{1,0:T(8,128)(2,1)} custom-call(bf16[1024,576]{1,0:T(8,128)(2,1)} %get-tuple-element.210.refs_0_.refs_4_, bf16[1024,576]{1,0:T(8,128)(2,1)} %get-tuple-element.211.refs_1_.refs_5_, bf16[1024,576]{1,0:T(8,128)(2,1)} %get-tuple-element.212.refs_2_.refs_6_, bf16[1024,576]{1,0:T(8,128)(2,1)} %get-tuple-element.213.refs_3_.refs_7_, ...), custom_call_target="tpu_custom_call" | custom-call | flops 1000 | bytes 1000 | tf_op jit(solution)/shard_map/other_grad/pallas_call | solution.py:136
  229.6 3.0 %collective-permute-start.36 = (bf16[56,768]{1,0:T(8,128)(2,1)S(1)}, bf16[56,768]{1,0:T(8,128)(2,1)S(1)}, u32[]{:S(2)}, u32[]{:S(2)}) collective-permute-start(bf16[56,768]{1,0:T(8,128)(2,1)S(1)} %constant_dynamic-slice_fusion.1), channel_id=1, source_target_pairs={{0,16},{4,20},{8,24},{12,28},{16,0},{20,4},{24,8},{28,12},{1,17},{... | collective-permute-start | bytes 258056 | tf_op jit(solution)/shard_map/ppermute | solution.py:784
  232.6 2.4 collective-permute-done.33
  236.2 2.5 collective-permute-done.37
  239.5 5.4 %collective-permute-done.40 = bf16[192,768]{1,0:T(8,128)(2,1)S(1)} collective-permute-done((bf16[192,768]{1,0:T(8,128)(2,1)S(1)}, bf16[192,768]{1,0:T(8,128)(2,1)S(1)}, u32[]{:S(2)}, u32[]{:S(2)}) %collective-permute-start.40) | collective-permute-done | bytes 294944 | tf_op jit(solution)/shard_map/ppermute | solution.py:784
  247.7 2.9 %collective-permute-done.38 = bf16[56,768]{1,0:T(8,128)(2,1)S(1)} collective-permute-done((bf16[56,768]{1,0:T(8,128)(2,1)S(1)}, bf16[56,768]{1,0:T(8,128)(2,1)S(1)}, u32[]{:S(2)}, u32[]{:S(2)}) %collective-permute-start.38) | collective-permute-done | bytes 86048 | tf_op jit(solution)/shard_map/ppermute | solution.py:784
  253.1 8.2 %take_back.1 = f32[512,768]{1,0:T(8,128)} custom-call(s32[4]{0:T(128)} %refs_0_.11, s32[1]{0:T(128)} %bitcast.me_ref.refs_1_, bf16[512,768]{1,0:T(8,128)(2,1)} %copy-done.27, bf16[512,768]{1,0:T(8,128)(2,1)} %copy-done.28, bf16[1024,576]{1,0:T(8,128)(2,1)} %get-tuple-element.210.refs_0_.refs_4_, bf16[1024,576]{1,0:T(8,128)(2,1)} %get-tuple-element.211.refs_1_.refs_5_, ...), custom_call_target="tpu_custom_call" | custom-call | flops 1000 | bytes 1000 | tf_op jit(solution)/shard_map/take_back/pallas_call | solution.py:136
  268.2 2.9 %fusion.1 = f32[768,768]{1,0:T(8,128)} fusion(bf16[384,768]{1,0:T(8,128)(2,1)} %collective-permute-done.45, bf16[384,768]{1,0:T(8,128)(2,1)S(1)} %maximum_select_fusion.6, pred[]{:T(512)S(6)} %eq.8), kind=kLoop, calls=%fused_computation.11 | loop fusion | flops 5898240 | bytes 3538945 | tf_op jit(solution)/shard_map/convert_element_type | solution.py:1017
  271.0 4.1 %collective-permute-done.44 = bf16[224,768]{1,0:T(8,128)(2,1)S(1)} collective-permute-done((bf16[224,768]{1,0:T(8,128)(2,1)S(1)}, bf16[224,768]{1,0:T(8,128)(2,1)S(1)}, u32[]{:S(2)}, u32[]{:S(2)}) %collective-permute-start.44) | collective-permute-done | bytes 344096 | tf_op jit(solution)/shard_map/ppermute | solution.py:784
  (199 shorter events, 71.6 us)
Async XLA Ops:
  0.7 18.2 %collective-permute-start.1 = (bf16[512,768]{1,0:T(8,128)(2,1)}, bf16[512,768]{1,0:T(8,128)(2,1)}, u32[]{:S(2)}, u32[]{:S(2)}) collective-permute-start(bf16[512,768]{1,0:T(8,128)(2,1)} %refs_11_.11), channel_id=1, source_target_pairs={{1,2},{2,1},{5,6},{6,5},{9,10},{10,9},{13,14},{14,13},{17,18},{18,... | collective-permute-start | bytes 2359304 | tf_op jit(solution)/shard_map/ppermute | solution.py:796
  4.7 25.7 %collective-permute-start.2 = (bf16[784,768]{1,0:T(8,128)(2,1)}, bf16[784,768]{1,0:T(8,128)(2,1)S(1)}, u32[]{:S(2)}, u32[]{:S(2)}) collective-permute-start(bf16[784,768]{1,0:T(8,128)(2,1)} %pack_joint.1.a0_ref.refs_2_.refs_13_.refs_5_.refs_4_.refs_8_), channel_id=1, source_target_pairs={{0,1},{1,0},{2,3},{3,2},{4,5},{5,4},{6,7},{7,6},{8,9},{9,8},{10,11... | collective-permute-start | bytes 3612680 | tf_op jit(solution)/shard_map/ppermute | solution.py:784
  18.8 28.2 %collective-permute-start.5 = (bf16[784,768]{1,0:T(8,128)(2,1)}, bf16[784,768]{1,0:T(8,128)(2,1)S(1)}, u32[]{:S(2)}, u32[]{:S(2)}) collective-permute-start(bf16[784,768]{1,0:T(8,128)(2,1)} %pack_joint.1.a0_ref.refs_2_.refs_13_.refs_5_.refs_4_.refs_8_), channel_id=1, source_target_pairs={{0,2},{1,3},{2,0},{3,1},{4,6},{5,7},{6,4},{7,5},{8,10},{9,11},{10,... | collective-permute-start | bytes 3612680 | tf_op jit(solution)/shard_map/ppermute | solution.py:784
  18.9 13.8 %collective-permute-start = (bf16[512,768]{1,0:T(8,128)(2,1)S(1)}, bf16[512,768]{1,0:T(8,128)(2,1)}, u32[]{:S(2)}, u32[]{:S(2)}) collective-permute-start(bf16[512,768]{1,0:T(8,128)(2,1)S(1)} %copy-done.3), channel_id=1, source_target_pairs={{0,1},{1,0},{2,3},{3,2},{4,5},{5,4},{6,7},{7,6},{8,9},{9,8},{10,11... | collective-permute-start | bytes 2359304 | tf_op jit(solution)/shard_map/ppermute | solution.py:784
  32.0 13.6 %collective-permute-start.6 = (bf16[192,768]{1,0:T(8,128)(2,1)S(1)}, bf16[192,768]{1,0:T(8,128)(2,1)}, u32[]{:S(2)}, u32[]{:S(2)}) collective-permute-start(bf16[192,768]{1,0:T(8,128)(2,1)S(1)} %maximum_select_fusion.9.refs_0_), channel_id=1, source_target_pairs={{0,8},{4,12},{8,0},{12,4},{16,24},{20,28},{24,16},{28,20},{1,9},{5... | collective-permute-start | bytes 884744 | tf_op jit(solution)/shard_map/ppermute | solution.py:784
  47.2 17.7 %collective-permute-start.8 = (bf16[768,768]{1,0:T(8,128)(2,1)}, bf16[768,768]{1,0:T(8,128)(2,1)}, u32[]{:S(2)}, u32[]{:S(2)}) collective-permute-start(bf16[768,768]{1,0:T(8,128)(2,1)} %refs_9_.5), channel_id=1, source_target_pairs={{0,1},{1,0},{2,3},{3,2},{4,5},{5,4},{6,7},{7,6},{8,9},{9,8},{10,11... | collective-permute-start | bytes 3538952 | tf_op jit(solution)/shard_map/ppermute | solution.py:784
  47.7 17.2 %collective-permute-start.9 = (bf16[768,768]{1,0:T(8,128)(2,1)}, bf16[768,768]{1,0:T(8,128)(2,1)}, u32[]{:S(2)}, u32[]{:S(2)}) collective-permute-start(bf16[768,768]{1,0:T(8,128)(2,1)} %refs_7_.1), channel_id=1, source_target_pairs={{0,1},{1,0},{2,3},{3,2},{4,5},{5,4},{6,7},{7,6},{8,9},{9,8},{10,11... | collective-permute-start | bytes 3538952 | tf_op jit(solution)/shard_map/ppermute | solution.py:784
  47.7 28.9 %collective-permute-start.10 = (bf16[768,768]{1,0:T(8,128)(2,1)}, bf16[768,768]{1,0:T(8,128)(2,1)}, u32[]{:S(2)}, u32[]{:S(2)}) collective-permute-start(bf16[768,768]{1,0:T(8,128)(2,1)} %refs_9_.5), channel_id=1, source_target_pairs={{0,2},{1,3},{2,0},{3,1},{4,6},{5,7},{6,4},{7,5},{8,10},{9,11},{10,... | collective-permute-start | bytes 3538952 | tf_op jit(solution)/shard_map/ppermute | solution.py:784
  49.3 25.7 %collective-permute-start.11 = (bf16[384,768]{1,0:T(8,128)(2,1)S(1)}, bf16[384,768]{1,0:T(8,128)(2,1)}, u32[]{:S(2)}, u32[]{:S(2)}) collective-permute-start(bf16[384,768]{1,0:T(8,128)(2,1)S(1)} %maximum_select_fusion.4.refs_0_), channel_id=1, source_target_pairs={{0,4},{4,0},{8,12},{12,8},{16,20},{20,16},{24,28},{28,24},{1,5},{5... | collective-permute-start | bytes 1769480 | tf_op jit(solution)/shard_map/ppermute | solution.py:784
  106.6 29.0 %collective-permute-start.17 = (bf16[768,768]{1,0:T(8,128)(2,1)S(1)}, bf16[768,768]{1,0:T(8,128)(2,1)}, u32[]{:S(2)}, u32[]{:S(2)}) collective-permute-start(bf16[768,768]{1,0:T(8,128)(2,1)S(1)} %add_convert_fusion.5.refs_15_), channel_id=1, source_target_pairs={{0,2},{1,3},{2,0},{3,1},{4,6},{5,7},{6,4},{7,5},{8,10},{9,11},{10,... | collective-permute-start | bytes 3538952 | tf_op jit(solution)/shard_map/ppermute | solution.py:784
  122.8 12.8 %collective-permute-start.16 = (bf16[768,768]{1,0:T(8,128)(2,1)}, bf16[768,768]{1,0:T(8,128)(2,1)}, u32[]{:S(2)}, u32[]{:S(2)}) collective-permute-start(bf16[768,768]{1,0:T(8,128)(2,1)} %get-tuple-element.179), channel_id=1, source_target_pairs={{0,1},{1,0},{2,3},{3,2},{4,5},{5,4},{6,7},{7,6},{8,9},{9,8},{10,11... | collective-permute-start | bytes 3538952 | tf_op jit(solution)/shard_map/ppermute | solution.py:784
  122.8 14.9 %collective-permute-start.19 = (bf16[768,768]{1,0:T(8,128)(2,1)}, bf16[768,768]{1,0:T(8,128)(2,1)}, u32[]{:S(2)}, u32[]{:S(2)}) collective-permute-start(bf16[768,768]{1,0:T(8,128)(2,1)} %get-tuple-element.195), channel_id=1, source_target_pairs={{0,1},{1,0},{2,3},{3,2},{4,5},{5,4},{6,7},{7,6},{8,9},{9,8},{10,11... | collective-permute-start | bytes 3538952 | tf_op jit(solution)/shard_map/ppermute | solution.py:784
  123.3 36.7 %collective-permute-start.21 = (bf16[768,768]{1,0:T(8,128)(2,1)S(1)}, bf16[768,768]{1,0:T(8,128)(2,1)}, u32[]{:S(2)}, u32[]{:S(2)}) collective-permute-start(bf16[768,768]{1,0:T(8,128)(2,1)S(1)} %copy-done.10), channel_id=1, source_target_pairs={{0,2},{1,3},{2,0},{3,1},{4,6},{5,7},{6,4},{7,5},{8,10},{9,11},{10,... | collective-permute-start | bytes 3538952 | tf_op jit(solution)/shard_map/ppermute | solution.py:784
  142.2 19.5 %collective-permute-start.20 = (bf16[832,768]{1,0:T(8,128)(2,1)}, bf16[832,768]{1,0:T(8,128)(2,1)}, u32[]{:S(2)}, u32[]{:S(2)}) collective-permute-start(bf16[832,768]{1,0:T(8,128)(2,1)} %get-tuple-element.198), channel_id=1, source_target_pairs={{0,1},{1,0},{2,3},{3,2},{4,5},{5,4},{6,7},{7,6},{8,9},{9,8},{10,11... | collective-permute-start | bytes 3833864 | tf_op jit(solution)/shard_map/ppermute | solution.py:784
  142.2 21.3 %collective-permute-start.18 = (bf16[384,768]{1,0:T(8,128)(2,1)S(1)}, bf16[384,768]{1,0:T(8,128)(2,1)}, u32[]{:S(2)}, u32[]{:S(2)}) collective-permute-start(bf16[384,768]{1,0:T(8,128)(2,1)S(1)} %constant_dynamic-slice_fusion.11.refs_14_), channel_id=1, source_target_pairs={{0,4},{4,0},{8,12},{12,8},{16,20},{20,16},{24,28},{28,24},{1,5},{5... | collective-permute-start | bytes 1769480 | tf_op jit(solution)/shard_map/ppermute | solution.py:784
  165.3 16.0 %collective-permute-start.22 = (bf16[192,768]{1,0:T(8,128)(2,1)S(1)}, bf16[192,768]{1,0:T(8,128)(2,1)}, u32[]{:S(2)}, u32[]{:S(2)}) collective-permute-start(bf16[192,768]{1,0:T(8,128)(2,1)S(1)} %constant_dynamic-slice_fusion.10.refs_15_), channel_id=1, source_target_pairs={{0,8},{4,12},{8,0},{12,4},{16,24},{20,28},{24,16},{28,20},{1,9},{5... | collective-permute-start | bytes 884744 | tf_op jit(solution)/shard_map/ppermute | solution.py:784
  167.3 15.1 %collective-permute-start.23 = (bf16[384,768]{1,0:T(8,128)(2,1)S(1)}, bf16[384,768]{1,0:T(8,128)(2,1)}, u32[]{:S(2)}, u32[]{:S(2)}) collective-permute-start(bf16[384,768]{1,0:T(8,128)(2,1)S(1)} %constant_dynamic-slice_fusion.9.refs_16_), channel_id=1, source_target_pairs={{0,4},{4,0},{8,12},{12,8},{16,20},{20,16},{24,28},{28,24},{1,5},{5... | collective-permute-start | bytes 1769480 | tf_op jit(solution)/shard_map/ppermute | solution.py:784
  168.9 30.2 %collective-permute-start.24 = (bf16[832,768]{1,0:T(8,128)(2,1)S(1)}, bf16[832,768]{1,0:T(8,128)(2,1)}, u32[]{:S(2)}, u32[]{:S(2)}) collective-permute-start(bf16[832,768]{1,0:T(8,128)(2,1)S(1)} %add_convert_fusion.refs_14_), channel_id=1, source_target_pairs={{0,2},{1,3},{2,0},{3,1},{4,6},{5,7},{6,4},{7,5},{8,10},{9,11},{10,... | collective-permute-start | bytes 3833864 | tf_op jit(solution)/shard_map/ppermute | solution.py:784
  183.8 15.3 %collective-permute-start.25 = (bf16[832,768]{1,0:T(8,128)(2,1)}, bf16[832,768]{1,0:T(8,128)(2,1)}, u32[]{:S(2)}, u32[]{:S(2)}) collective-permute-start(bf16[832,768]{1,0:T(8,128)(2,1)} %get-tuple-element.216), channel_id=1, source_target_pairs={{0,1},{1,0},{2,3},{3,2},{4,5},{5,4},{6,7},{7,6},{8,9},{9,8},{10,11... | collective-permute-start | bytes 3833864 | tf_op jit(solution)/shard_map/ppermute | solution.py:784
  183.9 20.9 %collective-permute-start.27 = (bf16[96,768]{1,0:T(8,128)(2,1)S(1)}, bf16[96,768]{1,0:T(8,128)(2,1)S(1)}, u32[]{:S(2)}, u32[]{:S(2)}) collective-permute-start(bf16[96,768]{1,0:T(8,128)(2,1)S(1)} %constant_dynamic-slice_fusion.8.refs_14_), channel_id=1, source_target_pairs={{0,16},{4,20},{8,24},{12,28},{16,0},{20,4},{24,8},{28,12},{1,17},{... | collective-permute-start | bytes 442376 | tf_op jit(solution)/shard_map/ppermute | solution.py:784
  186.6 19.3 %collective-permute-start.29 = (bf16[192,768]{1,0:T(8,128)(2,1)S(1)}, bf16[192,768]{1,0:T(8,128)(2,1)S(1)}, u32[]{:S(2)}, u32[]{:S(2)}) collective-permute-start(bf16[192,768]{1,0:T(8,128)(2,1)S(1)} %constant_dynamic-slice_fusion.7.refs_15_), channel_id=1, source_target_pairs={{0,8},{4,12},{8,0},{12,4},{16,24},{20,28},{24,16},{28,20},{1,9},{5... | collective-permute-start | bytes 884744 | tf_op jit(solution)/shard_map/ppermute | solution.py:784
  203.2 18.5 %collective-permute-start.26 = (bf16[192,768]{1,0:T(8,128)(2,1)S(1)}, bf16[192,768]{1,0:T(8,128)(2,1)S(1)}, u32[]{:S(2)}, u32[]{:S(2)}) collective-permute-start(bf16[192,768]{1,0:T(8,128)(2,1)S(1)} %constant_dynamic-slice_fusion.5), channel_id=1, source_target_pairs={{0,4},{4,0},{8,12},{12,8},{16,20},{20,16},{24,28},{28,24},{1,5},{5... | collective-permute-start | bytes 884744 | tf_op jit(solution)/shard_map/ppermute | solution.py:784
  204.8 15.7 %collective-permute-start.28 = (bf16[96,768]{1,0:T(8,128)(2,1)S(1)}, bf16[96,768]{1,0:T(8,128)(2,1)S(1)}, u32[]{:S(2)}, u32[]{:S(2)}) collective-permute-start(bf16[96,768]{1,0:T(8,128)(2,1)S(1)} %add_convert_fusion.17), channel_id=1, source_target_pairs={{0,16},{4,20},{8,24},{12,28},{16,0},{20,4},{24,8},{28,12},{1,17},{... | collective-permute-start | bytes 442376 | tf_op jit(solution)/shard_map/ppermute | solution.py:784
  206.0 14.4 %collective-permute-start.30 = (bf16[96,768]{1,0:T(8,128)(2,1)S(1)}, bf16[96,768]{1,0:T(8,128)(2,1)S(1)}, u32[]{:S(2)}, u32[]{:S(2)}) collective-permute-start(bf16[96,768]{1,0:T(8,128)(2,1)S(1)} %constant_dynamic-slice_fusion.4), channel_id=1, source_target_pairs={{0,16},{4,20},{8,24},{12,28},{16,0},{20,4},{24,8},{28,12},{1,17},{... | collective-permute-start | bytes 442376 | tf_op jit(solution)/shard_map/ppermute | solution.py:784
  212.1 17.5 %collective-permute-start.34 = (bf16[112,768]{1,0:T(8,128)(2,1)S(1)}, bf16[112,768]{1,0:T(8,128)(2,1)S(1)}, u32[]{:S(2)}, u32[]{:S(2)}) collective-permute-start(bf16[112,768]{1,0:T(8,128)(2,1)S(1)} %constant_dynamic-slice_fusion.3), channel_id=1, source_target_pairs={{0,8},{4,12},{8,0},{12,4},{16,24},{20,28},{24,16},{28,20},{1,9},{5... | collective-permute-start | bytes 516104 | tf_op jit(solution)/shard_map/ppermute | solution.py:784
  220.5 14.7 %collective-permute-start.32 = (bf16[96,768]{1,0:T(8,128)(2,1)S(1)}, bf16[96,768]{1,0:T(8,128)(2,1)S(1)}, u32[]{:S(2)}, u32[]{:S(2)}) collective-permute-start(bf16[96,768]{1,0:T(8,128)(2,1)S(1)} %add_convert_fusion.16), channel_id=1, source_target_pairs={{0,16},{4,20},{8,24},{12,28},{16,0},{20,4},{24,8},{28,12},{1,17},{... | collective-permute-start | bytes 442376 | tf_op jit(solution)/shard_map/ppermute | solution.py:784
  220.6 14.4 %collective-permute-start.33 = (bf16[192,768]{1,0:T(8,128)(2,1)S(1)}, bf16[192,768]{1,0:T(8,128)(2,1)S(1)}, u32[]{:S(2)}, u32[]{:S(2)}) collective-permute-start(bf16[192,768]{1,0:T(8,128)(2,1)S(1)} %maximum_select_fusion.10), channel_id=1, source_target_pairs={{0,8},{4,12},{8,0},{12,4},{16,24},{20,28},{24,16},{28,20},{1,9},{5... | collective-permute-start | bytes 884744 | tf_op jit(solution)/shard_map/ppermute | solution.py:784
  221.8 16.9 %collective-permute-start.37 = (bf16[96,768]{1,0:T(8,128)(2,1)S(1)}, bf16[96,768]{1,0:T(8,128)(2,1)S(1)}, u32[]{:S(2)}, u32[]{:S(2)}) collective-permute-start(bf16[96,768]{1,0:T(8,128)(2,1)S(1)} %constant_dynamic-slice_fusion.2.refs_8_), channel_id=1, source_target_pairs={{0,8},{4,12},{8,0},{12,4},{16,24},{20,28},{24,16},{28,20},{1,9},{5... | collective-permute-start | bytes 442376 | tf_op jit(solution)/shard_map/ppermute | solution.py:784
  235.4 15.3 %collective-permute-start.35 = (bf16[512,768]{1,0:T(8,128)(2,1)S(1)}, bf16[512,768]{1,0:T(8,128)(2,1)S(1)}, u32[]{:S(2)}, u32[]{:S(2)}) collective-permute-start(bf16[512,768]{1,0:T(8,128)(2,1)S(1)} %copy-done.29), channel_id=1, source_target_pairs={{0,1},{1,0},{2,3},{3,2},{4,5},{5,4},{6,7},{7,6},{8,9},{9,8},{10,11... | collective-permute-start | bytes 2359304 | tf_op jit(solution)/shard_map/ppermute | solution.py:784
  235.4 16.8 %collective-permute-start.41 = (bf16[512,768]{1,0:T(8,128)(2,1)S(1)}, bf16[512,768]{1,0:T(8,128)(2,1)S(1)}, u32[]{:S(2)}, u32[]{:S(2)}) collective-permute-start(bf16[512,768]{1,0:T(8,128)(2,1)S(1)} %copy-done.29), channel_id=1, source_target_pairs={{1,2},{2,1},{5,6},{6,5},{9,10},{10,9},{13,14},{14,13},{17,18},{18,... | collective-permute-start | bytes 2359304 | tf_op jit(solution)/shard_map/ppermute | solution.py:796
  238.7 26.0 %collective-permute-start.47 = (bf16[384,768]{1,0:T(8,128)(2,1)S(1)}, bf16[384,768]{1,0:T(8,128)(2,1)S(1)}, u32[]{:S(2)}, u32[]{:S(2)}) collective-permute-start(bf16[384,768]{1,0:T(8,128)(2,1)S(1)} %maximum_select_fusion.5), channel_id=1, source_target_pairs={{0,4},{4,0},{8,12},{12,8},{16,20},{20,16},{24,28},{28,24},{1,5},{5... | collective-permute-start | bytes 1769480 | tf_op jit(solution)/shard_map/ppermute | solution.py:784
  246.0 22.2 %collective-permute-start.45 = (bf16[384,768]{1,0:T(8,128)(2,1)S(1)}, bf16[384,768]{1,0:T(8,128)(2,1)}, u32[]{:S(2)}, u32[]{:S(2)}) collective-permute-start(bf16[384,768]{1,0:T(8,128)(2,1)S(1)} %maximum_select_fusion.6), channel_id=1, source_target_pairs={{0,4},{4,0},{8,12},{12,8},{16,20},{20,16},{24,28},{28,24},{1,5},{5... | collective-permute-start | bytes 1769480 | tf_op jit(solution)/shard_map/ppermute | solution.py:784
  (52 other events, 303.4 us)

commit v2 on v1

--- a/solution.py
+++ b/solution.py
@@ -408,7 +408,7 @@
             ups[0], joints[0], downs[0], ups[1], joints[1], downs[1],
         ),
         part={2 * i + 2: (3 * cols, cols) for i in range(4)} | {13: (at, 16), 16: (at, 16)},
-        after=after, first=12,
+        after=after, first=0,
     )
 
 
@@ -527,7 +527,7 @@
     return call(
         attend_back_kernel, "attend_back",
         [shape((4 * cols + 64, width), BF), shape((2 * rows, 3 * cols), BF)],
-        args, smem=2, raw=(2, 3), after=after, first=8, part={5: (3 * cols, cols)},
+        args, smem=2, raw=(2, 3), after=after, first=0, part={5: (3 * cols, cols)},
         scratch=[
             pltpu.VMEM((rows, width), BF), pltpu.SemaphoreType.DMA, pltpu.VMEM((16, width), F32),
             pltpu.VMEM((cols, rows), BF), pltpu.VMEM((cols, rows), BF),
@@ -684,7 +684,7 @@
             low, ups[0], joints[0], downs[0], ups[1], joints[1], downs[1], near, unit,
             gain1, shift1, b_down, gain2, shift2, out_grad,
         ),
-        part={2: (at, 16), 5: (at, 16)}, first=4, after=after,
+        part={2: (at, 16), 5: (at, 16)}, first=0, after=after,
         scratch=[pltpu.VMEM((rows, units), BF)] * 3 + [pltpu.VMEM((rows, width), F32)],
     )
 
@@ -705,7 +705,7 @@
     return call(
         ffn_back_kernel, "ffn_back",
         [*ffn_grad_outs(width, units), shape((rows, width), F32)],
-        (g, act, down, slope, low, up, acc), after=after, first=2,
+        (g, act, down, slope, low, up, acc), after=after, first=0,
         scratch=[pltpu.VMEM((rows, units), BF)],
     )
 
@@ -755,7 +755,7 @@
             g, acts[1], downs[1], slopes[1], low, ups[1], acts[0], downs[0], slopes[0], ups[0], acc,
             unit, inverse, gain, vecs,
         ),
-        after=after, first=2,
+        after=after, first=0,
         scratch=[pltpu.VMEM((rows, width), F32), pltpu.VMEM((rows, units), BF)],
     )
 

time: 282 us -> 281 us (level)
  transfers between devices with their start and end apart: 49 -> 49, of which waited for: 17 -> 17; matrix products, arithmetic and copies ran while one was open for 11% -> 11% of each run, Pallas kernels for 43% -> 42%
where the time goes in v2:
time: 281 us; the launch traced here: 280 us
  Pallas kernels  133 us (47%)
  waiting for transfers between devices  61.1 us (22%)
  starting transfers between devices  44.2 us (16%)
  other arithmetic  32.5 us (12%)
  local copies, waits for them, and re-layouts  8.32 us (3%)
    pallas_call x12, Pallas kernels, call(): pl.pallas_call(body, out_shape=tuple(out_shape), in_specs=in_specs + [ANY...  107 us
    ppermute x47, waiting for transfers between devices, swap(): return lax.ppermute(a, axis, [(i, i ^ distance) for i in range(size)])  61.1 us
    ppermute x47, starting transfers between devices, swap(): return lax.ppermute(a, axis, [(i, i ^ distance) for i in range(size)])  42 us
    pallas_call x2, Pallas kernels, attend_pair(): pl.pallas_call(functools.partial(attend_pair_kernel, after=len(after)), o...  25.7 us
    convert_element_type x20, other arithmetic, add_low(): return total.astype(BF)  19.3 us
    select_n x11, other arithmetic, in_order(): jnp.where(side == 0, jnp.concatenate([mine, got]), jnp.concatenate([got,...  7.3 us
    unnamed x70, local copies, waits for them, and re-layouts  5.62 us
  transfers between devices with their start and end apart: 49, of which 17 were waited for; matrix products, arithmetic and copies ran while one was open for 11% of the time, Pallas kernels for 42%

profile of v2, /device:TPU:0, one launch (start us, length us, event | category | flops | bytes accessed | tf_op | source)
XLA Modules:
  0.0 280.5 jit_solution(5360823271875912497)
XLA Ops:
  2.2 2.4 pack_joint.1.a0_ref.refs_2_.refs_13_.refs_5_.refs_4_.refs_8_
  4.7 3.5 %collective-permute-start.2 = (bf16[784,768]{1,0:T(8,128)(2,1)}, bf16[784,768]{1,0:T(8,128)(2,1)S(1)}, u32[]{:S(2)}, u32[]{:S(2)}) collective-permute-start(bf16[784,768]{1,0:T(8,128)(2,1)} %pack_joint.1.a0_ref.refs_2_.refs_13_.refs_5_.refs_4_.refs_8_), channel_id=1, source_target_pairs={{0,1},{1,0},{2,3},{3,2},{4,5},{5,4},{6,7},{7,6},{8,9},{9,8},{10,11... | collective-permute-start | bytes 3612680 | tf_op jit(solution)/shard_map/ppermute | solution.py:784
  9.2 9.7 %collective-permute-done.3 = bf16[96,768]{1,0:T(8,128)(2,1)S(1)} collective-permute-done((bf16[96,768]{1,0:T(8,128)(2,1)S(1)}, bf16[96,768]{1,0:T(8,128)(2,1)S(1)}, u32[]{:S(2)}, u32[]{:S(2)}) %collective-permute-start.3) | collective-permute-done | bytes 147488 | tf_op jit(solution)/shard_map/ppermute | solution.py:784
  19.8 2.6 collective-permute-start.4
  22.4 7.2 %collective-permute-done.4 = bf16[96,768]{1,0:T(8,128)(2,1)S(1)} collective-permute-done((bf16[96,768]{1,0:T(8,128)(2,1)S(1)}, bf16[96,768]{1,0:T(8,128)(2,1)S(1)}, u32[]{:S(2)}, u32[]{:S(2)}) %collective-permute-start.4) | collective-permute-done | bytes 147488 | tf_op jit(solution)/shard_map/ppermute | solution.py:784
  32.7 12.9 %attend_near.1 = (bf16[512,192]{1,0:T(8,128)(2,1)}, f32[192,512]{1,0:T(8,128)}, f32[3,512]{1,0:T(4,128)}, bf16[512,192]{1,0:T(8,128)(2,1)}, bf16[1024,192]{1,0:T...) custom-call(s32[4]{0:T(128)} %refs_0_.11, ...), custom_call_target="tpu_custom_call" | custom-call | flops 1000 | bytes 1000 | tf_op jit(solution)/shard_map/attend_near/pallas_call | solution.py:347
  52.0 12.8 %attend_far.1 = (bf16[512,192]{1,0:T(8,128)(2,1)}, f32[192,512]{1,0:T(8,128)}, f32[3,512]{1,0:T(4,128)}, bf16[512,192]{1,0:T(8,128)(2,1)}, bf16[1024,192]{1,0:T(...) custom-call(s32[4]{0:T(128)} %refs_0_.11, ...), custom_call_target="tpu_custom_call" | custom-call | flops 1000 | bytes 1000 | tf_op jit(solution)/shard_map/attend_far/pallas_call | solution.py:347
  64.9 10.1 %norm_near.1 = (f32[512,768]{1,0:T(8,128)}, f32[512,1]{1,0:T(8,128)}, bf16[512,768]{1,0:T(8,128)(2,1)}, bf16[512,768]{1,0:T(8,128)(2,1)}, bf16[512,768]{1,0:T(8,...) custom-call(bf16[512,768]{1,0:T(8,128)(2,1)} %refs_11_.11, ...), custom_call_target="tpu_custom_call" | custom-call | flops 1000 | bytes 1000 | tf_op jit(solution)/shard_map/norm_near/pallas_call | solution.py:136
  77.3 2.9 %collective-permute-done.12.refs_4_ = bf16[768,768]{1,0:T(8,128)(2,1)S(1)} collective-permute-done((bf16[768,768]{1,0:T(8,128)(2,1)}, bf16[768,768]{1,0:T(8,128)(2,1)S(1)}, u32[]{:S(2)}, u32[]{:S(2)}) %collective-permute-start.12) | collective-permute-done | bytes 1179680 | tf_op jit(solution)/shard_map/ppermute | solution.py:784
  82.3 13.8 %ffn_far.1 = (bf16[512,768]{1,0:T(8,128)(2,1)}, bf16[512,768]{1,0:T(8,128)(2,1)}, bf16[512,768]{1,0:T(8,128)(2,1)}, bf16[512,768]{1,0:T(8,128)(2,1)}, f32[8,768]...) custom-call(bf16[512,768]{1,0:T(8,128)(2,1)} %get-tuple-element.146., ...), custom_call_target="tpu_custom_call" | custom-call | flops 1000 | bytes 1000 | tf_op jit(solution)/shard_map/ffn_far/pallas_call | solution.py:136
  96.7 7.1 %ffn_back.1 = (bf16[768,768]{1,0:T(8,128)(2,1)}, bf16[768,768]{1,0:T(8,128)(2,1)}, f32[1,768]{1,0:T(1,128)}, f32[512,768]{1,0:T(8,128)}) custom-call(bf16[512,768]{1,0:T(8,128)(2,1)} %get-tuple-element.153.refs_0_, bf16[512,768]{1,0:T(8,128)(2,1)} %get-tuple-element.158.refs_1_, bf16[768,768]{1,0:T(8,128)(2,1)} %copy-done.5, ...), custom_call_target="tpu_custom_call" | custom-call | flops 1000 | bytes 1000 | tf_op jit(solution)/shard_map/ffn_back/pallas_call | solution.py:136
  103.8 2.0 add_convert_fusion.5.refs_15_
  108.8 12.5 %ffn_last.1 = (bf16[768,768]{1,0:T(8,128)(2,1)}, bf16[768,768]{1,0:T(8,128)(2,1)}, f32[1,768]{1,0:T(1,128)}, bf16[768,768]{1,0:T(8,128)(2,1)}, bf16[768,768]{1,0...) custom-call(bf16[512,768]{1,0:T(8,128)(2,1)} %get-tuple-element.153.refs_0_, ...), custom_call_target="tpu_custom_call" | custom-call | flops 1000 | bytes 1000 | tf_op jit(solution)/shard_map/ffn_last/pallas_call | solution.py:136
  122.3 11.2 %attend_back.4 = (bf16[832,768]{1,0:T(8,128)(2,1)}, bf16[1024,576]{1,0:T(8,128)(2,1)}) custom-call(s32[4]{0:T(128)} %refs_0_.11, s32[1]{0:T(128)} %bitcast.me_ref.refs_1_, bf16[512,768]{1,0:T(8,128)(2,1)} %collective-permute-done.core_ref.refs_2_, bf16[512,768]{1,0:T(8,128)(2,1)} %collective-permute-done.1.mid_ref.refs_3_, ...), custom_call_target="tpu_custom_call" | custom-call | flops 1000 | bytes 1000 | tf_op jit(solution)/shard_map/attend_back/pallas_call | solution.py:136
  134.8 2.0 add_convert_fusion.3
  138.8 2.6 add_convert_fusion.2.refs_15_
  143.0 11.2 %attend_back.5 = (bf16[832,768]{1,0:T(8,128)(2,1)}, bf16[1024,576]{1,0:T(8,128)(2,1)}) custom-call(s32[4]{0:T(128)} %refs_0_.11, s32[1]{0:T(128)} %bitcast.me_ref.refs_1_, bf16[512,768]{1,0:T(8,128)(2,1)} %collective-permute-done.core_ref.refs_2_, bf16[512,768]{1,0:T(8,128)(2,1)} %collective-permute-done.1.mid_ref.refs_3_, ...), custom_call_target="tpu_custom_call" | custom-call | flops 1000 | bytes 1000 | tf_op jit(solution)/shard_map/attend_back/pallas_call | solution.py:136
  154.3 5.0 %collective-permute-done.21 = bf16[768,768]{1,0:T(8,128)(2,1)} collective-permute-done((bf16[768,768]{1,0:T(8,128)(2,1)S(1)}, bf16[768,768]{1,0:T(8,128)(2,1)}, u32[]{:S(2)}, u32[]{:S(2)}) %collective-permute-start.21) | collective-permute-done | bytes 1179680 | tf_op jit(solution)/shard_map/ppermute | solution.py:784
  169.2 11.3 %attend_back.6 = (bf16[832,768]{1,0:T(8,128)(2,1)}, bf16[1024,576]{1,0:T(8,128)(2,1)}) custom-call(s32[4]{0:T(128)} %refs_0_.11, s32[1]{0:T(128)} %bitcast.me_ref.refs_1_, bf16[512,768]{1,0:T(8,128)(2,1)} %collective-permute-done.core_ref.refs_2_, bf16[512,768]{1,0:T(8,128)(2,1)} %collective-permute-done.1.mid_ref.refs_3_, ...), custom_call_target="tpu_custom_call" | custom-call | flops 1000 | bytes 1000 | tf_op jit(solution)/shard_map/attend_back/pallas_call | solution.py:136
  183.1 2.8 collective-permute-start.27
  187.2 11.1 %attend_back.7 = (bf16[832,768]{1,0:T(8,128)(2,1)}, bf16[1024,576]{1,0:T(8,128)(2,1)}) custom-call(s32[4]{0:T(128)} %refs_0_.11, s32[1]{0:T(128)} %bitcast.me_ref.refs_1_, bf16[512,768]{1,0:T(8,128)(2,1)} %collective-permute-done.core_ref.refs_2_, bf16[512,768]{1,0:T(8,128)(2,1)} %collective-permute-done.1.mid_ref.refs_3_, ...), custom_call_target="tpu_custom_call" | custom-call | flops 1000 | bytes 1000 | tf_op jit(solution)/shard_map/attend_back/pallas_call | solution.py:136
  207.2 4.0 %collective-permute-done.31 = bf16[224,768]{1,0:T(8,128)(2,1)S(1)} collective-permute-done((bf16[224,768]{1,0:T(8,128)(2,1)S(1)}, bf16[224,768]{1,0:T(8,128)(2,1)S(1)}, u32[]{:S(2)}, u32[]{:S(2)}) %collective-permute-start.31) | collective-permute-done | bytes 344096 | tf_op jit(solution)/shard_map/ppermute | solution.py:784
  212.0 7.6 %collective-permute-done.30 = bf16[96,768]{1,0:T(8,128)(2,1)S(1)} collective-permute-done((bf16[96,768]{1,0:T(8,128)(2,1)S(1)}, bf16[96,768]{1,0:T(8,128)(2,1)S(1)}, u32[]{:S(2)}, u32[]{:S(2)}) %collective-permute-start.30) | collective-permute-done | bytes 147488 | tf_op jit(solution)/shard_map/ppermute | solution.py:784
  222.1 6.6 %other_grad.1 = bf16[512,768]{1,0:T(8,128)(2,1)} custom-call(bf16[1024,576]{1,0:T(8,128)(2,1)} %get-tuple-element.210.refs_0_.refs_4_, bf16[1024,576]{1,0:T(8,128)(2,1)} %get-tuple-element.211.refs_1_.refs_5_, bf16[1024,576]{1,0:T(8,128)(2,1)} %get-tuple-element.212.refs_2_.refs_6_, bf16[1024,576]{1,0:T(8,128)(2,1)} %get-tuple-element.213.refs_3_.refs_7_, ...), custom_call_target="tpu_custom_call" | custom-call | flops 1000 | bytes 1000 | tf_op jit(solution)/shard_map/other_grad/pallas_call | solution.py:136
  228.8 3.0 %collective-permute-start.36 = (bf16[56,768]{1,0:T(8,128)(2,1)S(1)}, bf16[56,768]{1,0:T(8,128)(2,1)S(1)}, u32[]{:S(2)}, u32[]{:S(2)}) collective-permute-start(bf16[56,768]{1,0:T(8,128)(2,1)S(1)} %constant_dynamic-slice_fusion.1), channel_id=1, source_target_pairs={{0,16},{4,20},{8,24},{12,28},{16,0},{20,4},{24,8},{28,12},{1,17},{... | collective-permute-start | bytes 258056 | tf_op jit(solution)/shard_map/ppermute | solution.py:784
  231.8 2.4 collective-permute-done.33
  235.4 2.5 collective-permute-done.37
  238.7 5.4 %collective-permute-done.40 = bf16[192,768]{1,0:T(8,128)(2,1)S(1)} collective-permute-done((bf16[192,768]{1,0:T(8,128)(2,1)S(1)}, bf16[192,768]{1,0:T(8,128)(2,1)S(1)}, u32[]{:S(2)}, u32[]{:S(2)}) %collective-permute-start.40) | collective-permute-done | bytes 294944 | tf_op jit(solution)/shard_map/ppermute | solution.py:784
  246.9 2.9 %collective-permute-done.38 = bf16[56,768]{1,0:T(8,128)(2,1)S(1)} collective-permute-done((bf16[56,768]{1,0:T(8,128)(2,1)S(1)}, bf16[56,768]{1,0:T(8,128)(2,1)S(1)}, u32[]{:S(2)}, u32[]{:S(2)}) %collective-permute-start.38) | collective-permute-done | bytes 86048 | tf_op jit(solution)/shard_map/ppermute | solution.py:784
  252.3 8.2 %take_back.1 = f32[512,768]{1,0:T(8,128)} custom-call(s32[4]{0:T(128)} %refs_0_.11, s32[1]{0:T(128)} %bitcast.me_ref.refs_1_, bf16[512,768]{1,0:T(8,128)(2,1)} %copy-done.27, bf16[512,768]{1,0:T(8,128)(2,1)} %copy-done.28, bf16[1024,576]{1,0:T(8,128)(2,1)} %get-tuple-element.210.refs_0_.refs_4_, bf16[1024,576]{1,0:T(8,128)(2,1)} %get-tuple-element.211.refs_1_.refs_5_, ...), custom_call_target="tpu_custom_call" | custom-call | flops 1000 | bytes 1000 | tf_op jit(solution)/shard_map/take_back/pallas_call | solution.py:136
  267.4 2.9 %fusion.1 = f32[768,768]{1,0:T(8,128)} fusion(bf16[384,768]{1,0:T(8,128)(2,1)} %collective-permute-done.45, bf16[384,768]{1,0:T(8,128)(2,1)S(1)} %maximum_select_fusion.6, pred[]{:T(512)S(6)} %eq.8), kind=kLoop, calls=%fused_computation.11 | loop fusion | flops 5898240 | bytes 3538945 | tf_op jit(solution)/shard_map/convert_element_type | solution.py:1017
  270.3 4.1 %collective-permute-done.44 = bf16[224,768]{1,0:T(8,128)(2,1)S(1)} collective-permute-done((bf16[224,768]{1,0:T(8,128)(2,1)S(1)}, bf16[224,768]{1,0:T(8,128)(2,1)S(1)}, u32[]{:S(2)}, u32[]{:S(2)}) %collective-permute-start.44) | collective-permute-done | bytes 344096 | tf_op jit(solution)/shard_map/ppermute | solution.py:784
  (199 shorter events, 72.4 us)
Async XLA Ops:
  0.7 18.2 %collective-permute-start.1 = (bf16[512,768]{1,0:T(8,128)(2,1)}, bf16[512,768]{1,0:T(8,128)(2,1)}, u32[]{:S(2)}, u32[]{:S(2)}) collective-permute-start(bf16[512,768]{1,0:T(8,128)(2,1)} %refs_11_.11), channel_id=1, source_target_pairs={{1,2},{2,1},{5,6},{6,5},{9,10},{10,9},{13,14},{14,13},{17,18},{18,... | collective-permute-start | bytes 2359304 | tf_op jit(solution)/shard_map/ppermute | solution.py:796
  4.7 25.7 %collective-permute-start.2 = (bf16[784,768]{1,0:T(8,128)(2,1)}, bf16[784,768]{1,0:T(8,128)(2,1)S(1)}, u32[]{:S(2)}, u32[]{:S(2)}) collective-permute-start(bf16[784,768]{1,0:T(8,128)(2,1)} %pack_joint.1.a0_ref.refs_2_.refs_13_.refs_5_.refs_4_.refs_8_), channel_id=1, source_target_pairs={{0,1},{1,0},{2,3},{3,2},{4,5},{5,4},{6,7},{7,6},{8,9},{9,8},{10,11... | collective-permute-start | bytes 3612680 | tf_op jit(solution)/shard_map/ppermute | solution.py:784
  18.8 28.2 %collective-permute-start.5 = (bf16[784,768]{1,0:T(8,128)(2,1)}, bf16[784,768]{1,0:T(8,128)(2,1)S(1)}, u32[]{:S(2)}, u32[]{:S(2)}) collective-permute-start(bf16[784,768]{1,0:T(8,128)(2,1)} %pack_joint.1.a0_ref.refs_2_.refs_13_.refs_5_.refs_4_.refs_8_), channel_id=1, source_target_pairs={{0,2},{1,3},{2,0},{3,1},{4,6},{5,7},{6,4},{7,5},{8,10},{9,11},{10,... | collective-permute-start | bytes 3612680 | tf_op jit(solution)/shard_map/ppermute | solution.py:784
  18.9 13.8 %collective-permute-start = (bf16[512,768]{1,0:T(8,128)(2,1)S(1)}, bf16[512,768]{1,0:T(8,128)(2,1)}, u32[]{:S(2)}, u32[]{:S(2)}) collective-permute-start(bf16[512,768]{1,0:T(8,128)(2,1)S(1)} %copy-done.3), channel_id=1, source_target_pairs={{0,1},{1,0},{2,3},{3,2},{4,5},{5,4},{6,7},{7,6},{8,9},{9,8},{10,11... | collective-permute-start | bytes 2359304 | tf_op jit(solution)/shard_map/ppermute | solution.py:784
  32.0 13.6 %collective-permute-start.6 = (bf16[192,768]{1,0:T(8,128)(2,1)S(1)}, bf16[192,768]{1,0:T(8,128)(2,1)}, u32[]{:S(2)}, u32[]{:S(2)}) collective-permute-start(bf16[192,768]{1,0:T(8,128)(2,1)S(1)} %maximum_select_fusion.9.refs_0_), channel_id=1, source_target_pairs={{0,8},{4,12},{8,0},{12,4},{16,24},{20,28},{24,16},{28,20},{1,9},{5... | collective-permute-start | bytes 884744 | tf_op jit(solution)/shard_map/ppermute | solution.py:784
  47.2 17.7 %collective-permute-start.8 = (bf16[768,768]{1,0:T(8,128)(2,1)}, bf16[768,768]{1,0:T(8,128)(2,1)}, u32[]{:S(2)}, u32[]{:S(2)}) collective-permute-start(bf16[768,768]{1,0:T(8,128)(2,1)} %refs_9_.5), channel_id=1, source_target_pairs={{0,1},{1,0},{2,3},{3,2},{4,5},{5,4},{6,7},{7,6},{8,9},{9,8},{10,11... | collective-permute-start | bytes 3538952 | tf_op jit(solution)/shard_map/ppermute | solution.py:784
  47.7 17.2 %collective-permute-start.9 = (bf16[768,768]{1,0:T(8,128)(2,1)}, bf16[768,768]{1,0:T(8,128)(2,1)}, u32[]{:S(2)}, u32[]{:S(2)}) collective-permute-start(bf16[768,768]{1,0:T(8,128)(2,1)} %refs_7_.1), channel_id=1, source_target_pairs={{0,1},{1,0},{2,3},{3,2},{4,5},{5,4},{6,7},{7,6},{8,9},{9,8},{10,11... | collective-permute-start | bytes 3538952 | tf_op jit(solution)/shard_map/ppermute | solution.py:784
  47.7 28.9 %collective-permute-start.10 = (bf16[768,768]{1,0:T(8,128)(2,1)}, bf16[768,768]{1,0:T(8,128)(2,1)}, u32[]{:S(2)}, u32[]{:S(2)}) collective-permute-start(bf16[768,768]{1,0:T(8,128)(2,1)} %refs_9_.5), channel_id=1, source_target_pairs={{0,2},{1,3},{2,0},{3,1},{4,6},{5,7},{6,4},{7,5},{8,10},{9,11},{10,... | collective-permute-start | bytes 3538952 | tf_op jit(solution)/shard_map/ppermute | solution.py:784
  49.3 25.7 %collective-permute-start.11 = (bf16[384,768]{1,0:T(8,128)(2,1)S(1)}, bf16[384,768]{1,0:T(8,128)(2,1)}, u32[]{:S(2)}, u32[]{:S(2)}) collective-permute-start(bf16[384,768]{1,0:T(8,128)(2,1)S(1)} %maximum_select_fusion.4.refs_0_), channel_id=1, source_target_pairs={{0,4},{4,0},{8,12},{12,8},{16,20},{20,16},{24,28},{28,24},{1,5},{5... | collective-permute-start | bytes 1769480 | tf_op jit(solution)/shard_map/ppermute | solution.py:784
  105.9 29.0 %collective-permute-start.17 = (bf16[768,768]{1,0:T(8,128)(2,1)S(1)}, bf16[768,768]{1,0:T(8,128)(2,1)}, u32[]{:S(2)}, u32[]{:S(2)}) collective-permute-start(bf16[768,768]{1,0:T(8,128)(2,1)S(1)} %add_convert_fusion.5.refs_15_), channel_id=1, source_target_pairs={{0,2},{1,3},{2,0},{3,1},{4,6},{5,7},{6,4},{7,5},{8,10},{9,11},{10,... | collective-permute-start | bytes 3538952 | tf_op jit(solution)/shard_map/ppermute | solution.py:784
  121.3 13.5 %collective-permute-start.16 = (bf16[768,768]{1,0:T(8,128)(2,1)}, bf16[768,768]{1,0:T(8,128)(2,1)}, u32[]{:S(2)}, u32[]{:S(2)}) collective-permute-start(bf16[768,768]{1,0:T(8,128)(2,1)} %get-tuple-element.179), channel_id=1, source_target_pairs={{0,1},{1,0},{2,3},{3,2},{4,5},{5,4},{6,7},{7,6},{8,9},{9,8},{10,11... | collective-permute-start | bytes 3538952 | tf_op jit(solution)/shard_map/ppermute | solution.py:784
  121.4 15.6 %collective-permute-start.19 = (bf16[768,768]{1,0:T(8,128)(2,1)}, bf16[768,768]{1,0:T(8,128)(2,1)}, u32[]{:S(2)}, u32[]{:S(2)}) collective-permute-start(bf16[768,768]{1,0:T(8,128)(2,1)} %get-tuple-element.195), channel_id=1, source_target_pairs={{0,1},{1,0},{2,3},{3,2},{4,5},{5,4},{6,7},{7,6},{8,9},{9,8},{10,11... | collective-permute-start | bytes 3538952 | tf_op jit(solution)/shard_map/ppermute | solution.py:784
  121.9 37.4 %collective-permute-start.21 = (bf16[768,768]{1,0:T(8,128)(2,1)S(1)}, bf16[768,768]{1,0:T(8,128)(2,1)}, u32[]{:S(2)}, u32[]{:S(2)}) collective-permute-start(bf16[768,768]{1,0:T(8,128)(2,1)S(1)} %copy-done.10), channel_id=1, source_target_pairs={{0,2},{1,3},{2,0},{3,1},{4,6},{5,7},{6,4},{7,5},{8,10},{9,11},{10,... | collective-permute-start | bytes 3538952 | tf_op jit(solution)/shard_map/ppermute | solution.py:784
  141.4 19.5 %collective-permute-start.20 = (bf16[832,768]{1,0:T(8,128)(2,1)}, bf16[832,768]{1,0:T(8,128)(2,1)}, u32[]{:S(2)}, u32[]{:S(2)}) collective-permute-start(bf16[832,768]{1,0:T(8,128)(2,1)} %get-tuple-element.198), channel_id=1, source_target_pairs={{0,1},{1,0},{2,3},{3,2},{4,5},{5,4},{6,7},{7,6},{8,9},{9,8},{10,11... | collective-permute-start | bytes 3833864 | tf_op jit(solution)/shard_map/ppermute | solution.py:784
  141.5 21.3 %collective-permute-start.18 = (bf16[384,768]{1,0:T(8,128)(2,1)S(1)}, bf16[384,768]{1,0:T(8,128)(2,1)}, u32[]{:S(2)}, u32[]{:S(2)}) collective-permute-start(bf16[384,768]{1,0:T(8,128)(2,1)S(1)} %constant_dynamic-slice_fusion.11.refs_14_), channel_id=1, source_target_pairs={{0,4},{4,0},{8,12},{12,8},{16,20},{20,16},{24,28},{28,24},{1,5},{5... | collective-permute-start | bytes 1769480 | tf_op jit(solution)/shard_map/ppermute | solution.py:784
  164.5 16.0 %collective-permute-start.22 = (bf16[192,768]{1,0:T(8,128)(2,1)S(1)}, bf16[192,768]{1,0:T(8,128)(2,1)}, u32[]{:S(2)}, u32[]{:S(2)}) collective-permute-start(bf16[192,768]{1,0:T(8,128)(2,1)S(1)} %constant_dynamic-slice_fusion.10.refs_15_), channel_id=1, source_target_pairs={{0,8},{4,12},{8,0},{12,4},{16,24},{20,28},{24,16},{28,20},{1,9},{5... | collective-permute-start | bytes 884744 | tf_op jit(solution)/shard_map/ppermute | solution.py:784
  166.6 15.1 %collective-permute-start.23 = (bf16[384,768]{1,0:T(8,128)(2,1)S(1)}, bf16[384,768]{1,0:T(8,128)(2,1)}, u32[]{:S(2)}, u32[]{:S(2)}) collective-permute-start(bf16[384,768]{1,0:T(8,128)(2,1)S(1)} %constant_dynamic-slice_fusion.9.refs_16_), channel_id=1, source_target_pairs={{0,4},{4,0},{8,12},{12,8},{16,20},{20,16},{24,28},{28,24},{1,5},{5... | collective-permute-start | bytes 1769480 | tf_op jit(solution)/shard_map/ppermute | solution.py:784
  168.2 30.1 %collective-permute-start.24 = (bf16[832,768]{1,0:T(8,128)(2,1)S(1)}, bf16[832,768]{1,0:T(8,128)(2,1)}, u32[]{:S(2)}, u32[]{:S(2)}) collective-permute-start(bf16[832,768]{1,0:T(8,128)(2,1)S(1)} %add_convert_fusion.refs_14_), channel_id=1, source_target_pairs={{0,2},{1,3},{2,0},{3,1},{4,6},{5,7},{6,4},{7,5},{8,10},{9,11},{10,... | collective-permute-start | bytes 3833864 | tf_op jit(solution)/shard_map/ppermute | solution.py:784
  183.0 15.3 %collective-permute-start.25 = (bf16[832,768]{1,0:T(8,128)(2,1)}, bf16[832,768]{1,0:T(8,128)(2,1)}, u32[]{:S(2)}, u32[]{:S(2)}) collective-permute-start(bf16[832,768]{1,0:T(8,128)(2,1)} %get-tuple-element.216), channel_id=1, source_target_pairs={{0,1},{1,0},{2,3},{3,2},{4,5},{5,4},{6,7},{7,6},{8,9},{9,8},{10,11... | collective-permute-start | bytes 3833864 | tf_op jit(solution)/shard_map/ppermute | solution.py:784
  183.1 20.9 %collective-permute-start.27 = (bf16[96,768]{1,0:T(8,128)(2,1)S(1)}, bf16[96,768]{1,0:T(8,128)(2,1)S(1)}, u32[]{:S(2)}, u32[]{:S(2)}) collective-permute-start(bf16[96,768]{1,0:T(8,128)(2,1)S(1)} %constant_dynamic-slice_fusion.8.refs_14_), channel_id=1, source_target_pairs={{0,16},{4,20},{8,24},{12,28},{16,0},{20,4},{24,8},{28,12},{1,17},{... | collective-permute-start | bytes 442376 | tf_op jit(solution)/shard_map/ppermute | solution.py:784
  185.9 19.3 %collective-permute-start.29 = (bf16[192,768]{1,0:T(8,128)(2,1)S(1)}, bf16[192,768]{1,0:T(8,128)(2,1)S(1)}, u32[]{:S(2)}, u32[]{:S(2)}) collective-permute-start(bf16[192,768]{1,0:T(8,128)(2,1)S(1)} %constant_dynamic-slice_fusion.7.refs_15_), channel_id=1, source_target_pairs={{0,8},{4,12},{8,0},{12,4},{16,24},{20,28},{24,16},{28,20},{1,9},{5... | collective-permute-start | bytes 884744 | tf_op jit(solution)/shard_map/ppermute | solution.py:784
  202.4 18.4 %collective-permute-start.26 = (bf16[192,768]{1,0:T(8,128)(2,1)S(1)}, bf16[192,768]{1,0:T(8,128)(2,1)S(1)}, u32[]{:S(2)}, u32[]{:S(2)}) collective-permute-start(bf16[192,768]{1,0:T(8,128)(2,1)S(1)} %constant_dynamic-slice_fusion.5), channel_id=1, source_target_pairs={{0,4},{4,0},{8,12},{12,8},{16,20},{20,16},{24,28},{28,24},{1,5},{5... | collective-permute-start | bytes 884744 | tf_op jit(solution)/shard_map/ppermute | solution.py:784
  204.0 15.7 %collective-permute-start.28 = (bf16[96,768]{1,0:T(8,128)(2,1)S(1)}, bf16[96,768]{1,0:T(8,128)(2,1)S(1)}, u32[]{:S(2)}, u32[]{:S(2)}) collective-permute-start(bf16[96,768]{1,0:T(8,128)(2,1)S(1)} %add_convert_fusion.17), channel_id=1, source_target_pairs={{0,16},{4,20},{8,24},{12,28},{16,0},{20,4},{24,8},{28,12},{1,17},{... | collective-permute-start | bytes 442376 | tf_op jit(solution)/shard_map/ppermute | solution.py:784
  205.3 14.3 %collective-permute-start.30 = (bf16[96,768]{1,0:T(8,128)(2,1)S(1)}, bf16[96,768]{1,0:T(8,128)(2,1)S(1)}, u32[]{:S(2)}, u32[]{:S(2)}) collective-permute-start(bf16[96,768]{1,0:T(8,128)(2,1)S(1)} %constant_dynamic-slice_fusion.4), channel_id=1, source_target_pairs={{0,16},{4,20},{8,24},{12,28},{16,0},{20,4},{24,8},{28,12},{1,17},{... | collective-permute-start | bytes 442376 | tf_op jit(solution)/shard_map/ppermute | solution.py:784
  211.3 17.5 %collective-permute-start.34 = (bf16[112,768]{1,0:T(8,128)(2,1)S(1)}, bf16[112,768]{1,0:T(8,128)(2,1)S(1)}, u32[]{:S(2)}, u32[]{:S(2)}) collective-permute-start(bf16[112,768]{1,0:T(8,128)(2,1)S(1)} %constant_dynamic-slice_fusion.3), channel_id=1, source_target_pairs={{0,8},{4,12},{8,0},{12,4},{16,24},{20,28},{24,16},{28,20},{1,9},{5... | collective-permute-start | bytes 516104 | tf_op jit(solution)/shard_map/ppermute | solution.py:784
  219.7 14.7 %collective-permute-start.32 = (bf16[96,768]{1,0:T(8,128)(2,1)S(1)}, bf16[96,768]{1,0:T(8,128)(2,1)S(1)}, u32[]{:S(2)}, u32[]{:S(2)}) collective-permute-start(bf16[96,768]{1,0:T(8,128)(2,1)S(1)} %add_convert_fusion.16), channel_id=1, source_target_pairs={{0,16},{4,20},{8,24},{12,28},{16,0},{20,4},{24,8},{28,12},{1,17},{... | collective-permute-start | bytes 442376 | tf_op jit(solution)/shard_map/ppermute | solution.py:784
  219.8 14.4 %collective-permute-start.33 = (bf16[192,768]{1,0:T(8,128)(2,1)S(1)}, bf16[192,768]{1,0:T(8,128)(2,1)S(1)}, u32[]{:S(2)}, u32[]{:S(2)}) collective-permute-start(bf16[192,768]{1,0:T(8,128)(2,1)S(1)} %maximum_select_fusion.10), channel_id=1, source_target_pairs={{0,8},{4,12},{8,0},{12,4},{16,24},{20,28},{24,16},{28,20},{1,9},{5... | collective-permute-start | bytes 884744 | tf_op jit(solution)/shard_map/ppermute | solution.py:784
  221.0 16.9 %collective-permute-start.37 = (bf16[96,768]{1,0:T(8,128)(2,1)S(1)}, bf16[96,768]{1,0:T(8,128)(2,1)S(1)}, u32[]{:S(2)}, u32[]{:S(2)}) collective-permute-start(bf16[96,768]{1,0:T(8,128)(2,1)S(1)} %constant_dynamic-slice_fusion.2.refs_8_), channel_id=1, source_target_pairs={{0,8},{4,12},{8,0},{12,4},{16,24},{20,28},{24,16},{28,20},{1,9},{5... | collective-permute-start | bytes 442376 | tf_op jit(solution)/shard_map/ppermute | solution.py:784
  234.6 15.3 %collective-permute-start.35 = (bf16[512,768]{1,0:T(8,128)(2,1)S(1)}, bf16[512,768]{1,0:T(8,128)(2,1)S(1)}, u32[]{:S(2)}, u32[]{:S(2)}) collective-permute-start(bf16[512,768]{1,0:T(8,128)(2,1)S(1)} %copy-done.29), channel_id=1, source_target_pairs={{0,1},{1,0},{2,3},{3,2},{4,5},{5,4},{6,7},{7,6},{8,9},{9,8},{10,11... | collective-permute-start | bytes 2359304 | tf_op jit(solution)/shard_map/ppermute | solution.py:784
  234.7 16.8 %collective-permute-start.41 = (bf16[512,768]{1,0:T(8,128)(2,1)S(1)}, bf16[512,768]{1,0:T(8,128)(2,1)S(1)}, u32[]{:S(2)}, u32[]{:S(2)}) collective-permute-start(bf16[512,768]{1,0:T(8,128)(2,1)S(1)} %copy-done.29), channel_id=1, source_target_pairs={{1,2},{2,1},{5,6},{6,5},{9,10},{10,9},{13,14},{14,13},{17,18},{18,... | collective-permute-start | bytes 2359304 | tf_op jit(solution)/shard_map/ppermute | solution.py:796
  237.9 26.1 %collective-permute-start.47 = (bf16[384,768]{1,0:T(8,128)(2,1)S(1)}, bf16[384,768]{1,0:T(8,128)(2,1)S(1)}, u32[]{:S(2)}, u32[]{:S(2)}) collective-permute-start(bf16[384,768]{1,0:T(8,128)(2,1)S(1)} %maximum_select_fusion.5), channel_id=1, source_target_pairs={{0,4},{4,0},{8,12},{12,8},{16,20},{20,16},{24,28},{28,24},{1,5},{5... | collective-permute-start | bytes 1769480 | tf_op jit(solution)/shard_map/ppermute | solution.py:784
  246.1 21.3 %collective-permute-start.45 = (bf16[384,768]{1,0:T(8,128)(2,1)S(1)}, bf16[384,768]{1,0:T(8,128)(2,1)}, u32[]{:S(2)}, u32[]{:S(2)}) collective-permute-start(bf16[384,768]{1,0:T(8,128)(2,1)S(1)} %maximum_select_fusion.6), channel_id=1, source_target_pairs={{0,4},{4,0},{8,12},{12,8},{16,20},{20,16},{24,28},{28,24},{1,5},{5... | collective-permute-start | bytes 1769480 | tf_op jit(solution)/shard_map/ppermute | solution.py:784
  (52 other events, 303.0 us)

commit v3 on v2

--- a/solution.py
+++ b/solution.py
@@ -484,7 +484,7 @@
     b_s[8:16] = vec_ref[...]
     at = 2 * cols
     grad_ref[at : at + 16] = b_s[...].astype(BF)
-    grad_ref[at + 16 : at + 64] = jnp.zeros((48, b_s.shape[1]), BF)
+    grad_ref[at + 16 : at + 32] = jnp.zeros((16, b_s.shape[1]), BF)
     other()
     send(d_s)
     arrive(own_ref)
@@ -497,8 +497,8 @@
             dot(t_s[cols : 3 * cols, near], tok) + dot(t_s[cols : 3 * cols, far], other.buffer[:, cs])
         ).astype(BF)
         grad_ref[cols : 2 * cols, cs] = terms[0:cols]
-        grad_ref[at + 64 : at + 64 + cols, cs] = terms[cols : 2 * cols]
-        grad_ref[at + 64 + cols : at + 64 + 2 * cols, cs] = dot(
+        grad_ref[at + 32 : at + 32 + cols, cs] = terms[cols : 2 * cols]
+        grad_ref[at + 32 + cols : at + 32 + 2 * cols, cs] = dot(
             t_s[3 * cols : 4 * cols, near], g_ref[:, cs]
         ).astype(BF)
 
@@ -526,7 +526,7 @@
     args = (lens, me, tok_core, tok_mid, g, a, q, k, lse, v, ct, own, bu, vecs)
     return call(
         attend_back_kernel, "attend_back",
-        [shape((4 * cols + 64, width), BF), shape((2 * rows, 3 * cols), BF)],
+        [shape((4 * cols + 32, width), BF), shape((2 * rows, 3 * cols), BF)],
         args, smem=2, raw=(2, 3), after=after, first=0, part={5: (3 * cols, cols)},
         scratch=[
             pltpu.VMEM((rows, width), BF), pltpu.SemaphoreType.DMA, pltpu.VMEM((16, width), F32),
@@ -983,7 +983,7 @@
     joint_back = hold(joint_back, joint_sum)
 
     def rows_of(a, part):
-        return a[: 2 * cols + 64] if part == 0 else a[2 * cols + 64 :]
+        return a[: 2 * cols + 32] if part == 0 else a[2 * cols + 32 :]
 
     def joint_part(i, own, got):
         return WideSum(add_low(rows_of(own, i), rows_of(got, i), rows_of(joint_back, i)))

time: 281 us -> 281 us (level)
  transfers between devices with their start and end apart: 49 -> 49, of which waited for: 17 -> 17; matrix products, arithmetic and copies ran while one was open for 11% -> 11% of each run, Pallas kernels for 42% -> 43%
where the time goes in v3:
time: 281 us; the launch traced here: 280 us
  Pallas kernels  133 us (47%)
  waiting for transfers between devices  59.3 us (21%)
  starting transfers between devices  45.5 us (16%)
  other arithmetic  32.3 us (11%)
  local copies, waits for them, and re-layouts  8.34 us (3%)
    pallas_call x12, Pallas kernels, call(): pl.pallas_call(body, out_shape=tuple(out_shape), in_specs=in_specs + [ANY...  107 us
    ppermute x47, waiting for transfers between devices, swap(): return lax.ppermute(a, axis, [(i, i ^ distance) for i in range(size)])  59.3 us
    ppermute x47, starting transfers between devices, swap(): return lax.ppermute(a, axis, [(i, i ^ distance) for i in range(size)])  43.2 us
    pallas_call x2, Pallas kernels, attend_pair(): pl.pallas_call(functools.partial(attend_pair_kernel, after=len(after)), o...  25.7 us
    convert_element_type x20, other arithmetic, add_low(): return total.astype(BF)  19.2 us
    select_n x11, other arithmetic, in_order(): jnp.where(side == 0, jnp.concatenate([mine, got]), jnp.concatenate([got,...  7.31 us
    unnamed x70, local copies, waits for them, and re-layouts  5.64 us
  transfers between devices with their start and end apart: 49, of which 17 were waited for; matrix products, arithmetic and copies ran while one was open for 11% of the time, Pallas kernels for 43%

profile of v3, /device:TPU:0, one launch (start us, length us, event | category | flops | bytes accessed | tf_op | source)
XLA Modules:
  0.0 279.8 jit_solution(18252704184040342191)
XLA Ops:
  2.2 2.5 pack_joint.1.a0_ref.refs_2_.refs_13_.refs_5_.refs_4_.refs_8_
  4.7 3.5 %collective-permute-start.2 = (bf16[784,768]{1,0:T(8,128)(2,1)}, bf16[784,768]{1,0:T(8,128)(2,1)S(1)}, u32[]{:S(2)}, u32[]{:S(2)}) collective-permute-start(bf16[784,768]{1,0:T(8,128)(2,1)} %pack_joint.1.a0_ref.refs_2_.refs_13_.refs_5_.refs_4_.refs_8_), channel_id=1, source_target_pairs={{0,1},{1,0},{2,3},{3,2},{4,5},{5,4},{6,7},{7,6},{8,9},{9,8},{10,11... | collective-permute-start | bytes 3612680 | tf_op jit(solution)/shard_map/ppermute | solution.py:784
  9.2 9.7 %collective-permute-done.3 = bf16[96,768]{1,0:T(8,128)(2,1)S(1)} collective-permute-done((bf16[96,768]{1,0:T(8,128)(2,1)S(1)}, bf16[96,768]{1,0:T(8,128)(2,1)S(1)}, u32[]{:S(2)}, u32[]{:S(2)}) %collective-permute-start.3) | collective-permute-done | bytes 147488 | tf_op jit(solution)/shard_map/ppermute | solution.py:784
  19.8 2.6 collective-permute-start.4
  22.4 7.2 %collective-permute-done.4 = bf16[96,768]{1,0:T(8,128)(2,1)S(1)} collective-permute-done((bf16[96,768]{1,0:T(8,128)(2,1)S(1)}, bf16[96,768]{1,0:T(8,128)(2,1)S(1)}, u32[]{:S(2)}, u32[]{:S(2)}) %collective-permute-start.4) | collective-permute-done | bytes 147488 | tf_op jit(solution)/shard_map/ppermute | solution.py:784
  32.7 12.8 %attend_near.1 = (bf16[512,192]{1,0:T(8,128)(2,1)}, f32[192,512]{1,0:T(8,128)}, f32[3,512]{1,0:T(4,128)}, bf16[512,192]{1,0:T(8,128)(2,1)}, bf16[1024,192]{1,0:T...) custom-call(s32[4]{0:T(128)} %refs_0_.11, ...), custom_call_target="tpu_custom_call" | custom-call | flops 1000 | bytes 1000 | tf_op jit(solution)/shard_map/attend_near/pallas_call | solution.py:347
  52.0 12.8 %attend_far.1 = (bf16[512,192]{1,0:T(8,128)(2,1)}, f32[192,512]{1,0:T(8,128)}, f32[3,512]{1,0:T(4,128)}, bf16[512,192]{1,0:T(8,128)(2,1)}, bf16[1024,192]{1,0:T(...) custom-call(s32[4]{0:T(128)} %refs_0_.11, ...), custom_call_target="tpu_custom_call" | custom-call | flops 1000 | bytes 1000 | tf_op jit(solution)/shard_map/attend_far/pallas_call | solution.py:347
  64.8 10.1 %norm_near.1 = (f32[512,768]{1,0:T(8,128)}, f32[512,1]{1,0:T(8,128)}, bf16[512,768]{1,0:T(8,128)(2,1)}, bf16[512,768]{1,0:T(8,128)(2,1)}, bf16[512,768]{1,0:T(8,...) custom-call(bf16[512,768]{1,0:T(8,128)(2,1)} %refs_11_.11, ...), custom_call_target="tpu_custom_call" | custom-call | flops 1000 | bytes 1000 | tf_op jit(solution)/shard_map/norm_near/pallas_call | solution.py:136
  77.2 2.9 %collective-permute-done.12.refs_4_ = bf16[768,768]{1,0:T(8,128)(2,1)S(1)} collective-permute-done((bf16[768,768]{1,0:T(8,128)(2,1)}, bf16[768,768]{1,0:T(8,128)(2,1)S(1)}, u32[]{:S(2)}, u32[]{:S(2)}) %collective-permute-start.12) | collective-permute-done | bytes 1179680 | tf_op jit(solution)/shard_map/ppermute | solution.py:784
  82.3 13.8 %ffn_far.1 = (bf16[512,768]{1,0:T(8,128)(2,1)}, bf16[512,768]{1,0:T(8,128)(2,1)}, bf16[512,768]{1,0:T(8,128)(2,1)}, bf16[512,768]{1,0:T(8,128)(2,1)}, f32[8,768]...) custom-call(bf16[512,768]{1,0:T(8,128)(2,1)} %get-tuple-element.146., ...), custom_call_target="tpu_custom_call" | custom-call | flops 1000 | bytes 1000 | tf_op jit(solution)/shard_map/ffn_far/pallas_call | solution.py:136
  96.6 7.1 %ffn_back.1 = (bf16[768,768]{1,0:T(8,128)(2,1)}, bf16[768,768]{1,0:T(8,128)(2,1)}, f32[1,768]{1,0:T(1,128)}, f32[512,768]{1,0:T(8,128)}) custom-call(bf16[512,768]{1,0:T(8,128)(2,1)} %get-tuple-element.153.refs_0_, bf16[512,768]{1,0:T(8,128)(2,1)} %get-tuple-element.158.refs_1_, bf16[768,768]{1,0:T(8,128)(2,1)} %copy-done.5, ...), custom_call_target="tpu_custom_call" | custom-call | flops 1000 | bytes 1000 | tf_op jit(solution)/shard_map/ffn_back/pallas_call | solution.py:136
  108.7 12.5 %ffn_last.1 = (bf16[768,768]{1,0:T(8,128)(2,1)}, bf16[768,768]{1,0:T(8,128)(2,1)}, f32[1,768]{1,0:T(1,128)}, bf16[768,768]{1,0:T(8,128)(2,1)}, bf16[768,768]{1,0...) custom-call(bf16[512,768]{1,0:T(8,128)(2,1)} %get-tuple-element.153.refs_0_, ...), custom_call_target="tpu_custom_call" | custom-call | flops 1000 | bytes 1000 | tf_op jit(solution)/shard_map/ffn_last/pallas_call | solution.py:136
  122.2 11.2 %attend_back.4 = (bf16[800,768]{1,0:T(8,128)(2,1)}, bf16[1024,576]{1,0:T(8,128)(2,1)}) custom-call(s32[4]{0:T(128)} %refs_0_.11, s32[1]{0:T(128)} %bitcast.me_ref.refs_1_, bf16[512,768]{1,0:T(8,128)(2,1)} %collective-permute-done.core_ref.refs_2_, bf16[512,768]{1,0:T(8,128)(2,1)} %collective-permute-done.1.mid_ref.refs_3_, ...), custom_call_target="tpu_custom_call" | custom-call | flops 1000 | bytes 1000 | tf_op jit(solution)/shard_map/attend_back/pallas_call | solution.py:136
  138.7 2.6 add_convert_fusion.2.refs_15_
  143.0 11.2 %attend_back.5 = (bf16[800,768]{1,0:T(8,128)(2,1)}, bf16[1024,576]{1,0:T(8,128)(2,1)}) custom-call(s32[4]{0:T(128)} %refs_0_.11, s32[1]{0:T(128)} %bitcast.me_ref.refs_1_, bf16[512,768]{1,0:T(8,128)(2,1)} %collective-permute-done.core_ref.refs_2_, bf16[512,768]{1,0:T(8,128)(2,1)} %collective-permute-done.1.mid_ref.refs_3_, ...), custom_call_target="tpu_custom_call" | custom-call | flops 1000 | bytes 1000 | tf_op jit(solution)/shard_map/attend_back/pallas_call | solution.py:136
  154.2 5.1 %collective-permute-done.21 = bf16[768,768]{1,0:T(8,128)(2,1)} collective-permute-done((bf16[768,768]{1,0:T(8,128)(2,1)S(1)}, bf16[768,768]{1,0:T(8,128)(2,1)}, u32[]{:S(2)}, u32[]{:S(2)}) %collective-permute-start.21) | collective-permute-done | bytes 1179680 | tf_op jit(solution)/shard_map/ppermute | solution.py:784
  164.4 2.3 collective-permute-start.22
  169.1 11.3 %attend_back.6 = (bf16[800,768]{1,0:T(8,128)(2,1)}, bf16[1024,576]{1,0:T(8,128)(2,1)}) custom-call(s32[4]{0:T(128)} %refs_0_.11, s32[1]{0:T(128)} %bitcast.me_ref.refs_1_, bf16[512,768]{1,0:T(8,128)(2,1)} %collective-permute-done.core_ref.refs_2_, bf16[512,768]{1,0:T(8,128)(2,1)} %collective-permute-done.1.mid_ref.refs_3_, ...), custom_call_target="tpu_custom_call" | custom-call | flops 1000 | bytes 1000 | tf_op jit(solution)/shard_map/attend_back/pallas_call | solution.py:136
  183.0 2.8 collective-permute-start.27
  187.1 11.1 %attend_back.7 = (bf16[800,768]{1,0:T(8,128)(2,1)}, bf16[1024,576]{1,0:T(8,128)(2,1)}) custom-call(s32[4]{0:T(128)} %refs_0_.11, s32[1]{0:T(128)} %bitcast.me_ref.refs_1_, bf16[512,768]{1,0:T(8,128)(2,1)} %collective-permute-done.core_ref.refs_2_, bf16[512,768]{1,0:T(8,128)(2,1)} %collective-permute-done.1.mid_ref.refs_3_, ...), custom_call_target="tpu_custom_call" | custom-call | flops 1000 | bytes 1000 | tf_op jit(solution)/shard_map/attend_back/pallas_call | solution.py:136
  204.6 2.4 collective-permute-start.30
  207.0 3.4 %collective-permute-done.31 = bf16[208,768]{1,0:T(8,128)(2,1)S(1)} collective-permute-done((bf16[208,768]{1,0:T(8,128)(2,1)S(1)}, bf16[208,768]{1,0:T(8,128)(2,1)S(1)}, u32[]{:S(2)}, u32[]{:S(2)}) %collective-permute-start.31) | collective-permute-done | bytes 319520 | tf_op jit(solution)/shard_map/ppermute | solution.py:784
  211.3 8.1 %collective-permute-done.30 = bf16[96,768]{1,0:T(8,128)(2,1)S(1)} collective-permute-done((bf16[96,768]{1,0:T(8,128)(2,1)S(1)}, bf16[96,768]{1,0:T(8,128)(2,1)S(1)}, u32[]{:S(2)}, u32[]{:S(2)}) %collective-permute-start.30) | collective-permute-done | bytes 147488 | tf_op jit(solution)/shard_map/ppermute | solution.py:784
  221.9 6.6 %other_grad.1 = bf16[512,768]{1,0:T(8,128)(2,1)} custom-call(bf16[1024,576]{1,0:T(8,128)(2,1)} %get-tuple-element.210.refs_0_.refs_4_, bf16[1024,576]{1,0:T(8,128)(2,1)} %get-tuple-element.211.refs_1_.refs_5_, bf16[1024,576]{1,0:T(8,128)(2,1)} %get-tuple-element.212.refs_2_.refs_6_, bf16[1024,576]{1,0:T(8,128)(2,1)} %get-tuple-element.213.refs_3_.refs_7_, ...), custom_call_target="tpu_custom_call" | custom-call | flops 1000 | bytes 1000 | tf_op jit(solution)/shard_map/other_grad/pallas_call | solution.py:136
  228.6 3.0 %collective-permute-start.36 = (bf16[52,768]{1,0:T(8,128)(2,1)S(1)}, bf16[52,768]{1,0:T(8,128)(2,1)S(1)}, u32[]{:S(2)}, u32[]{:S(2)}) collective-permute-start(bf16[52,768]{1,0:T(8,128)(2,1)S(1)} %constant_dynamic-slice_fusion.1), channel_id=1, source_target_pairs={{0,16},{4,20},{8,24},{12,28},{16,0},{20,4},{24,8},{28,12},{1,17},{... | collective-permute-start | bytes 239624 | tf_op jit(solution)/shard_map/ppermute | solution.py:784
  231.6 2.3 collective-permute-done.33
  235.1 2.5 collective-permute-done.37
  238.7 4.4 %collective-permute-done.40 = bf16[192,768]{1,0:T(8,128)(2,1)S(1)} collective-permute-done((bf16[192,768]{1,0:T(8,128)(2,1)S(1)}, bf16[192,768]{1,0:T(8,128)(2,1)S(1)}, u32[]{:S(2)}, u32[]{:S(2)}) %collective-permute-start.40) | collective-permute-done | bytes 294944 | tf_op jit(solution)/shard_map/ppermute | solution.py:784
  243.3 3.2 %collective-permute-done.39 = bf16[48,768]{1,0:T(8,128)(2,1)S(1)} collective-permute-done((bf16[48,768]{1,0:T(8,128)(2,1)S(1)}, bf16[48,768]{1,0:T(8,128)(2,1)S(1)}, u32[]{:S(2)}, u32[]{:S(2)}) %collective-permute-start.39) | collective-permute-done | bytes 73760 | tf_op jit(solution)/shard_map/ppermute | solution.py:784
  252.5 8.2 %take_back.1 = f32[512,768]{1,0:T(8,128)} custom-call(s32[4]{0:T(128)} %refs_0_.11, s32[1]{0:T(128)} %bitcast.me_ref.refs_1_, bf16[512,768]{1,0:T(8,128)(2,1)} %copy-done.27, bf16[512,768]{1,0:T(8,128)(2,1)} %copy-done.28, bf16[1024,576]{1,0:T(8,128)(2,1)} %get-tuple-element.210.refs_0_.refs_4_, bf16[1024,576]{1,0:T(8,128)(2,1)} %get-tuple-element.211.refs_1_.refs_5_, ...), custom_call_target="tpu_custom_call" | custom-call | flops 1000 | bytes 1000 | tf_op jit(solution)/shard_map/take_back/pallas_call | solution.py:136
  267.9 2.9 %fusion.1 = f32[768,768]{1,0:T(8,128)} fusion(bf16[384,768]{1,0:T(8,128)(2,1)} %collective-permute-done.45, bf16[384,768]{1,0:T(8,128)(2,1)S(1)} %maximum_select_fusion.6, pred[]{:T(512)S(6)} %eq.8), kind=kLoop, calls=%fused_computation.11 | loop fusion | flops 5898240 | bytes 3538945 | tf_op jit(solution)/shard_map/convert_element_type | solution.py:1017
  270.8 2.8 %collective-permute-done.44 = bf16[208,768]{1,0:T(8,128)(2,1)S(1)} collective-permute-done((bf16[208,768]{1,0:T(8,128)(2,1)S(1)}, bf16[208,768]{1,0:T(8,128)(2,1)S(1)}, u32[]{:S(2)}, u32[]{:S(2)}) %collective-permute-start.44) | collective-permute-done | bytes 319520 | tf_op jit(solution)/shard_map/ppermute | solution.py:784
  (199 shorter events, 73.1 us)
Async XLA Ops:
  0.7 18.2 %collective-permute-start.1 = (bf16[512,768]{1,0:T(8,128)(2,1)}, bf16[512,768]{1,0:T(8,128)(2,1)}, u32[]{:S(2)}, u32[]{:S(2)}) collective-permute-start(bf16[512,768]{1,0:T(8,128)(2,1)} %refs_11_.11), channel_id=1, source_target_pairs={{1,2},{2,1},{5,6},{6,5},{9,10},{10,9},{13,14},{14,13},{17,18},{18,... | collective-permute-start | bytes 2359304 | tf_op jit(solution)/shard_map/ppermute | solution.py:796
  4.7 25.6 %collective-permute-start.2 = (bf16[784,768]{1,0:T(8,128)(2,1)}, bf16[784,768]{1,0:T(8,128)(2,1)S(1)}, u32[]{:S(2)}, u32[]{:S(2)}) collective-permute-start(bf16[784,768]{1,0:T(8,128)(2,1)} %pack_joint.1.a0_ref.refs_2_.refs_13_.refs_5_.refs_4_.refs_8_), channel_id=1, source_target_pairs={{0,1},{1,0},{2,3},{3,2},{4,5},{5,4},{6,7},{7,6},{8,9},{9,8},{10,11... | collective-permute-start | bytes 3612680 | tf_op jit(solution)/shard_map/ppermute | solution.py:784
  18.8 28.1 %collective-permute-start.5 = (bf16[784,768]{1,0:T(8,128)(2,1)}, bf16[784,768]{1,0:T(8,128)(2,1)S(1)}, u32[]{:S(2)}, u32[]{:S(2)}) collective-permute-start(bf16[784,768]{1,0:T(8,128)(2,1)} %pack_joint.1.a0_ref.refs_2_.refs_13_.refs_5_.refs_4_.refs_8_), channel_id=1, source_target_pairs={{0,2},{1,3},{2,0},{3,1},{4,6},{5,7},{6,4},{7,5},{8,10},{9,11},{10,... | collective-permute-start | bytes 3612680 | tf_op jit(solution)/shard_map/ppermute | solution.py:784
  18.9 13.8 %collective-permute-start = (bf16[512,768]{1,0:T(8,128)(2,1)S(1)}, bf16[512,768]{1,0:T(8,128)(2,1)}, u32[]{:S(2)}, u32[]{:S(2)}) collective-permute-start(bf16[512,768]{1,0:T(8,128)(2,1)S(1)} %copy-done.3), channel_id=1, source_target_pairs={{0,1},{1,0},{2,3},{3,2},{4,5},{5,4},{6,7},{7,6},{8,9},{9,8},{10,11... | collective-permute-start | bytes 2359304 | tf_op jit(solution)/shard_map/ppermute | solution.py:784
  32.0 13.6 %collective-permute-start.6 = (bf16[192,768]{1,0:T(8,128)(2,1)S(1)}, bf16[192,768]{1,0:T(8,128)(2,1)}, u32[]{:S(2)}, u32[]{:S(2)}) collective-permute-start(bf16[192,768]{1,0:T(8,128)(2,1)S(1)} %maximum_select_fusion.9.refs_0_), channel_id=1, source_target_pairs={{0,8},{4,12},{8,0},{12,4},{16,24},{20,28},{24,16},{28,20},{1,9},{5... | collective-permute-start | bytes 884744 | tf_op jit(solution)/shard_map/ppermute | solution.py:784
  47.1 17.7 %collective-permute-start.8 = (bf16[768,768]{1,0:T(8,128)(2,1)}, bf16[768,768]{1,0:T(8,128)(2,1)}, u32[]{:S(2)}, u32[]{:S(2)}) collective-permute-start(bf16[768,768]{1,0:T(8,128)(2,1)} %refs_9_.5), channel_id=1, source_target_pairs={{0,1},{1,0},{2,3},{3,2},{4,5},{5,4},{6,7},{7,6},{8,9},{9,8},{10,11... | collective-permute-start | bytes 3538952 | tf_op jit(solution)/shard_map/ppermute | solution.py:784
  47.6 17.2 %collective-permute-start.9 = (bf16[768,768]{1,0:T(8,128)(2,1)}, bf16[768,768]{1,0:T(8,128)(2,1)}, u32[]{:S(2)}, u32[]{:S(2)}) collective-permute-start(bf16[768,768]{1,0:T(8,128)(2,1)} %refs_7_.1), channel_id=1, source_target_pairs={{0,1},{1,0},{2,3},{3,2},{4,5},{5,4},{6,7},{7,6},{8,9},{9,8},{10,11... | collective-permute-start | bytes 3538952 | tf_op jit(solution)/shard_map/ppermute | solution.py:784
  47.6 29.0 %collective-permute-start.10 = (bf16[768,768]{1,0:T(8,128)(2,1)}, bf16[768,768]{1,0:T(8,128)(2,1)}, u32[]{:S(2)}, u32[]{:S(2)}) collective-permute-start(bf16[768,768]{1,0:T(8,128)(2,1)} %refs_9_.5), channel_id=1, source_target_pairs={{0,2},{1,3},{2,0},{3,1},{4,6},{5,7},{6,4},{7,5},{8,10},{9,11},{10,... | collective-permute-start | bytes 3538952 | tf_op jit(solution)/shard_map/ppermute | solution.py:784
  49.2 25.7 %collective-permute-start.11 = (bf16[384,768]{1,0:T(8,128)(2,1)S(1)}, bf16[384,768]{1,0:T(8,128)(2,1)}, u32[]{:S(2)}, u32[]{:S(2)}) collective-permute-start(bf16[384,768]{1,0:T(8,128)(2,1)S(1)} %maximum_select_fusion.4.refs_0_), channel_id=1, source_target_pairs={{0,4},{4,0},{8,12},{12,8},{16,20},{20,16},{24,28},{28,24},{1,5},{5... | collective-permute-start | bytes 1769480 | tf_op jit(solution)/shard_map/ppermute | solution.py:784
  105.8 29.0 %collective-permute-start.17 = (bf16[768,768]{1,0:T(8,128)(2,1)S(1)}, bf16[768,768]{1,0:T(8,128)(2,1)}, u32[]{:S(2)}, u32[]{:S(2)}) collective-permute-start(bf16[768,768]{1,0:T(8,128)(2,1)S(1)} %add_convert_fusion.5.refs_15_), channel_id=1, source_target_pairs={{0,2},{1,3},{2,0},{3,1},{4,6},{5,7},{6,4},{7,5},{8,10},{9,11},{10,... | collective-permute-start | bytes 3538952 | tf_op jit(solution)/shard_map/ppermute | solution.py:784
  121.2 13.5 %collective-permute-start.16 = (bf16[768,768]{1,0:T(8,128)(2,1)}, bf16[768,768]{1,0:T(8,128)(2,1)}, u32[]{:S(2)}, u32[]{:S(2)}) collective-permute-start(bf16[768,768]{1,0:T(8,128)(2,1)} %get-tuple-element.179), channel_id=1, source_target_pairs={{0,1},{1,0},{2,3},{3,2},{4,5},{5,4},{6,7},{7,6},{8,9},{9,8},{10,11... | collective-permute-start | bytes 3538952 | tf_op jit(solution)/shard_map/ppermute | solution.py:784
  121.3 15.6 %collective-permute-start.19 = (bf16[768,768]{1,0:T(8,128)(2,1)}, bf16[768,768]{1,0:T(8,128)(2,1)}, u32[]{:S(2)}, u32[]{:S(2)}) collective-permute-start(bf16[768,768]{1,0:T(8,128)(2,1)} %get-tuple-element.195), channel_id=1, source_target_pairs={{0,1},{1,0},{2,3},{3,2},{4,5},{5,4},{6,7},{7,6},{8,9},{9,8},{10,11... | collective-permute-start | bytes 3538952 | tf_op jit(solution)/shard_map/ppermute | solution.py:784
  121.8 37.4 %collective-permute-start.21 = (bf16[768,768]{1,0:T(8,128)(2,1)S(1)}, bf16[768,768]{1,0:T(8,128)(2,1)}, u32[]{:S(2)}, u32[]{:S(2)}) collective-permute-start(bf16[768,768]{1,0:T(8,128)(2,1)S(1)} %copy-done.10), channel_id=1, source_target_pairs={{0,2},{1,3},{2,0},{3,1},{4,6},{5,7},{6,4},{7,5},{8,10},{9,11},{10,... | collective-permute-start | bytes 3538952 | tf_op jit(solution)/shard_map/ppermute | solution.py:784
  141.4 19.6 %collective-permute-start.20 = (bf16[800,768]{1,0:T(8,128)(2,1)}, bf16[800,768]{1,0:T(8,128)(2,1)}, u32[]{:S(2)}, u32[]{:S(2)}) collective-permute-start(bf16[800,768]{1,0:T(8,128)(2,1)} %get-tuple-element.198), channel_id=1, source_target_pairs={{0,1},{1,0},{2,3},{3,2},{4,5},{5,4},{6,7},{7,6},{8,9},{9,8},{10,11... | collective-permute-start | bytes 3686408 | tf_op jit(solution)/shard_map/ppermute | solution.py:784
  141.4 21.3 %collective-permute-start.18 = (bf16[384,768]{1,0:T(8,128)(2,1)S(1)}, bf16[384,768]{1,0:T(8,128)(2,1)}, u32[]{:S(2)}, u32[]{:S(2)}) collective-permute-start(bf16[384,768]{1,0:T(8,128)(2,1)S(1)} %constant_dynamic-slice_fusion.11.refs_14_), channel_id=1, source_target_pairs={{0,4},{4,0},{8,12},{12,8},{16,20},{20,16},{24,28},{28,24},{1,5},{5... | collective-permute-start | bytes 1769480 | tf_op jit(solution)/shard_map/ppermute | solution.py:784
  164.4 16.0 %collective-permute-start.22 = (bf16[192,768]{1,0:T(8,128)(2,1)S(1)}, bf16[192,768]{1,0:T(8,128)(2,1)}, u32[]{:S(2)}, u32[]{:S(2)}) collective-permute-start(bf16[192,768]{1,0:T(8,128)(2,1)S(1)} %constant_dynamic-slice_fusion.10.refs_15_), channel_id=1, source_target_pairs={{0,8},{4,12},{8,0},{12,4},{16,24},{20,28},{24,16},{28,20},{1,9},{5... | collective-permute-start | bytes 884744 | tf_op jit(solution)/shard_map/ppermute | solution.py:784
  166.8 14.8 %collective-permute-start.23 = (bf16[384,768]{1,0:T(8,128)(2,1)S(1)}, bf16[384,768]{1,0:T(8,128)(2,1)}, u32[]{:S(2)}, u32[]{:S(2)}) collective-permute-start(bf16[384,768]{1,0:T(8,128)(2,1)S(1)} %constant_dynamic-slice_fusion.9.refs_16_), channel_id=1, source_target_pairs={{0,4},{4,0},{8,12},{12,8},{16,20},{20,16},{24,28},{28,24},{1,5},{5... | collective-permute-start | bytes 1769480 | tf_op jit(solution)/shard_map/ppermute | solution.py:784
  168.4 29.8 %collective-permute-start.24 = (bf16[800,768]{1,0:T(8,128)(2,1)S(1)}, bf16[800,768]{1,0:T(8,128)(2,1)}, u32[]{:S(2)}, u32[]{:S(2)}) collective-permute-start(bf16[800,768]{1,0:T(8,128)(2,1)S(1)} %add_convert_fusion.refs_14_), channel_id=1, source_target_pairs={{0,2},{1,3},{2,0},{3,1},{4,6},{5,7},{6,4},{7,5},{8,10},{9,11},{10,... | collective-permute-start | bytes 3686408 | tf_op jit(solution)/shard_map/ppermute | solution.py:784
  182.9 15.3 %collective-permute-start.25 = (bf16[800,768]{1,0:T(8,128)(2,1)}, bf16[800,768]{1,0:T(8,128)(2,1)}, u32[]{:S(2)}, u32[]{:S(2)}) collective-permute-start(bf16[800,768]{1,0:T(8,128)(2,1)} %get-tuple-element.216), channel_id=1, source_target_pairs={{0,1},{1,0},{2,3},{3,2},{4,5},{5,4},{6,7},{7,6},{8,9},{9,8},{10,11... | collective-permute-start | bytes 3686408 | tf_op jit(solution)/shard_map/ppermute | solution.py:784
  183.0 20.8 %collective-permute-start.27 = (bf16[96,768]{1,0:T(8,128)(2,1)S(1)}, bf16[96,768]{1,0:T(8,128)(2,1)S(1)}, u32[]{:S(2)}, u32[]{:S(2)}) collective-permute-start(bf16[96,768]{1,0:T(8,128)(2,1)S(1)} %constant_dynamic-slice_fusion.8.refs_14_), channel_id=1, source_target_pairs={{0,16},{4,20},{8,24},{12,28},{16,0},{20,4},{24,8},{28,12},{1,17},{... | collective-permute-start | bytes 442376 | tf_op jit(solution)/shard_map/ppermute | solution.py:784
  185.7 18.7 %collective-permute-start.29 = (bf16[192,768]{1,0:T(8,128)(2,1)S(1)}, bf16[192,768]{1,0:T(8,128)(2,1)S(1)}, u32[]{:S(2)}, u32[]{:S(2)}) collective-permute-start(bf16[192,768]{1,0:T(8,128)(2,1)S(1)} %constant_dynamic-slice_fusion.7.refs_15_), channel_id=1, source_target_pairs={{0,8},{4,12},{8,0},{12,4},{16,24},{20,28},{24,16},{28,20},{1,9},{5... | collective-permute-start | bytes 884744 | tf_op jit(solution)/shard_map/ppermute | solution.py:784
  202.3 18.3 %collective-permute-start.26 = (bf16[192,768]{1,0:T(8,128)(2,1)S(1)}, bf16[192,768]{1,0:T(8,128)(2,1)S(1)}, u32[]{:S(2)}, u32[]{:S(2)}) collective-permute-start(bf16[192,768]{1,0:T(8,128)(2,1)S(1)} %constant_dynamic-slice_fusion.5), channel_id=1, source_target_pairs={{0,4},{4,0},{8,12},{12,8},{16,20},{20,16},{24,28},{28,24},{1,5},{5... | collective-permute-start | bytes 884744 | tf_op jit(solution)/shard_map/ppermute | solution.py:784
  203.8 15.7 %collective-permute-start.28 = (bf16[96,768]{1,0:T(8,128)(2,1)S(1)}, bf16[96,768]{1,0:T(8,128)(2,1)S(1)}, u32[]{:S(2)}, u32[]{:S(2)}) collective-permute-start(bf16[96,768]{1,0:T(8,128)(2,1)S(1)} %add_convert_fusion.17), channel_id=1, source_target_pairs={{0,16},{4,20},{8,24},{12,28},{16,0},{20,4},{24,8},{28,12},{1,17},{... | collective-permute-start | bytes 442376 | tf_op jit(solution)/shard_map/ppermute | solution.py:784
  204.6 14.9 %collective-permute-start.30 = (bf16[96,768]{1,0:T(8,128)(2,1)S(1)}, bf16[96,768]{1,0:T(8,128)(2,1)S(1)}, u32[]{:S(2)}, u32[]{:S(2)}) collective-permute-start(bf16[96,768]{1,0:T(8,128)(2,1)S(1)} %constant_dynamic-slice_fusion.4), channel_id=1, source_target_pairs={{0,16},{4,20},{8,24},{12,28},{16,0},{20,4},{24,8},{28,12},{1,17},{... | collective-permute-start | bytes 442376 | tf_op jit(solution)/shard_map/ppermute | solution.py:784
  210.5 18.0 %collective-permute-start.34 = (bf16[104,768]{1,0:T(8,128)(2,1)S(1)}, bf16[104,768]{1,0:T(8,128)(2,1)S(1)}, u32[]{:S(2)}, u32[]{:S(2)}) collective-permute-start(bf16[104,768]{1,0:T(8,128)(2,1)S(1)} %constant_dynamic-slice_fusion.3), channel_id=1, source_target_pairs={{0,8},{4,12},{8,0},{12,4},{16,24},{20,28},{24,16},{28,20},{1,9},{5... | collective-permute-start | bytes 479240 | tf_op jit(solution)/shard_map/ppermute | solution.py:784
  219.5 14.7 %collective-permute-start.32 = (bf16[96,768]{1,0:T(8,128)(2,1)S(1)}, bf16[96,768]{1,0:T(8,128)(2,1)S(1)}, u32[]{:S(2)}, u32[]{:S(2)}) collective-permute-start(bf16[96,768]{1,0:T(8,128)(2,1)S(1)} %add_convert_fusion.16), channel_id=1, source_target_pairs={{0,16},{4,20},{8,24},{12,28},{16,0},{20,4},{24,8},{28,12},{1,17},{... | collective-permute-start | bytes 442376 | tf_op jit(solution)/shard_map/ppermute | solution.py:784
  219.6 14.3 %collective-permute-start.33 = (bf16[192,768]{1,0:T(8,128)(2,1)S(1)}, bf16[192,768]{1,0:T(8,128)(2,1)S(1)}, u32[]{:S(2)}, u32[]{:S(2)}) collective-permute-start(bf16[192,768]{1,0:T(8,128)(2,1)S(1)} %maximum_select_fusion.10), channel_id=1, source_target_pairs={{0,8},{4,12},{8,0},{12,4},{16,24},{20,28},{24,16},{28,20},{1,9},{5... | collective-permute-start | bytes 884744 | tf_op jit(solution)/shard_map/ppermute | solution.py:784
  220.7 16.9 %collective-permute-start.37 = (bf16[96,768]{1,0:T(8,128)(2,1)S(1)}, bf16[96,768]{1,0:T(8,128)(2,1)S(1)}, u32[]{:S(2)}, u32[]{:S(2)}) collective-permute-start(bf16[96,768]{1,0:T(8,128)(2,1)S(1)} %constant_dynamic-slice_fusion.2.refs_8_), channel_id=1, source_target_pairs={{0,8},{4,12},{8,0},{12,4},{16,24},{20,28},{24,16},{28,20},{1,9},{5... | collective-permute-start | bytes 442376 | tf_op jit(solution)/shard_map/ppermute | solution.py:784
  234.3 15.0 %collective-permute-start.35 = (bf16[512,768]{1,0:T(8,128)(2,1)S(1)}, bf16[512,768]{1,0:T(8,128)(2,1)S(1)}, u32[]{:S(2)}, u32[]{:S(2)}) collective-permute-start(bf16[512,768]{1,0:T(8,128)(2,1)S(1)} %copy-done.29), channel_id=1, source_target_pairs={{0,1},{1,0},{2,3},{3,2},{4,5},{5,4},{6,7},{7,6},{8,9},{9,8},{10,11... | collective-permute-start | bytes 2359304 | tf_op jit(solution)/shard_map/ppermute | solution.py:784
  234.4 17.2 %collective-permute-start.41 = (bf16[512,768]{1,0:T(8,128)(2,1)S(1)}, bf16[512,768]{1,0:T(8,128)(2,1)S(1)}, u32[]{:S(2)}, u32[]{:S(2)}) collective-permute-start(bf16[512,768]{1,0:T(8,128)(2,1)S(1)} %copy-done.29), channel_id=1, source_target_pairs={{1,2},{2,1},{5,6},{6,5},{9,10},{10,9},{13,14},{14,13},{17,18},{18,... | collective-permute-start | bytes 2359304 | tf_op jit(solution)/shard_map/ppermute | solution.py:796
  237.6 26.4 %collective-permute-start.47 = (bf16[384,768]{1,0:T(8,128)(2,1)S(1)}, bf16[384,768]{1,0:T(8,128)(2,1)S(1)}, u32[]{:S(2)}, u32[]{:S(2)}) collective-permute-start(bf16[384,768]{1,0:T(8,128)(2,1)S(1)} %maximum_select_fusion.5), channel_id=1, source_target_pairs={{0,4},{4,0},{8,12},{12,8},{16,20},{20,16},{24,28},{28,24},{1,5},{5... | collective-permute-start | bytes 1769480 | tf_op jit(solution)/shard_map/ppermute | solution.py:784
  246.6 21.4 %collective-permute-start.45 = (bf16[384,768]{1,0:T(8,128)(2,1)S(1)}, bf16[384,768]{1,0:T(8,128)(2,1)}, u32[]{:S(2)}, u32[]{:S(2)}) collective-permute-start(bf16[384,768]{1,0:T(8,128)(2,1)S(1)} %maximum_select_fusion.6), channel_id=1, source_target_pairs={{0,4},{4,0},{8,12},{12,8},{16,20},{20,16},{24,28},{28,24},{1,5},{5... | collective-permute-start | bytes 1769480 | tf_op jit(solution)/shard_map/ppermute | solution.py:784
  (52 other events, 303.9 us)

commit v4 on v3

--- a/solution.py
+++ b/solution.py
@@ -484,7 +484,6 @@
     b_s[8:16] = vec_ref[...]
     at = 2 * cols
     grad_ref[at : at + 16] = b_s[...].astype(BF)
-    grad_ref[at + 16 : at + 32] = jnp.zeros((16, b_s.shape[1]), BF)
     other()
     send(d_s)
     arrive(own_ref)
@@ -497,8 +496,8 @@
             dot(t_s[cols : 3 * cols, near], tok) + dot(t_s[cols : 3 * cols, far], other.buffer[:, cs])
         ).astype(BF)
         grad_ref[cols : 2 * cols, cs] = terms[0:cols]
-        grad_ref[at + 32 : at + 32 + cols, cs] = terms[cols : 2 * cols]
-        grad_ref[at + 32 + cols : at + 32 + 2 * cols, cs] = dot(
+        grad_ref[at + 16 : at + 16 + cols, cs] = terms[cols : 2 * cols]
+        grad_ref[at + 16 + cols : at + 16 + 2 * cols, cs] = dot(
             t_s[3 * cols : 4 * cols, near], g_ref[:, cs]
         ).astype(BF)
 
@@ -526,7 +525,7 @@
     args = (lens, me, tok_core, tok_mid, g, a, q, k, lse, v, ct, own, bu, vecs)
     return call(
         attend_back_kernel, "attend_back",
-        [shape((4 * cols + 32, width), BF), shape((2 * rows, 3 * cols), BF)],
+        [shape((4 * cols + 16, width), BF), shape((2 * rows, 3 * cols), BF)],
         args, smem=2, raw=(2, 3), after=after, first=0, part={5: (3 * cols, cols)},
         scratch=[
             pltpu.VMEM((rows, width), BF), pltpu.SemaphoreType.DMA, pltpu.VMEM((16, width), F32),
@@ -983,7 +982,7 @@
     joint_back = hold(joint_back, joint_sum)
 
     def rows_of(a, part):
-        return a[: 2 * cols + 32] if part == 0 else a[2 * cols + 32 :]
+        return a[: 2 * cols + 16] if part == 0 else a[2 * cols + 16 :]
 
     def joint_part(i, own, got):
         return WideSum(add_low(rows_of(own, i), rows_of(got, i), rows_of(joint_back, i)))

time: 281 us -> 280 us (level)
  no operation moved by 1% of the time
where the time goes in v4:
time: 280 us; the launch traced here: 279 us
  Pallas kernels  133 us (48%)
  waiting for transfers between devices  59.7 us (21%)
  starting transfers between devices  44.8 us (16%)
  other arithmetic  32.3 us (12%)
  local copies, waits for them, and re-layouts  8.3 us (3%)
    pallas_call x12, Pallas kernels, call(): pl.pallas_call(body, out_shape=tuple(out_shape), in_specs=in_specs + [ANY...  107 us
    ppermute x47, waiting for transfers between devices, swap(): return lax.ppermute(a, axis, [(i, i ^ distance) for i in range(size)])  59.7 us
    ppermute x47, starting transfers between devices, swap(): return lax.ppermute(a, axis, [(i, i ^ distance) for i in range(size)])  42.5 us
    pallas_call x2, Pallas kernels, attend_pair(): pl.pallas_call(functools.partial(attend_pair_kernel, after=len(after)), o...  25.7 us
    convert_element_type x20, other arithmetic, add_low(): return total.astype(BF)  19.2 us
    select_n x11, other arithmetic, in_order(): jnp.where(side == 0, jnp.concatenate([mine, got]), jnp.concatenate([got,...  7.31 us
  transfers between devices with their start and end apart: 49, of which 17 were waited for; matrix products, arithmetic and copies ran while one was open for 11% of the time, Pallas kernels for 43%

profile of v4, /device:TPU:0, one launch (start us, length us, event | category | flops | bytes accessed | tf_op | source)
XLA Modules:
  0.0 279.4 jit_solution(16952172791672137669)
XLA Ops:
  2.2 2.5 pack_joint.1.a0_ref.refs_2_.refs_13_.refs_5_.refs_4_.refs_8_
  4.7 3.5 %collective-permute-start.2 = (bf16[784,768]{1,0:T(8,128)(2,1)}, bf16[784,768]{1,0:T(8,128)(2,1)S(1)}, u32[]{:S(2)}, u32[]{:S(2)}) collective-permute-start(bf16[784,768]{1,0:T(8,128)(2,1)} %pack_joint.1.a0_ref.refs_2_.refs_13_.refs_5_.refs_4_.refs_8_), channel_id=1, source_target_pairs={{0,1},{1,0},{2,3},{3,2},{4,5},{5,4},{6,7},{7,6},{8,9},{9,8},{10,11... | collective-permute-start | bytes 3612680 | tf_op jit(solution)/shard_map/ppermute | solution.py:783
  9.2 9.6 %collective-permute-done.3 = bf16[96,768]{1,0:T(8,128)(2,1)S(1)} collective-permute-done((bf16[96,768]{1,0:T(8,128)(2,1)S(1)}, bf16[96,768]{1,0:T(8,128)(2,1)S(1)}, u32[]{:S(2)}, u32[]{:S(2)}) %collective-permute-start.3) | collective-permute-done | bytes 147488 | tf_op jit(solution)/shard_map/ppermute | solution.py:783
  19.8 2.6 collective-permute-start.4
  22.4 7.2 %collective-permute-done.4 = bf16[96,768]{1,0:T(8,128)(2,1)S(1)} collective-permute-done((bf16[96,768]{1,0:T(8,128)(2,1)S(1)}, bf16[96,768]{1,0:T(8,128)(2,1)S(1)}, u32[]{:S(2)}, u32[]{:S(2)}) %collective-permute-start.4) | collective-permute-done | bytes 147488 | tf_op jit(solution)/shard_map/ppermute | solution.py:783
  32.7 12.8 %attend_near.1 = (bf16[512,192]{1,0:T(8,128)(2,1)}, f32[192,512]{1,0:T(8,128)}, f32[3,512]{1,0:T(4,128)}, bf16[512,192]{1,0:T(8,128)(2,1)}, bf16[1024,192]{1,0:T...) custom-call(s32[4]{0:T(128)} %refs_0_.11, ...), custom_call_target="tpu_custom_call" | custom-call | flops 1000 | bytes 1000 | tf_op jit(solution)/shard_map/attend_near/pallas_call | solution.py:347
  51.9 12.8 %attend_far.1 = (bf16[512,192]{1,0:T(8,128)(2,1)}, f32[192,512]{1,0:T(8,128)}, f32[3,512]{1,0:T(4,128)}, bf16[512,192]{1,0:T(8,128)(2,1)}, bf16[1024,192]{1,0:T(...) custom-call(s32[4]{0:T(128)} %refs_0_.11, ...), custom_call_target="tpu_custom_call" | custom-call | flops 1000 | bytes 1000 | tf_op jit(solution)/shard_map/attend_far/pallas_call | solution.py:347
  64.7 10.1 %norm_near.1 = (f32[512,768]{1,0:T(8,128)}, f32[512,1]{1,0:T(8,128)}, bf16[512,768]{1,0:T(8,128)(2,1)}, bf16[512,768]{1,0:T(8,128)(2,1)}, bf16[512,768]{1,0:T(8,...) custom-call(bf16[512,768]{1,0:T(8,128)(2,1)} %refs_11_.11, ...), custom_call_target="tpu_custom_call" | custom-call | flops 1000 | bytes 1000 | tf_op jit(solution)/shard_map/norm_near/pallas_call | solution.py:136
  77.1 2.8 %collective-permute-done.12.refs_4_ = bf16[768,768]{1,0:T(8,128)(2,1)S(1)} collective-permute-done((bf16[768,768]{1,0:T(8,128)(2,1)}, bf16[768,768]{1,0:T(8,128)(2,1)S(1)}, u32[]{:S(2)}, u32[]{:S(2)}) %collective-permute-start.12) | collective-permute-done | bytes 1179680 | tf_op jit(solution)/shard_map/ppermute | solution.py:783
  82.2 13.8 %ffn_far.1 = (bf16[512,768]{1,0:T(8,128)(2,1)}, bf16[512,768]{1,0:T(8,128)(2,1)}, bf16[512,768]{1,0:T(8,128)(2,1)}, bf16[512,768]{1,0:T(8,128)(2,1)}, f32[8,768]...) custom-call(bf16[512,768]{1,0:T(8,128)(2,1)} %get-tuple-element.146., ...), custom_call_target="tpu_custom_call" | custom-call | flops 1000 | bytes 1000 | tf_op jit(solution)/shard_map/ffn_far/pallas_call | solution.py:136
  96.5 7.1 %ffn_back.1 = (bf16[768,768]{1,0:T(8,128)(2,1)}, bf16[768,768]{1,0:T(8,128)(2,1)}, f32[1,768]{1,0:T(1,128)}, f32[512,768]{1,0:T(8,128)}) custom-call(bf16[512,768]{1,0:T(8,128)(2,1)} %get-tuple-element.153.refs_0_, bf16[512,768]{1,0:T(8,128)(2,1)} %get-tuple-element.158.refs_1_, bf16[768,768]{1,0:T(8,128)(2,1)} %copy-done.5, ...), custom_call_target="tpu_custom_call" | custom-call | flops 1000 | bytes 1000 | tf_op jit(solution)/shard_map/ffn_back/pallas_call | solution.py:136
  108.6 12.4 %ffn_last.1 = (bf16[768,768]{1,0:T(8,128)(2,1)}, bf16[768,768]{1,0:T(8,128)(2,1)}, f32[1,768]{1,0:T(1,128)}, bf16[768,768]{1,0:T(8,128)(2,1)}, bf16[768,768]{1,0...) custom-call(bf16[512,768]{1,0:T(8,128)(2,1)} %get-tuple-element.153.refs_0_, ...), custom_call_target="tpu_custom_call" | custom-call | flops 1000 | bytes 1000 | tf_op jit(solution)/shard_map/ffn_last/pallas_call | solution.py:136
  122.1 11.2 %attend_back.4 = (bf16[784,768]{1,0:T(8,128)(2,1)}, bf16[1024,576]{1,0:T(8,128)(2,1)}) custom-call(s32[4]{0:T(128)} %refs_0_.11, s32[1]{0:T(128)} %bitcast.me_ref.refs_1_, bf16[512,768]{1,0:T(8,128)(2,1)} %collective-permute-done.core_ref.refs_2_, bf16[512,768]{1,0:T(8,128)(2,1)} %collective-permute-done.1.mid_ref.refs_3_, ...), custom_call_target="tpu_custom_call" | custom-call | flops 1000 | bytes 1000 | tf_op jit(solution)/shard_map/attend_back/pallas_call | solution.py:136
  138.7 2.6 add_convert_fusion.2.refs_15_
  142.9 11.2 %attend_back.5 = (bf16[784,768]{1,0:T(8,128)(2,1)}, bf16[1024,576]{1,0:T(8,128)(2,1)}) custom-call(s32[4]{0:T(128)} %refs_0_.11, s32[1]{0:T(128)} %bitcast.me_ref.refs_1_, bf16[512,768]{1,0:T(8,128)(2,1)} %collective-permute-done.core_ref.refs_2_, bf16[512,768]{1,0:T(8,128)(2,1)} %collective-permute-done.1.mid_ref.refs_3_, ...), custom_call_target="tpu_custom_call" | custom-call | flops 1000 | bytes 1000 | tf_op jit(solution)/shard_map/attend_back/pallas_call | solution.py:136
  154.1 5.1 %collective-permute-done.21 = bf16[768,768]{1,0:T(8,128)(2,1)} collective-permute-done((bf16[768,768]{1,0:T(8,128)(2,1)S(1)}, bf16[768,768]{1,0:T(8,128)(2,1)}, u32[]{:S(2)}, u32[]{:S(2)}) %collective-permute-start.21) | collective-permute-done | bytes 1179680 | tf_op jit(solution)/shard_map/ppermute | solution.py:783
  164.3 2.3 collective-permute-start.22
  169.0 11.3 %attend_back.6 = (bf16[784,768]{1,0:T(8,128)(2,1)}, bf16[1024,576]{1,0:T(8,128)(2,1)}) custom-call(s32[4]{0:T(128)} %refs_0_.11, s32[1]{0:T(128)} %bitcast.me_ref.refs_1_, bf16[512,768]{1,0:T(8,128)(2,1)} %collective-permute-done.core_ref.refs_2_, bf16[512,768]{1,0:T(8,128)(2,1)} %collective-permute-done.1.mid_ref.refs_3_, ...), custom_call_target="tpu_custom_call" | custom-call | flops 1000 | bytes 1000 | tf_op jit(solution)/shard_map/attend_back/pallas_call | solution.py:136
  182.9 2.8 collective-permute-start.27
  187.1 11.1 %attend_back.7 = (bf16[784,768]{1,0:T(8,128)(2,1)}, bf16[1024,576]{1,0:T(8,128)(2,1)}) custom-call(s32[4]{0:T(128)} %refs_0_.11, s32[1]{0:T(128)} %bitcast.me_ref.refs_1_, bf16[512,768]{1,0:T(8,128)(2,1)} %collective-permute-done.core_ref.refs_2_, bf16[512,768]{1,0:T(8,128)(2,1)} %collective-permute-done.1.mid_ref.refs_3_, ...), custom_call_target="tpu_custom_call" | custom-call | flops 1000 | bytes 1000 | tf_op jit(solution)/shard_map/attend_back/pallas_call | solution.py:136
  204.0 2.9 %collective-permute-start.30 = (bf16[96,768]{1,0:T(8,128)(2,1)S(1)}, bf16[96,768]{1,0:T(8,128)(2,1)S(1)}, u32[]{:S(2)}, u32[]{:S(2)}) collective-permute-start(bf16[96,768]{1,0:T(8,128)(2,1)S(1)} %constant_dynamic-slice_fusion.4), channel_id=1, source_target_pairs={{0,16},{4,20},{8,24},{12,28},{16,0},{20,4},{24,8},{28,12},{1,17},{... | collective-permute-start | bytes 442376 | tf_op jit(solution)/shard_map/ppermute | solution.py:783
  206.9 3.2 %collective-permute-done.31 = bf16[200,768]{1,0:T(8,128)(2,1)S(1)} collective-permute-done((bf16[200,768]{1,0:T(8,128)(2,1)S(1)}, bf16[200,768]{1,0:T(8,128)(2,1)S(1)}, u32[]{:S(2)}, u32[]{:S(2)}) %collective-permute-start.31) | collective-permute-done | bytes 307232 | tf_op jit(solution)/shard_map/ppermute | solution.py:783
  211.0 8.4 %collective-permute-done.30 = bf16[96,768]{1,0:T(8,128)(2,1)S(1)} collective-permute-done((bf16[96,768]{1,0:T(8,128)(2,1)S(1)}, bf16[96,768]{1,0:T(8,128)(2,1)S(1)}, u32[]{:S(2)}, u32[]{:S(2)}) %collective-permute-start.30) | collective-permute-done | bytes 147488 | tf_op jit(solution)/shard_map/ppermute | solution.py:783
  221.9 6.6 %other_grad.1 = bf16[512,768]{1,0:T(8,128)(2,1)} custom-call(bf16[1024,576]{1,0:T(8,128)(2,1)} %get-tuple-element.210.refs_0_.refs_4_, bf16[1024,576]{1,0:T(8,128)(2,1)} %get-tuple-element.211.refs_1_.refs_5_, bf16[1024,576]{1,0:T(8,128)(2,1)} %get-tuple-element.212.refs_2_.refs_6_, bf16[1024,576]{1,0:T(8,128)(2,1)} %get-tuple-element.213.refs_3_.refs_7_, ...), custom_call_target="tpu_custom_call" | custom-call | flops 1000 | bytes 1000 | tf_op jit(solution)/shard_map/other_grad/pallas_call | solution.py:136
  228.6 3.0 %collective-permute-start.36 = (bf16[50,768]{1,0:T(8,128)(2,1)S(1)}, bf16[50,768]{1,0:T(8,128)(2,1)S(1)}, u32[]{:S(2)}, u32[]{:S(2)}) collective-permute-start(bf16[50,768]{1,0:T(8,128)(2,1)S(1)} %constant_dynamic-slice_fusion.1), channel_id=1, source_target_pairs={{0,16},{4,20},{8,24},{12,28},{16,0},{20,4},{24,8},{28,12},{1,17},{... | collective-permute-start | bytes 230408 | tf_op jit(solution)/shard_map/ppermute | solution.py:783
  231.6 2.3 collective-permute-done.33
  235.1 2.5 collective-permute-done.37
  238.6 4.5 %collective-permute-done.40 = bf16[192,768]{1,0:T(8,128)(2,1)S(1)} collective-permute-done((bf16[192,768]{1,0:T(8,128)(2,1)S(1)}, bf16[192,768]{1,0:T(8,128)(2,1)S(1)}, u32[]{:S(2)}, u32[]{:S(2)}) %collective-permute-start.40) | collective-permute-done | bytes 294944 | tf_op jit(solution)/shard_map/ppermute | solution.py:783
  243.3 3.2 %collective-permute-done.39 = bf16[48,768]{1,0:T(8,128)(2,1)S(1)} collective-permute-done((bf16[48,768]{1,0:T(8,128)(2,1)S(1)}, bf16[48,768]{1,0:T(8,128)(2,1)S(1)}, u32[]{:S(2)}, u32[]{:S(2)}) %collective-permute-start.39) | collective-permute-done | bytes 73760 | tf_op jit(solution)/shard_map/ppermute | solution.py:783
  252.3 8.2 %take_back.1 = f32[512,768]{1,0:T(8,128)} custom-call(s32[4]{0:T(128)} %refs_0_.11, s32[1]{0:T(128)} %bitcast.me_ref.refs_1_, bf16[512,768]{1,0:T(8,128)(2,1)} %copy-done.27, bf16[512,768]{1,0:T(8,128)(2,1)} %copy-done.28, bf16[1024,576]{1,0:T(8,128)(2,1)} %get-tuple-element.210.refs_0_.refs_4_, bf16[1024,576]{1,0:T(8,128)(2,1)} %get-tuple-element.211.refs_1_.refs_5_, ...), custom_call_target="tpu_custom_call" | custom-call | flops 1000 | bytes 1000 | tf_op jit(solution)/shard_map/take_back/pallas_call | solution.py:136
  267.6 2.9 %fusion.1 = f32[768,768]{1,0:T(8,128)} fusion(bf16[384,768]{1,0:T(8,128)(2,1)} %collective-permute-done.45, bf16[384,768]{1,0:T(8,128)(2,1)S(1)} %maximum_select_fusion.6, pred[]{:T(512)S(6)} %eq.8), kind=kLoop, calls=%fused_computation.11 | loop fusion | flops 5898240 | bytes 3538945 | tf_op jit(solution)/shard_map/convert_element_type | solution.py:1016
  270.4 2.8 %collective-permute-done.44 = bf16[200,768]{1,0:T(8,128)(2,1)S(1)} collective-permute-done((bf16[200,768]{1,0:T(8,128)(2,1)S(1)}, bf16[200,768]{1,0:T(8,128)(2,1)S(1)}, u32[]{:S(2)}, u32[]{:S(2)}) %collective-permute-start.44) | collective-permute-done | bytes 307232 | tf_op jit(solution)/shard_map/ppermute | solution.py:783
  (199 shorter events, 72.3 us)
Async XLA Ops:
  0.7 18.2 %collective-permute-start.1 = (bf16[512,768]{1,0:T(8,128)(2,1)}, bf16[512,768]{1,0:T(8,128)(2,1)}, u32[]{:S(2)}, u32[]{:S(2)}) collective-permute-start(bf16[512,768]{1,0:T(8,128)(2,1)} %refs_11_.11), channel_id=1, source_target_pairs={{1,2},{2,1},{5,6},{6,5},{9,10},{10,9},{13,14},{14,13},{17,18},{18,... | collective-permute-start | bytes 2359304 | tf_op jit(solution)/shard_map/ppermute | solution.py:795
  4.7 25.6 %collective-permute-start.2 = (bf16[784,768]{1,0:T(8,128)(2,1)}, bf16[784,768]{1,0:T(8,128)(2,1)S(1)}, u32[]{:S(2)}, u32[]{:S(2)}) collective-permute-start(bf16[784,768]{1,0:T(8,128)(2,1)} %pack_joint.1.a0_ref.refs_2_.refs_13_.refs_5_.refs_4_.refs_8_), channel_id=1, source_target_pairs={{0,1},{1,0},{2,3},{3,2},{4,5},{5,4},{6,7},{7,6},{8,9},{9,8},{10,11... | collective-permute-start | bytes 3612680 | tf_op jit(solution)/shard_map/ppermute | solution.py:783
  18.8 28.1 %collective-permute-start.5 = (bf16[784,768]{1,0:T(8,128)(2,1)}, bf16[784,768]{1,0:T(8,128)(2,1)S(1)}, u32[]{:S(2)}, u32[]{:S(2)}) collective-permute-start(bf16[784,768]{1,0:T(8,128)(2,1)} %pack_joint.1.a0_ref.refs_2_.refs_13_.refs_5_.refs_4_.refs_8_), channel_id=1, source_target_pairs={{0,2},{1,3},{2,0},{3,1},{4,6},{5,7},{6,4},{7,5},{8,10},{9,11},{10,... | collective-permute-start | bytes 3612680 | tf_op jit(solution)/shard_map/ppermute | solution.py:783
  18.9 13.8 %collective-permute-start = (bf16[512,768]{1,0:T(8,128)(2,1)S(1)}, bf16[512,768]{1,0:T(8,128)(2,1)}, u32[]{:S(2)}, u32[]{:S(2)}) collective-permute-start(bf16[512,768]{1,0:T(8,128)(2,1)S(1)} %copy-done.3), channel_id=1, source_target_pairs={{0,1},{1,0},{2,3},{3,2},{4,5},{5,4},{6,7},{7,6},{8,9},{9,8},{10,11... | collective-permute-start | bytes 2359304 | tf_op jit(solution)/shard_map/ppermute | solution.py:783
  32.0 13.6 %collective-permute-start.6 = (bf16[192,768]{1,0:T(8,128)(2,1)S(1)}, bf16[192,768]{1,0:T(8,128)(2,1)}, u32[]{:S(2)}, u32[]{:S(2)}) collective-permute-start(bf16[192,768]{1,0:T(8,128)(2,1)S(1)} %maximum_select_fusion.9.refs_0_), channel_id=1, source_target_pairs={{0,8},{4,12},{8,0},{12,4},{16,24},{20,28},{24,16},{28,20},{1,9},{5... | collective-permute-start | bytes 884744 | tf_op jit(solution)/shard_map/ppermute | solution.py:783
  47.1 17.7 %collective-permute-start.8 = (bf16[768,768]{1,0:T(8,128)(2,1)}, bf16[768,768]{1,0:T(8,128)(2,1)}, u32[]{:S(2)}, u32[]{:S(2)}) collective-permute-start(bf16[768,768]{1,0:T(8,128)(2,1)} %refs_9_.5), channel_id=1, source_target_pairs={{0,1},{1,0},{2,3},{3,2},{4,5},{5,4},{6,7},{7,6},{8,9},{9,8},{10,11... | collective-permute-start | bytes 3538952 | tf_op jit(solution)/shard_map/ppermute | solution.py:783
  47.6 17.2 %collective-permute-start.9 = (bf16[768,768]{1,0:T(8,128)(2,1)}, bf16[768,768]{1,0:T(8,128)(2,1)}, u32[]{:S(2)}, u32[]{:S(2)}) collective-permute-start(bf16[768,768]{1,0:T(8,128)(2,1)} %refs_7_.1), channel_id=1, source_target_pairs={{0,1},{1,0},{2,3},{3,2},{4,5},{5,4},{6,7},{7,6},{8,9},{9,8},{10,11... | collective-permute-start | bytes 3538952 | tf_op jit(solution)/shard_map/ppermute | solution.py:783
  47.6 28.9 %collective-permute-start.10 = (bf16[768,768]{1,0:T(8,128)(2,1)}, bf16[768,768]{1,0:T(8,128)(2,1)}, u32[]{:S(2)}, u32[]{:S(2)}) collective-permute-start(bf16[768,768]{1,0:T(8,128)(2,1)} %refs_9_.5), channel_id=1, source_target_pairs={{0,2},{1,3},{2,0},{3,1},{4,6},{5,7},{6,4},{7,5},{8,10},{9,11},{10,... | collective-permute-start | bytes 3538952 | tf_op jit(solution)/shard_map/ppermute | solution.py:783
  49.2 25.6 %collective-permute-start.11 = (bf16[384,768]{1,0:T(8,128)(2,1)S(1)}, bf16[384,768]{1,0:T(8,128)(2,1)}, u32[]{:S(2)}, u32[]{:S(2)}) collective-permute-start(bf16[384,768]{1,0:T(8,128)(2,1)S(1)} %maximum_select_fusion.4.refs_0_), channel_id=1, source_target_pairs={{0,4},{4,0},{8,12},{12,8},{16,20},{20,16},{24,28},{28,24},{1,5},{5... | collective-permute-start | bytes 1769480 | tf_op jit(solution)/shard_map/ppermute | solution.py:783
  105.7 29.0 %collective-permute-start.17 = (bf16[768,768]{1,0:T(8,128)(2,1)S(1)}, bf16[768,768]{1,0:T(8,128)(2,1)}, u32[]{:S(2)}, u32[]{:S(2)}) collective-permute-start(bf16[768,768]{1,0:T(8,128)(2,1)S(1)} %add_convert_fusion.5.refs_15_), channel_id=1, source_target_pairs={{0,2},{1,3},{2,0},{3,1},{4,6},{5,7},{6,4},{7,5},{8,10},{9,11},{10,... | collective-permute-start | bytes 3538952 | tf_op jit(solution)/shard_map/ppermute | solution.py:783
  121.1 13.6 %collective-permute-start.16 = (bf16[768,768]{1,0:T(8,128)(2,1)}, bf16[768,768]{1,0:T(8,128)(2,1)}, u32[]{:S(2)}, u32[]{:S(2)}) collective-permute-start(bf16[768,768]{1,0:T(8,128)(2,1)} %get-tuple-element.179), channel_id=1, source_target_pairs={{0,1},{1,0},{2,3},{3,2},{4,5},{5,4},{6,7},{7,6},{8,9},{9,8},{10,11... | collective-permute-start | bytes 3538952 | tf_op jit(solution)/shard_map/ppermute | solution.py:783
  121.2 15.6 %collective-permute-start.19 = (bf16[768,768]{1,0:T(8,128)(2,1)}, bf16[768,768]{1,0:T(8,128)(2,1)}, u32[]{:S(2)}, u32[]{:S(2)}) collective-permute-start(bf16[768,768]{1,0:T(8,128)(2,1)} %get-tuple-element.195), channel_id=1, source_target_pairs={{0,1},{1,0},{2,3},{3,2},{4,5},{5,4},{6,7},{7,6},{8,9},{9,8},{10,11... | collective-permute-start | bytes 3538952 | tf_op jit(solution)/shard_map/ppermute | solution.py:783
  121.7 37.5 %collective-permute-start.21 = (bf16[768,768]{1,0:T(8,128)(2,1)S(1)}, bf16[768,768]{1,0:T(8,128)(2,1)}, u32[]{:S(2)}, u32[]{:S(2)}) collective-permute-start(bf16[768,768]{1,0:T(8,128)(2,1)S(1)} %copy-done.10), channel_id=1, source_target_pairs={{0,2},{1,3},{2,0},{3,1},{4,6},{5,7},{6,4},{7,5},{8,10},{9,11},{10,... | collective-permute-start | bytes 3538952 | tf_op jit(solution)/shard_map/ppermute | solution.py:783
  141.3 19.6 %collective-permute-start.20 = (bf16[784,768]{1,0:T(8,128)(2,1)}, bf16[784,768]{1,0:T(8,128)(2,1)}, u32[]{:S(2)}, u32[]{:S(2)}) collective-permute-start(bf16[784,768]{1,0:T(8,128)(2,1)} %get-tuple-element.198), channel_id=1, source_target_pairs={{0,1},{1,0},{2,3},{3,2},{4,5},{5,4},{6,7},{7,6},{8,9},{9,8},{10,11... | collective-permute-start | bytes 3612680 | tf_op jit(solution)/shard_map/ppermute | solution.py:783
  141.3 21.3 %collective-permute-start.18 = (bf16[384,768]{1,0:T(8,128)(2,1)S(1)}, bf16[384,768]{1,0:T(8,128)(2,1)}, u32[]{:S(2)}, u32[]{:S(2)}) collective-permute-start(bf16[384,768]{1,0:T(8,128)(2,1)S(1)} %constant_dynamic-slice_fusion.11.refs_14_), channel_id=1, source_target_pairs={{0,4},{4,0},{8,12},{12,8},{16,20},{20,16},{24,28},{28,24},{1,5},{5... | collective-permute-start | bytes 1769480 | tf_op jit(solution)/shard_map/ppermute | solution.py:783
  164.3 16.0 %collective-permute-start.22 = (bf16[192,768]{1,0:T(8,128)(2,1)S(1)}, bf16[192,768]{1,0:T(8,128)(2,1)}, u32[]{:S(2)}, u32[]{:S(2)}) collective-permute-start(bf16[192,768]{1,0:T(8,128)(2,1)S(1)} %constant_dynamic-slice_fusion.10.refs_15_), channel_id=1, source_target_pairs={{0,8},{4,12},{8,0},{12,4},{16,24},{20,28},{24,16},{28,20},{1,9},{5... | collective-permute-start | bytes 884744 | tf_op jit(solution)/shard_map/ppermute | solution.py:783
  166.7 14.8 %collective-permute-start.23 = (bf16[384,768]{1,0:T(8,128)(2,1)S(1)}, bf16[384,768]{1,0:T(8,128)(2,1)}, u32[]{:S(2)}, u32[]{:S(2)}) collective-permute-start(bf16[384,768]{1,0:T(8,128)(2,1)S(1)} %constant_dynamic-slice_fusion.9.refs_16_), channel_id=1, source_target_pairs={{0,4},{4,0},{8,12},{12,8},{16,20},{20,16},{24,28},{28,24},{1,5},{5... | collective-permute-start | bytes 1769480 | tf_op jit(solution)/shard_map/ppermute | solution.py:783
  168.3 29.9 %collective-permute-start.24 = (bf16[784,768]{1,0:T(8,128)(2,1)S(1)}, bf16[784,768]{1,0:T(8,128)(2,1)}, u32[]{:S(2)}, u32[]{:S(2)}) collective-permute-start(bf16[784,768]{1,0:T(8,128)(2,1)S(1)} %add_convert_fusion.refs_14_), channel_id=1, source_target_pairs={{0,2},{1,3},{2,0},{3,1},{4,6},{5,7},{6,4},{7,5},{8,10},{9,11},{10,... | collective-permute-start | bytes 3612680 | tf_op jit(solution)/shard_map/ppermute | solution.py:783
  182.8 15.3 %collective-permute-start.25 = (bf16[784,768]{1,0:T(8,128)(2,1)}, bf16[784,768]{1,0:T(8,128)(2,1)}, u32[]{:S(2)}, u32[]{:S(2)}) collective-permute-start(bf16[784,768]{1,0:T(8,128)(2,1)} %get-tuple-element.216), channel_id=1, source_target_pairs={{0,1},{1,0},{2,3},{3,2},{4,5},{5,4},{6,7},{7,6},{8,9},{9,8},{10,11... | collective-permute-start | bytes 3612680 | tf_op jit(solution)/shard_map/ppermute | solution.py:783
  182.9 20.8 %collective-permute-start.27 = (bf16[96,768]{1,0:T(8,128)(2,1)S(1)}, bf16[96,768]{1,0:T(8,128)(2,1)S(1)}, u32[]{:S(2)}, u32[]{:S(2)}) collective-permute-start(bf16[96,768]{1,0:T(8,128)(2,1)S(1)} %constant_dynamic-slice_fusion.8.refs_14_), channel_id=1, source_target_pairs={{0,16},{4,20},{8,24},{12,28},{16,0},{20,4},{24,8},{28,12},{1,17},{... | collective-permute-start | bytes 442376 | tf_op jit(solution)/shard_map/ppermute | solution.py:783
  185.7 18.2 %collective-permute-start.29 = (bf16[192,768]{1,0:T(8,128)(2,1)S(1)}, bf16[192,768]{1,0:T(8,128)(2,1)S(1)}, u32[]{:S(2)}, u32[]{:S(2)}) collective-permute-start(bf16[192,768]{1,0:T(8,128)(2,1)S(1)} %constant_dynamic-slice_fusion.7.refs_15_), channel_id=1, source_target_pairs={{0,8},{4,12},{8,0},{12,4},{16,24},{20,28},{24,16},{28,20},{1,9},{5... | collective-permute-start | bytes 884744 | tf_op jit(solution)/shard_map/ppermute | solution.py:783
  202.2 18.4 %collective-permute-start.26 = (bf16[192,768]{1,0:T(8,128)(2,1)S(1)}, bf16[192,768]{1,0:T(8,128)(2,1)S(1)}, u32[]{:S(2)}, u32[]{:S(2)}) collective-permute-start(bf16[192,768]{1,0:T(8,128)(2,1)S(1)} %constant_dynamic-slice_fusion.5), channel_id=1, source_target_pairs={{0,4},{4,0},{8,12},{12,8},{16,20},{20,16},{24,28},{28,24},{1,5},{5... | collective-permute-start | bytes 884744 | tf_op jit(solution)/shard_map/ppermute | solution.py:783
  203.8 15.8 %collective-permute-start.28 = (bf16[96,768]{1,0:T(8,128)(2,1)S(1)}, bf16[96,768]{1,0:T(8,128)(2,1)S(1)}, u32[]{:S(2)}, u32[]{:S(2)}) collective-permute-start(bf16[96,768]{1,0:T(8,128)(2,1)S(1)} %add_convert_fusion.17), channel_id=1, source_target_pairs={{0,16},{4,20},{8,24},{12,28},{16,0},{20,4},{24,8},{28,12},{1,17},{... | collective-permute-start | bytes 442376 | tf_op jit(solution)/shard_map/ppermute | solution.py:783
  204.0 15.4 %collective-permute-start.30 = (bf16[96,768]{1,0:T(8,128)(2,1)S(1)}, bf16[96,768]{1,0:T(8,128)(2,1)S(1)}, u32[]{:S(2)}, u32[]{:S(2)}) collective-permute-start(bf16[96,768]{1,0:T(8,128)(2,1)S(1)} %constant_dynamic-slice_fusion.4), channel_id=1, source_target_pairs={{0,16},{4,20},{8,24},{12,28},{16,0},{20,4},{24,8},{28,12},{1,17},{... | collective-permute-start | bytes 442376 | tf_op jit(solution)/shard_map/ppermute | solution.py:783
  210.3 18.3 %collective-permute-start.34 = (bf16[100,768]{1,0:T(8,128)(2,1)S(1)}, bf16[100,768]{1,0:T(8,128)(2,1)S(1)}, u32[]{:S(2)}, u32[]{:S(2)}) collective-permute-start(bf16[100,768]{1,0:T(8,128)(2,1)S(1)} %constant_dynamic-slice_fusion.3), channel_id=1, source_target_pairs={{0,8},{4,12},{8,0},{12,4},{16,24},{20,28},{24,16},{28,20},{1,9},{5... | collective-permute-start | bytes 460808 | tf_op jit(solution)/shard_map/ppermute | solution.py:783
  219.4 14.7 %collective-permute-start.32 = (bf16[96,768]{1,0:T(8,128)(2,1)S(1)}, bf16[96,768]{1,0:T(8,128)(2,1)S(1)}, u32[]{:S(2)}, u32[]{:S(2)}) collective-permute-start(bf16[96,768]{1,0:T(8,128)(2,1)S(1)} %add_convert_fusion.16), channel_id=1, source_target_pairs={{0,16},{4,20},{8,24},{12,28},{16,0},{20,4},{24,8},{28,12},{1,17},{... | collective-permute-start | bytes 442376 | tf_op jit(solution)/shard_map/ppermute | solution.py:783
  219.6 14.4 %collective-permute-start.33 = (bf16[192,768]{1,0:T(8,128)(2,1)S(1)}, bf16[192,768]{1,0:T(8,128)(2,1)S(1)}, u32[]{:S(2)}, u32[]{:S(2)}) collective-permute-start(bf16[192,768]{1,0:T(8,128)(2,1)S(1)} %maximum_select_fusion.10), channel_id=1, source_target_pairs={{0,8},{4,12},{8,0},{12,4},{16,24},{20,28},{24,16},{28,20},{1,9},{5... | collective-permute-start | bytes 884744 | tf_op jit(solution)/shard_map/ppermute | solution.py:783
  220.7 16.9 %collective-permute-start.37 = (bf16[96,768]{1,0:T(8,128)(2,1)S(1)}, bf16[96,768]{1,0:T(8,128)(2,1)S(1)}, u32[]{:S(2)}, u32[]{:S(2)}) collective-permute-start(bf16[96,768]{1,0:T(8,128)(2,1)S(1)} %constant_dynamic-slice_fusion.2.refs_8_), channel_id=1, source_target_pairs={{0,8},{4,12},{8,0},{12,4},{16,24},{20,28},{24,16},{28,20},{1,9},{5... | collective-permute-start | bytes 442376 | tf_op jit(solution)/shard_map/ppermute | solution.py:783
  234.3 15.1 %collective-permute-start.35 = (bf16[512,768]{1,0:T(8,128)(2,1)S(1)}, bf16[512,768]{1,0:T(8,128)(2,1)S(1)}, u32[]{:S(2)}, u32[]{:S(2)}) collective-permute-start(bf16[512,768]{1,0:T(8,128)(2,1)S(1)} %copy-done.29), channel_id=1, source_target_pairs={{0,1},{1,0},{2,3},{3,2},{4,5},{5,4},{6,7},{7,6},{8,9},{9,8},{10,11... | collective-permute-start | bytes 2359304 | tf_op jit(solution)/shard_map/ppermute | solution.py:783
  234.4 17.1 %collective-permute-start.41 = (bf16[512,768]{1,0:T(8,128)(2,1)S(1)}, bf16[512,768]{1,0:T(8,128)(2,1)S(1)}, u32[]{:S(2)}, u32[]{:S(2)}) collective-permute-start(bf16[512,768]{1,0:T(8,128)(2,1)S(1)} %copy-done.29), channel_id=1, source_target_pairs={{1,2},{2,1},{5,6},{6,5},{9,10},{10,9},{13,14},{14,13},{17,18},{18,... | collective-permute-start | bytes 2359304 | tf_op jit(solution)/shard_map/ppermute | solution.py:795
  237.6 26.1 %collective-permute-start.47 = (bf16[384,768]{1,0:T(8,128)(2,1)S(1)}, bf16[384,768]{1,0:T(8,128)(2,1)S(1)}, u32[]{:S(2)}, u32[]{:S(2)}) collective-permute-start(bf16[384,768]{1,0:T(8,128)(2,1)S(1)} %maximum_select_fusion.5), channel_id=1, source_target_pairs={{0,4},{4,0},{8,12},{12,8},{16,20},{20,16},{24,28},{28,24},{1,5},{5... | collective-permute-start | bytes 1769480 | tf_op jit(solution)/shard_map/ppermute | solution.py:783
  246.5 21.1 %collective-permute-start.45 = (bf16[384,768]{1,0:T(8,128)(2,1)S(1)}, bf16[384,768]{1,0:T(8,128)(2,1)}, u32[]{:S(2)}, u32[]{:S(2)}) collective-permute-start(bf16[384,768]{1,0:T(8,128)(2,1)S(1)} %maximum_select_fusion.6), channel_id=1, source_target_pairs={{0,4},{4,0},{8,12},{12,8},{16,20},{20,16},{24,28},{28,24},{1,5},{5... | collective-permute-start | bytes 1769480 | tf_op jit(solution)/shard_map/ppermute | solution.py:783
  (52 other events, 302.4 us)
